TPU v7x, 32 devices: a whole 2x2x4 slice. The times are simulated.
32 devices in a mesh: dp: 8 (over y, x, core), mp: 4 (over z).
Axes of the slice: x: 2, y: 2, z: 4, core: 2. Of those that a mesh axis runs over, the one named last changes fastest.
Arguments:
- token_ids: int32 [8192], P('dp'), may hold values from 0 to 8191
- segment_ids: int32 [8192], P('dp'), may hold values from 0 to 64, as said below
- timesteps: int32 [8], P('dp'), may hold values from 0 to 999
- token_table: bfloat16 [8192, 768], P(None, 'mp'), may hold values from -4.1875 to 4.1875
- time_table: bfloat16 [1000, 768], P(None, 'mp'), may hold values from -4.1875 to 4.1875
- ln1_gain: float32 [768], replicated, may hold values from 0.1 to 1.9
- ln1_bias: float32 [768], replicated, may hold values from -1.8 to 1.8
- w_qkv: bfloat16 [768, 3, 768], P(None, None, 'mp'), may hold values from -0.3125 to 0.3125
- w_out: bfloat16 [768, 768], P('mp'), may hold values from -1.25 to 1.25
- attn_bias: float32 [768], replicated, may hold values from -3 to 3
- ln2_gain: float32 [768], replicated, may hold values from 0.1 to 1.9
- ln2_bias: float32 [768], replicated, may hold values from -1.8 to 1.8
- w_up: bfloat16 [768, 3072], P(None, 'mp'), may hold values from -0.21875 to 0.21875
- w_down: bfloat16 [3072, 768], P('mp'), may hold values from -0.15625 to 0.15625
- mlp_bias: float32 [768], replicated, may hold values from -3 to 3
- cotangent: bfloat16 [8192, 768], P(('dp', 'mp')), may hold values from -6 to 6
Outputs:
- output: bfloat16 [8192, 768], P(('dp', 'mp'))
- input_grad: float32 [8192, 768], P(('dp', 'mp'))
- grad_token_table: float32 [8192, 768], P('dp', 'mp')
- grad_time_table: float32 [1000, 768], replicated
- grad_ln1_gain: float32 [768], replicated
- grad_ln1_bias: float32 [768], replicated
- grad_w_qkv: float32 [768, 3, 768], P('dp', None, 'mp')
- grad_w_out: float32 [768, 768], P('mp', 'dp')
- grad_attn_bias: float32 [768], replicated
- grad_ln2_gain: float32 [768], replicated
- grad_ln2_bias: float32 [768], replicated
- grad_w_up: float32 [768, 3072], P('dp', 'mp')
- grad_w_down: float32 [3072, 768], P('mp', 'dp')
- grad_mlp_bias: float32 [768], replicated
Inputs may be any that keep to these rules, and one draw needn't show every extreme that they name: `segment_ids`: within each sequence of 1024 tokens the ids start at 1 and rise by 0 or 1 from one token to the next; a tail of padding zeros may follow.
All inputs are finite; a program needn't handle non-finite values.
Results may differ from a plain program's by a relative error of at most 0.018.
The roundings to bfloat16 on the way count: a program that leaves them out, or rounds other values in their place, can miss the bound.
Values may be sent and summed in bfloat16 or wider, within the bound.
A program may use at most 128 MiB of HBM per device.

v0:
```python
import jax
import jax.numpy as jnp
from jax import lax
from jax.sharding import PartitionSpec as P

D = 768
HD = 64
L = 1024
QBLK = 512


PRECISE = lax.Precision.HIGHEST


def as_sent(array):
    return jax.tree.map(lambda a: a.astype(jnp.bfloat16) if a.dtype == jnp.float32 else a, array)


def layer_norm(stream, gain, shift):
    average = jnp.mean(stream, axis=-1, keepdims=True)
    centered = stream - average
    variance = jnp.mean(centered * centered, axis=-1, keepdims=True)
    return centered * lax.rsqrt(variance + 1e-05) * gain + shift


def allowed_pairs(seg_query, segments, first_row):
    key_pos = jnp.arange(L)
    query_pos = first_row + jnp.arange(QBLK)
    same_text = seg_query[:, None] == segments[None, :]
    self_or_text = (seg_query[:, None] != 0) | (query_pos[:, None] == key_pos[None, :])
    return same_text & self_or_text


def attend_forward(queries, key_rows, value_rows, segments):
    outputs = []
    log_parts = []
    for block_index in range(L // QBLK):
        first_row = block_index * QBLK
        query_block = queries[first_row : first_row + QBLK]
        allowed = allowed_pairs(segments[first_row : first_row + QBLK], segments, first_row)
        scores = (
            jnp.einsum("qhd,khd->hqk", query_block, key_rows, preferred_element_type=jnp.float32)
            * 0.125
        )
        masked = jnp.where(allowed[None], scores, -1e30)
        highest = jnp.max(masked, axis=-1, keepdims=True)
        exponents = jnp.exp(masked - highest)
        totals = jnp.sum(exponents, axis=-1, keepdims=True)
        weights = (exponents / totals).astype(jnp.bfloat16)
        outputs.append(
            jnp.einsum(
                "hqk,khd->qhd", weights, value_rows, preferred_element_type=jnp.float32
            ).astype(jnp.bfloat16)
        )
        log_parts.append((highest + jnp.log(totals))[..., 0])
    return (jnp.concatenate(outputs, axis=0), jnp.concatenate(log_parts, axis=1))


def attend_backward(queries, key_rows, value_rows, segments, log_sums, grad_heads):
    grad_keys = jnp.zeros(key_rows.shape, jnp.float32)
    grad_values = jnp.zeros(value_rows.shape, jnp.float32)
    grad_queries = []
    for block_index in range(L // QBLK):
        first_row = block_index * QBLK
        query_block = queries[first_row : first_row + QBLK]
        grad_block = grad_heads[first_row : first_row + QBLK]
        allowed = allowed_pairs(segments[first_row : first_row + QBLK], segments, first_row)
        scores = (
            jnp.einsum("qhd,khd->hqk", query_block, key_rows, preferred_element_type=jnp.float32)
            * 0.125
        )
        masked = jnp.where(allowed[None], scores, -1e30)
        probs = jnp.exp(masked - log_sums[:, first_row : first_row + QBLK, None])
        rounded = probs.astype(jnp.bfloat16)
        grad_probs = jnp.einsum(
            "qhd,khd->hqk", grad_block, value_rows, preferred_element_type=jnp.float32
        )
        inner = jnp.sum(probs * grad_probs, axis=-1, keepdims=True)
        grad_scores = (probs * (grad_probs - inner)).astype(jnp.bfloat16)
        grad_queries.append(
            jnp.einsum("hqk,khd->qhd", grad_scores, key_rows, preferred_element_type=jnp.float32)
            * 0.125
        )
        grad_keys = (
            grad_keys
            + jnp.einsum(
                "hqk,qhd->khd", grad_scores, query_block, preferred_element_type=jnp.float32
            )
            * 0.125
        )
        grad_values = grad_values + jnp.einsum(
            "hqk,qhd->khd", rounded, grad_block, preferred_element_type=jnp.float32
        )
    return (
        jnp.concatenate(grad_queries, axis=0).astype(jnp.bfloat16),
        grad_keys.astype(jnp.bfloat16),
        grad_values.astype(jnp.bfloat16),
    )


def block_forward(
    stream_in,
    segment_ids,
    ln1_gain,
    ln1_bias,
    w_qkv,
    w_out,
    attn_bias,
    ln2_gain,
    ln2_bias,
    w_up,
    w_down,
    mlp_bias,
):
    own_rows = stream_in.shape[0]
    normed_one = layer_norm(stream_in, ln1_gain, ln1_bias).astype(jnp.bfloat16)
    gathered_one = lax.all_gather(normed_one, "mp", axis=0, tiled=True)
    tokens_all = gathered_one.shape[0]
    local_width = w_qkv.shape[2]
    heads_local = local_width // HD
    packed = jnp.dot(
        gathered_one, w_qkv.reshape(D, 3 * local_width), preferred_element_type=jnp.float32
    ).astype(jnp.bfloat16)
    packed = packed.reshape(tokens_all // L, L, 3, heads_local, HD)
    queries = packed[:, :, 0]
    key_rows = packed[:, :, 1]
    value_rows = packed[:, :, 2]
    attended, log_sums = lax.map(
        lambda per_seq: attend_forward(per_seq[0], per_seq[1], per_seq[2], per_seq[3]),
        (queries, key_rows, value_rows, segment_ids.reshape(tokens_all // L, L)),
    )
    attended_flat = attended.reshape(tokens_all, local_width)
    attn_rows = lax.psum_scatter(
        jnp.dot(
            lax.slice_in_dim(attended_flat, 0, own_rows * lax.axis_size("mp"), axis=0),
            w_out,
            preferred_element_type=jnp.float32,
        ),
        "mp",
        scatter_dimension=0,
        tiled=True,
    )
    stream_mid = stream_in + attn_rows + attn_bias
    normed_two = layer_norm(stream_mid, ln2_gain, ln2_bias).astype(jnp.bfloat16)
    gathered_two = lax.all_gather(normed_two, "mp", axis=0, tiled=True)
    pre_act = jnp.dot(gathered_two, w_up, preferred_element_type=jnp.float32)
    activation = jax.nn.gelu(pre_act, approximate=True).astype(jnp.bfloat16)
    mlp_rows = lax.psum_scatter(
        jnp.dot(
            lax.slice_in_dim(activation, 0, own_rows * lax.axis_size("mp"), axis=0),
            w_down,
            preferred_element_type=jnp.float32,
        ).astype(jnp.bfloat16),
        "mp",
        scatter_dimension=0,
        tiled=True,
    ).astype(jnp.float32)
    output = stream_mid + mlp_rows + mlp_bias
    saved = (
        stream_mid,
        gathered_one,
        queries,
        key_rows,
        value_rows,
        attended_flat,
        log_sums,
        gathered_two,
        pre_act,
        activation,
    )
    return (output, saved)


def contract_rows(left, right):
    return lax.dot_general(
        left, right, (((0,), (0,)), ((), ())), preferred_element_type=jnp.float32
    )


def contract_cols(left, right):
    return lax.dot_general(
        left, right, (((1,), (1,)), ((), ())), preferred_element_type=jnp.float32
    )


def on_device(
    token_ids,
    segment_ids,
    timesteps,
    token_table,
    time_table,
    ln1_gain,
    ln1_bias,
    w_qkv,
    w_out,
    attn_bias,
    ln2_gain,
    ln2_bias,
    w_up,
    w_down,
    mlp_bias,
    cotangent,
):
    group_size = lax.axis_size("mp")
    member = lax.axis_index("mp")
    tokens_all = token_ids.shape[0]
    own_rows = tokens_all // group_size
    seq_count = timesteps.shape[0]
    local_width = token_table.shape[1]
    step_match = timesteps[:, None] == jnp.arange(time_table.shape[0])[None, :]
    time_rows = jnp.dot(
        step_match.astype(jnp.bfloat16), time_table, preferred_element_type=jnp.float32
    )
    embedded = (
        token_table[token_ids].astype(jnp.float32).reshape(seq_count, L, local_width)
        + time_rows[:, None, :]
    )
    stream_in = lax.all_to_all(
        embedded.reshape(tokens_all, local_width), "mp", split_axis=0, concat_axis=1, tiled=True
    )
    weights = (
        ln1_gain,
        ln1_bias,
        w_qkv,
        w_out,
        attn_bias,
        ln2_gain,
        ln2_bias,
        w_up,
        w_down,
        mlp_bias,
    )
    output, saved = block_forward(stream_in, segment_ids, *weights)
    repeated, saved = block_forward(lax.optimization_barrier(stream_in), segment_ids, *weights)
    (
        stream_mid,
        gathered_one,
        queries,
        key_rows,
        value_rows,
        attended_flat,
        log_sums,
        gathered_two,
        pre_act,
        activation,
    ) = saved
    own_segments = lax.dynamic_slice_in_dim(segment_ids, member * own_rows, own_rows, 0)
    grad_out = cotangent.astype(jnp.float32) * (own_segments != 0).astype(jnp.float32)[:, None]
    grad_mlp_bias = jnp.sum(grad_out, axis=0)
    grad_mlp_all = lax.all_gather(grad_out.astype(jnp.bfloat16), "mp", axis=0, tiled=True)
    grad_w_down = contract_rows(activation, grad_mlp_all)
    grad_act = contract_cols(grad_mlp_all, w_down)
    gelu_back = jax.vjp(lambda inner: jax.nn.gelu(inner, approximate=True), pre_act)[1]
    grad_pre = gelu_back(grad_act)[0].astype(jnp.bfloat16)
    grad_w_up = contract_rows(gathered_two, grad_pre)
    grad_norm_two = lax.psum_scatter(
        contract_cols(
            lax.slice_in_dim(grad_pre, 0, own_rows * lax.axis_size("mp"), axis=0), w_up
        ).astype(jnp.bfloat16),
        "mp",
        scatter_dimension=0,
        tiled=True,
    ).astype(jnp.float32)
    norm_back_two = jax.vjp(layer_norm, stream_mid, ln2_gain, ln2_bias)[1]
    grad_mid_norm, grad_ln2_gain, grad_ln2_bias = norm_back_two(grad_norm_two)
    grad_mid = grad_out + grad_mid_norm
    grad_attn_bias = jnp.sum(grad_mid, axis=0)
    grad_attn_all = lax.all_gather(grad_mid.astype(jnp.bfloat16), "mp", axis=0, tiled=True)
    grad_w_out = contract_rows(attended_flat, grad_attn_all)
    grad_attended = contract_cols(grad_attn_all, w_out).astype(jnp.bfloat16)
    heads_local = local_width // HD
    grad_heads = grad_attended.reshape(seq_count, L, heads_local, HD)
    grad_q, grad_k, grad_v = lax.map(
        lambda per_seq: attend_backward(
            per_seq[0], per_seq[1], per_seq[2], per_seq[3], per_seq[4], per_seq[5]
        ),
        (queries, key_rows, value_rows, segment_ids.reshape(seq_count, L), log_sums, grad_heads),
    )
    grad_packed = jnp.stack((grad_q, grad_k, grad_v), axis=2).reshape(tokens_all, 3 * local_width)
    grad_w_qkv = contract_rows(gathered_one, grad_packed).reshape(D, 3, local_width)
    qkv_flat = w_qkv.reshape(D, 3 * local_width)
    grad_norm_one = lax.psum_scatter(
        contract_cols(grad_packed, qkv_flat).astype(jnp.bfloat16),
        "mp",
        scatter_dimension=0,
        tiled=True,
    ).astype(jnp.float32)
    norm_back_one = jax.vjp(layer_norm, stream_in, ln1_gain, ln1_bias)[1]
    grad_in_norm, grad_ln1_gain, grad_ln1_bias = norm_back_one(grad_norm_one)
    input_grad = grad_mid + grad_in_norm
    grad_columns = lax.all_to_all(
        as_sent(input_grad), "mp", split_axis=1, concat_axis=0, tiled=True
    ).astype(input_grad.dtype)
    grad_token_table = (
        jnp.zeros((token_table.shape[0], local_width), jnp.float32).at[token_ids].add(grad_columns)
    )
    seq_of_row = (member * own_rows + jnp.arange(own_rows)) // L
    seq_onehot = (seq_of_row[:, None] == jnp.arange(seq_count)[None, :]).astype(jnp.float32)
    seq_sums = lax.dot_general(
        seq_onehot,
        input_grad,
        (((0,), (0,)), ((), ())),
        precision=PRECISE,
        preferred_element_type=jnp.float32,
    )
    grad_time_table = lax.dot_general(
        step_match.astype(jnp.float32),
        seq_sums,
        (((0,), (0,)), ((), ())),
        precision=PRECISE,
        preferred_element_type=jnp.float32,
    )
    small_sums = lax.psum(
        (
            grad_time_table,
            grad_ln1_gain,
            grad_ln1_bias,
            grad_attn_bias,
            grad_ln2_gain,
            grad_ln2_bias,
            grad_mlp_bias,
        ),
        ("dp", "mp"),
    )
    sum_qkv, sum_out, sum_up, sum_down, sum_token = (
        lax.psum_scatter(grad_w_qkv, "dp", scatter_dimension=0, tiled=True),
        lax.psum_scatter(grad_w_out, "dp", scatter_dimension=1, tiled=True),
        lax.psum_scatter(grad_w_up, "dp", scatter_dimension=0, tiled=True),
        lax.psum_scatter(grad_w_down, "dp", scatter_dimension=1, tiled=True),
        lax.psum_scatter(grad_token_table, "dp", scatter_dimension=0, tiled=True),
    )
    return (
        output.astype(jnp.bfloat16),
        input_grad,
        sum_token,
        small_sums[0],
        small_sums[1],
        small_sums[2],
        sum_qkv,
        sum_out,
        small_sums[3],
        small_sums[4],
        small_sums[5],
        sum_up,
        sum_down,
        small_sums[6],
    )


def solution(mesh):
    placed = (
        P("dp"),
        P("dp"),
        P("dp"),
        P(None, "mp"),
        P(None, "mp"),
        P(),
        P(),
        P(None, None, "mp"),
        P("mp", None),
        P(),
        P(),
        P(),
        P(None, "mp"),
        P("mp", None),
        P(),
        P(("dp", "mp"), None),
    )
    return jax.shard_map(
        on_device,
        mesh=mesh,
        in_specs=placed,
        out_specs=(
            P(("dp", "mp"), None),
            P(("dp", "mp"), None),
            P("dp", "mp"),
            P(),
            P(),
            P(),
            P("dp", None, "mp"),
            P("mp", "dp"),
            P(),
            P(),
            P(),
            P("dp", "mp"),
            P("mp", "dp"),
            P(),
        ),
        check_vma=False,
    )
```

profile of v0, /device:TPU:0, one launch (start us, length us, event | category | flops | bytes accessed | tf_op | source)
XLA Modules:
  0.0 1000.9 jit_solution(7275968648900086361)
XLA Ops:
  9.9 5.9 copy.54
  15.8 6.2 gather_fusion
  22.6 26.2 %all_to_all.29 = f32[4,256,192]{1,2,0:T(8,128)S(1)} all-to-all(f32[4,256,192]{1,2,0:T(8,128)S(1)} %broadcast_add_fusion), channel_id=1, replica_groups=mesh['dp'=8,'mp'=4] {'mp'}, dimensions={0} | all-to-all | bytes 1572864 | tf_op jit(solution)/shard_map/all_to_all | solution.py:218
  51.0 2.1 fusion.42
  53.1 33.7 %all-gather.13.cloned.1.call-done = bf16[1024,768]{1,0:T(8,128)(2,1)} async-done(((bf16[256,768]{1,0:T(8,128)(2,1)}), bf16[1024,768]{1,0:T(8,128)(2,1)}) %all-gather.13.cloned.1.call-update) | async-done | bytes 1572880 | tf_op jit(solution)/shard_map/all_gather | solution.py:117
  86.8 2.8 convolution_convert_fusion.3
  101.0 2.3 fusion.135
  104.4 58.2 %reduce-scatter.17.cloned.1.call-done = f32[256,768]{1,0:T(8,128)} async-done(((f32[1024,768]{1,0:T(8,128)}), f32[256,768]{1,0:T(8,128)}) %reduce-scatter.17.cloned.1.call-update) | async-done | bytes 786448 | tf_op jit(solution)/shard_map/reduce_scatter | solution.py:133
  165.4 36.5 %all-gather.11.cloned.1.call-done = bf16[1024,768]{1,0:T(8,128)(2,1)} async-done(((bf16[256,768]{1,0:T(8,128)(2,1)}), bf16[1024,768]{1,0:T(8,128)(2,1)}) %all-gather.11.cloned.1.call-update) | async-done | bytes 1572880 | tf_op jit(solution)/shard_map/all_gather | solution.py:250
  201.9 4.8 fusion.134
  206.7 33.2 %all-gather.15.cloned.1.call-done = bf16[1024,768]{1,0:T(8,128)(2,1)} async-done(((bf16[256,768]{1,0:T(8,128)(2,1)}), bf16[1024,768]{1,0:T(8,128)(2,1)}) %all-gather.15.cloned.1.call-update) | async-done | bytes 1572880 | tf_op jit(solution)/shard_map/all_gather | solution.py:145
  239.9 6.5 fusion.16
  247.7 2.6 convolution_convert_fusion.1
  250.3 34.3 %reduce-scatter.19.cloned.1.call-done = bf16[256,768]{1,0:T(8,128)(2,1)} async-done(((bf16[1024,768]{1,0:T(8,128)(2,1)}), bf16[256,768]{1,0:T(8,128)(2,1)}) %reduce-scatter.19.cloned.1.call-update) | async-done | bytes 393232 | tf_op jit(solution)/shard_map/reduce_scatter | solution.py:256
  288.5 2.1 fusion.120
  293.0 34.7 %all-gather.17.cloned.1.call-done = bf16[1024,768]{1,0:T(8,128)(2,1)} async-done(((bf16[256,768]{1,0:T(8,128)(2,1)}), bf16[1024,768]{1,0:T(8,128)(2,1)}) %all-gather.17.cloned.1.call-update) | async-done | bytes 1572880 | tf_op jit(solution)/shard_map/all_gather | solution.py:268
  327.7 2.2 convolution_convert_fusion.5
  329.9 3.9 multiply_reduce_fusion.1
  346.4 2.6 convolution_convert_fusion
  351.4 31.9 %reduce-scatter.21.cloned.1.call-done = bf16[256,768]{1,0:T(8,128)(2,1)} async-done(((bf16[1024,768]{1,0:T(8,128)(2,1)}), bf16[256,768]{1,0:T(8,128)(2,1)}) %reduce-scatter.21.cloned.1.call-update) | async-done | bytes 393232 | tf_op jit(solution)/shard_map/reduce_scatter | solution.py:282
  385.9 2.1 fusion.88
  387.9 2.5 fusion.121
  391.0 35.7 %all-gather.7.cloned.1.call-done = bf16[1024,768]{1,0:T(8,128)(2,1)} async-done(((bf16[256,768]{1,0:T(8,128)(2,1)}), bf16[1024,768]{1,0:T(8,128)(2,1)}) %all-gather.7.cloned.1.call-update) | async-done | bytes 1572880 | tf_op jit(solution)/shard_map/all_gather | solution.py:117
  426.7 3.8 convolution_convert_fusion.4
  430.5 6.0 fusion.128
  436.5 6.0 fusion.129
  442.6 4.2 fusion.76
  447.3 2.2 fusion.75
  449.6 2.3 fusion.133
  451.9 59.2 %reduce-scatter.13.cloned.1.call-done = f32[256,768]{1,0:T(8,128)} async-done(((f32[1024,768]{1,0:T(8,128)}), f32[256,768]{1,0:T(8,128)}) %reduce-scatter.13.cloned.1.call-update) | async-done | bytes 786448 | tf_op jit(solution)/shard_map/reduce_scatter | solution.py:133
  513.7 3.0 convolution_bitcast_fusion
  517.0 25.0 %all_to_all.30 = bf16[256,4,192]{0,2,1:T(8,128)(2,1)S(1)} all-to-all(bf16[256,4,192]{0,2,1:T(8,128)(2,1)S(1)} %bitcast.201), channel_id=1, replica_groups=mesh['dp'=8,'mp'=4] {'mp'}, dimensions={1} | all-to-all | bytes 786432 | tf_op jit(solution)/shard_map/all_to_all | solution.py:291
  543.4 10.3 %scatter_custom_fusion = f32[8192,192]{1,0:T(8,128)} fusion(s32[1024]{0:T(1024)} %get-tuple-element.151, f32[1024,192]{1,0:T(8,128)} %bitcast.204, f32[]{:T(128)} %constant.117.clone.1), kind=kCustom, calls=%fused_computation.31 | custom fusion | flops 196608 | bytes 6291968 | tf_op jit(solution)/shard_map/scatter-add | solution.py:295
  553.8 4.4 all-gather.9.cloned.1.call-done
  558.2 5.8 convolution_convert_fusion.2
  564.0 5.1 fusion.45
  569.1 4.8 fusion.136
  574.1 4.7 fusion.47
  581.4 14.4 %reduce-scatter.31.cloned.1.call-done = f32[96,192]{1,0:T(8,128)} async-done(((f32[768,192]{1,0:T(8,128)}), f32[96,192]{1,0:T(8,128)}) %reduce-scatter.31.cloned.1.call-update) | async-done | bytes 73744
  597.5 40.3 %all-reduce = (f32[768]{0:T(1024)}, f32[768]{0:T(1024)}, f32[768]{0:T(1024)}, f32[768]{0:T(1024)}, f32[768]{0:T(1024)}, /*index=5*/f32[768]{0:T(1024)}) all-reduce(f32[768]{0:T(1024)S(1)} %copy-done.35, f32[768]{0:T(1024)S(1)} %copy-done.34, f32[768]{0:T(1024)S(1)} %copy-done.32, ...), channel_id=1, replica_groups=mesh['dp'=8,'mp'=4] {'dp','mp'}, use_global_device_ids=true, to_apply=%region_31.32 | all-reduce | flops 4608 | bytes 36864 | tf_op jit(solution)/shard_map/psum | solution.py:313
  637.9 33.2 %reduce-scatter.23.cloned.1.call-done = f32[1024,192]{1,0:T(8,128)} async-done(((f32[8192,192]{1,0:T(8,128)}), f32[1024,192]{1,0:T(8,128)}) %reduce-scatter.23.cloned.1.call-update) | async-done | bytes 786448 | tf_op jit(solution)/shard_map/reduce_scatter | solution.py:330
  671.1 2.4 copy.64
  673.5 35.3 %reduce-scatter.15.cloned.1.call-done = bf16[256,768]{1,0:T(8,128)(2,1)} async-done(((bf16[1024,768]{1,0:T(8,128)(2,1)}), bf16[256,768]{1,0:T(8,128)(2,1)}) %reduce-scatter.15.cloned.1.call-update) | async-done | bytes 393232 | tf_op jit(solution)/shard_map/reduce_scatter | solution.py:148
  710.7 43.8 %reduce-scatter.29.cloned.1.call-done = f32[768,96]{0,1:T(8,128)} async-done(((f32[768,768]{0,1:T(8,128)}), f32[768,96]{0,1:T(8,128)}) %reduce-scatter.29.cloned.1.call-update) | async-done | bytes 294928 | tf_op jit(solution)/shard_map/reduce_scatter | solution.py:329
  754.5 46.3 %reduce-scatter.27.cloned.1.call-done = f32[96,768]{1,0:T(8,128)} async-done(((f32[768,768]{1,0:T(8,128)}), f32[96,768]{1,0:T(8,128)}) %reduce-scatter.27.cloned.1.call-update) | async-done | bytes 294928 | tf_op jit(solution)/shard_map/reduce_scatter | solution.py:328
  800.8 46.7 %reduce-scatter.25.cloned.1.call-done = f32[96,3,192]{2,0,1:T(8,128)} async-done(((f32[768,3,192]{2,0,1:T(8,128)}), f32[96,3,192]{2,0,1:T(8,128)}) %reduce-scatter.25.cloned.1.call-update) | async-done | bytes 221200 | tf_op jit(solution)/shard_map/reduce_scatter | solution.py:326
  847.4 143.0 %all-reduce.3.cloned.1.call-done = f32[1000,768]{1,0:T(8,128)} async-done(((f32[1000,768]{1,0:T(8,128)}), f32[1000,768]{1,0:T(8,128)}) %all-reduce.3.cloned.1.call-update) | async-done | bytes 3072016 | tf_op jit(solution)/shard_map/psum | solution.py:313
  990.4 3.7 copy.73
  (199 shorter events, 56.1 us)
Async XLA Ops:
  7.2 232.7 %copy-start = (bf16[768,768]{1,0:T(8,128)(2,1)S(1)}, bf16[768,768]{1,0:T(8,128)(2,1)}, u32[]{:S(2)}) copy-start(bf16[768,768]{1,0:T(8,128)(2,1)} %param.28) | copy-start | bytes 3538948
  7.2 79.6 %all-gather.13.cloned.1.call-start = ((), (), s32[]{:S(2)}) async-start(), calls=%async_computation.17 | async-start | bytes 1966080 | tf_op jit(solution)/shard_map/all_gather | solution.py:117
  15.8 6.5 copy-start.17
  22.4 27.0 %copy-start.19 = (f32[768]{0:T(1024)S(1)}, f32[768]{0:T(1024)}, u32[]{:S(2)}) copy-start(f32[768]{0:T(1024)} %param.21) | copy-start | bytes 9220
  22.4 27.0 %copy-start.36 = (f32[768]{0:T(1024)S(1)}, f32[768]{0:T(1024)}, u32[]{:S(2)}) copy-start(f32[768]{0:T(1024)} %param.22) | copy-start | bytes 9220
  22.6 28.4 %copy-start.20 = (s32[1024]{0:T(1024)S(1)}, s32[1024]{0:T(1024)}, u32[]{:S(2)}) copy-start(s32[1024]{0:T(1024)} %param.17) | copy-start | bytes 12292
  50.5 112.2 %reduce-scatter.17.cloned.1.call-start = ((), (), s32[]{:S(2)}) async-start(), calls=%async_computation.18 | async-start | bytes 3932160 | tf_op jit(solution)/shard_map/reduce_scatter | solution.py:133
  53.1 42.2 %copy-start.13 = (pred[512,1024]{1,0:T(8,128)(4,1)}, pred[512,1024]{1,0:T(8,128)(4,1)S(1)}, u32[]{:S(2)}) copy-start(pred[512,1024]{1,0:T(8,128)(4,1)S(1)} %get-tuple-element.153) | copy-start | bytes 1572868
  86.8 2.8 copy-start.15
  89.6 8.6 copy-start.5
  91.1 2.7 copy-start.21
  101.0 61.7 %copy-start.25 = (f32[768]{0:T(1024)S(1)}, f32[768]{0:T(1024)}, u32[]{:S(2)}) copy-start(f32[768]{0:T(1024)} %param.25) | copy-start | bytes 9220
  103.3 60.9 %copy-start.18 = (f32[768]{0:T(1024)S(1)}, f32[768]{0:T(1024)}, u32[]{:S(2)}) copy-start(f32[768]{0:T(1024)} %param.26) | copy-start | bytes 9220
  103.3 98.6 %all-gather.11.cloned.1.call-start = ((), (), s32[]{:S(2)}) async-start(), calls=%async_computation.16 | async-start | bytes 1966080 | tf_op jit(solution)/shard_map/all_gather | solution.py:250
  104.4 135.5 %all-gather.15.cloned.1.call-start = ((), (), s32[]{:S(2)}) async-start(), calls=%async_computation.19 | async-start | bytes 1966080 | tf_op jit(solution)/shard_map/all_gather | solution.py:145
  164.2 122.3 %copy-start.28 = (f32[256]{0:T(256)}, f32[256]{0:T(256)S(1)}, u32[]{:S(2)}) copy-start(f32[256]{0:T(256)S(1)} %fusion.104) | copy-start | bytes 3076
  165.2 119.4 %reduce-scatter.19.cloned.1.call-start = ((), (), s32[]{:S(2)}) async-start(), calls=%async_computation.20 | async-start | bytes 1966080 | tf_op jit(solution)/shard_map/reduce_scatter | solution.py:256
  250.3 77.4 %all-gather.17.cloned.1.call-start = ((), (), s32[]{:S(2)}) async-start(), calls=%async_computation.21 | async-start | bytes 1966080 | tf_op jit(solution)/shard_map/all_gather | solution.py:268
  291.5 91.8 %reduce-scatter.21.cloned.1.call-start = ((), (), s32[]{:S(2)}) async-start(), calls=%async_computation.22 | async-start | bytes 1966080 | tf_op jit(solution)/shard_map/reduce_scatter | solution.py:282
  329.9 4.0 slice-start.2
  329.9 4.7 slice-start.3
  333.9 3.9 slice-start
  334.6 3.1 slice-start.1
  349.0 77.7 %all-gather.7.cloned.1.call-start = ((), (), s32[]{:S(2)}) async-start(), calls=%async_computation.12 | async-start | bytes 1966080 | tf_op jit(solution)/shard_map/all_gather | solution.py:117
  390.5 40.0 %copy-start.16 = (pred[512,1024]{1,0:T(8,128)(4,1)S(1)}, pred[512,1024]{1,0:T(8,128)(4,1)}, u32[]{:S(2)}) copy-start(pred[512,1024]{1,0:T(8,128)(4,1)} %get-tuple-element.154) | copy-start | bytes 1572868
  390.5 120.6 %reduce-scatter.13.cloned.1.call-start = ((), (), s32[]{:S(2)}) async-start(), calls=%async_computation.13 | async-start | bytes 3932160 | tf_op jit(solution)/shard_map/reduce_scatter | solution.py:133
  430.5 6.1 copy-start.14
  442.6 4.7 copy-start.41
  451.8 60.9 %copy-start.27 = (f32[768]{0:T(1024)S(1)}, f32[768]{0:T(1024)}, u32[]{:S(2)}) copy-start(f32[768]{0:T(1024)} %param.27) | copy-start | bytes 9220
  451.8 61.9 %copy-start.4 = (bf16[1024,3,64]{0,2,1:T(8,128)(2,1)S(1)}, bf16[1024,3,64]{0,2,1:T(8,128)(2,1)}, u32[]{:S(2)}) copy-start(bf16[1024,3,64]{0,2,1:T(8,128)(2,1)} %copy-done.3) | copy-start | bytes 1179652
  451.9 106.3 %all-gather.9.cloned.1.call-start = ((), (), s32[]{:S(2)}) async-start(), calls=%async_computation.14 | async-start | bytes 1966080 | tf_op jit(solution)/shard_map/all_gather | solution.py:145
  512.4 4.4 copy-start.9
  513.6 82.2 %reduce-scatter.31.cloned.1.call-start = ((), (), s32[]{:S(2)}) async-start(), calls=%async_computation.28 | async-start | bytes 884736
  516.7 154.4 %reduce-scatter.23.cloned.1.call-start = ((), (), s32[]{:S(2)}) async-start(), calls=%async_computation.23 | async-start | bytes 9437184 | tf_op jit(solution)/shard_map/reduce_scatter | solution.py:330
  553.7 10.3 %copy-start.39 = (bf16[1024,768]{1,0:T(8,128)(2,1)S(1)}, bf16[1024,768]{1,0:T(8,128)(2,1)}, u32[]{:S(2)}) copy-start(bf16[1024,768]{1,0:T(8,128)(2,1)} %all-gather.11.cloned.1.call-done) | copy-start | bytes 4718596
  553.7 155.1 %reduce-scatter.15.cloned.1.call-start = ((), (), s32[]{:S(2)}) async-start(), calls=%async_computation.15 | async-start | bytes 1966080 | tf_op jit(solution)/shard_map/reduce_scatter | solution.py:148
  564.0 190.5 %reduce-scatter.29.cloned.1.call-start = ((), (), s32[]{:S(2)}) async-start(), calls=%async_computation.27 | async-start | bytes 2654208 | tf_op jit(solution)/shard_map/reduce_scatter | solution.py:329
  569.1 231.7 %reduce-scatter.27.cloned.1.call-start = ((), (), s32[]{:S(2)}) async-start(), calls=%async_computation.26 | async-start | bytes 2654208 | tf_op jit(solution)/shard_map/reduce_scatter | solution.py:328
  574.0 273.4 %reduce-scatter.25.cloned.1.call-start = ((), (), s32[]{:S(2)}) async-start(), calls=%async_computation.25 | async-start | bytes 2654208 | tf_op jit(solution)/shard_map/reduce_scatter | solution.py:326
  574.0 4.8 copy-start.7
  578.8 411.6 %all-reduce.3.cloned.1.call-start = ((), (), s32[]{:S(2)}) async-start(), calls=%async_computation.24 | async-start | bytes 6144000 | tf_op jit(solution)/shard_map/psum | solution.py:313
  579.5 18.0 %copy-start.30 = (f32[768]{0:T(1024)S(1)}, f32[768]{0:T(1024)}, u32[]{:S(2)}) copy-start(f32[768]{0:T(1024)} %get-tuple-element.129) | copy-start | bytes 9220
  579.5 18.0 %copy-start.31 = (f32[768]{0:T(1024)S(1)}, f32[768]{0:T(1024)}, u32[]{:S(2)}) copy-start(f32[768]{0:T(1024)} %get-tuple-element.125) | copy-start | bytes 9220
  579.5 18.0 %copy-start.32 = (f32[768]{0:T(1024)S(1)}, f32[768]{0:T(1024)}, u32[]{:S(2)}) copy-start(f32[768]{0:T(1024)} %get-tuple-element.139) | copy-start | bytes 9220
  579.5 18.0 %copy-start.33 = (f32[768]{0:T(1024)S(1)}, f32[768]{0:T(1024)}, u32[]{:S(2)}) copy-start(f32[768]{0:T(1024)} %get-tuple-element.148) | copy-start | bytes 9220
  579.5 18.1 %copy-start.34 = (f32[768]{0:T(1024)S(1)}, f32[768]{0:T(1024)}, u32[]{:S(2)}) copy-start(f32[768]{0:T(1024)} %get-tuple-element.131) | copy-start | bytes 9220
  579.5 18.1 %copy-start.35 = (f32[768]{0:T(1024)S(1)}, f32[768]{0:T(1024)}, u32[]{:S(2)}) copy-start(f32[768]{0:T(1024)} %get-tuple-element.127) | copy-start | bytes 9220
  581.4 127.4 %copy-start.38 = (f32[768]{0:T(1024)S(1)}, f32[768]{0:T(1024)}, u32[]{:S(2)}) copy-start(f32[768]{0:T(1024)} %param.30) | copy-start | bytes 9220
  (16 other events, 29.3 us)
Sparse Core Ops, SparseCore 0:
  50.6 36.1 all-gather.12
  103.5 59.1 reduce-scatter.16
  164.8 37.0 all-gather.10
  203.9 35.9 all-gather.14
  250.4 34.1 reduce-scatter.18
  291.6 36.0 all-gather.16
  349.1 34.1 reduce-scatter.20
  390.6 36.0 all-gather.6
  452.0 59.0 reduce-scatter.12
  513.8 44.3 all-gather.8
  561.9 33.9 reduce-scatter.30
  599.2 71.8 reduce-scatter.22
  673.5 35.2 reduce-scatter.14
  713.0 41.4 reduce-scatter.28
  758.3 42.4 reduce-scatter.26
  804.9 42.4 reduce-scatter.24
  853.4 137.0 all-reduce.2
where the time goes:
time: 1000 us
  waiting for transfers between devices  725 us (72%)
  blocking collectives  91.6 us (9%)
  matrix products  89.9 us (9%)
  other arithmetic  48.9 us (5%)
  local copies, waits for them, and re-layouts  28.3 us (3%)
  between operations  15.6 us (2%)
    psum x1, waiting for transfers between devices, on_device(): lax.psum((grad_time_table, grad_ln1_gain, grad_ln1_bias, grad_attn_bias,...  143 us
    reduce_scatter x2, waiting for transfers between devices, block_forward(): lax.psum_scatter(jnp.dot(lax.slice_in_dim(attended_flat, 0, own_rows * la...  117 us
    all_gather x2, waiting for transfers between devices, block_forward(): gathered_one = lax.all_gather(normed_one, 'mp', axis=0, tiled=True)  69.5 us
    reduce_scatter x1, waiting for transfers between devices, on_device(): lax.psum_scatter(grad_w_qkv, 'dp', scatter_dimension=0, tiled=True)  46.7 us
    reduce_scatter x1, waiting for transfers between devices, on_device(): lax.psum_scatter(grad_w_up, 'dp', scatter_dimension=0, tiled=True)  46.3 us
    reduce_scatter x1, waiting for transfers between devices, on_device(): lax.psum_scatter(grad_w_down, 'dp', scatter_dimension=1, tiled=True)  43.8 us
    psum x1, blocking collectives, on_device(): lax.psum((grad_time_table, grad_ln1_gain, grad_ln1_bias, grad_attn_bias,...  40.3 us
    all_gather x2, waiting for transfers between devices, block_forward(): gathered_two = lax.all_gather(normed_two, 'mp', axis=0, tiled=True)  37.6 us
  transfers between devices with their start and end apart: 17, of which 17 were waited for; matrix products, arithmetic and copies ran while one was open for 6% of the time, Pallas kernels for 0%

commit v1 on v0

v1 whole, which is shorter than its diff:
```python
import functools

import jax
import jax.numpy as jnp
from jax import lax
from jax.experimental import pallas as pl
from jax.experimental.pallas import tpu as pltpu
from jax.sharding import PartitionSpec as P

D = 768
HD = 64
L = 1024
QBLK = 512
BF = jnp.bfloat16
F32 = jnp.float32
MESH = pl.DeviceIdType.MESH
ANY = pl.BlockSpec(memory_space=pl.ANY)
DMA = pltpu.SemaphoreType.DMA


class Place:
    def __init__(self):
        self.p = p = lax.axis_index("dp")
        self.j = lax.axis_index("mp")
        core, x, y = p % 2, (p // 2) % 2, p // 4
        self.core, self.m = core, p // 2
        self.px = p + 2 - 4 * x
        self.py = p + 4 - 8 * y
        self.pd = self.px + 4 - 8 * y
        self.pc = p + 1 - 2 * core
        self.mx = self.px // 2
        self.my = self.py // 2
        self.md = self.pd // 2

    def z(self, hop):
        return (self.p, (self.j + hop) % 4)

    def at(self, dp):
        return (dp, self.j)


def meet(devices):
    barrier = pltpu.get_barrier_semaphore()
    for device in devices:
        pl.semaphore_signal(barrier, inc=1, device_id=device, device_id_type=MESH)
    pl.semaphore_wait(barrier, len(devices))


def push(src, dst, send, recv, device):
    return pltpu.make_async_remote_copy(
        src_ref=src, dst_ref=dst, send_sem=send, recv_sem=recv, device_id=device, device_id_type=MESH
    )


def params(cid):
    return pltpu.CompilerParams(collective_id=cid, has_side_effects=True, vmem_limit_bytes=56 << 20)


def gather_kernel(emb, trow, ids, w2, wo, E, TR, IDS, W2, WO, zs, zr, ts, tr, is_, ir, ps, pr, ls):
    me = Place()
    p, j = me.p, me.j
    plane = [me.at((p + k) % 8) for k in range(1, 8)]
    meet([me.z(1), me.z(2), me.z(3)] + plane)

    def part(a, q, piece, half=None):
        if a == 0:
            lo, n = (0, 96) if half is None else (48 * half, 48)
            return W2.at[q, :, pl.ds(96 * piece + lo, n), :]
        lo, n = (0, 144) if half is None else ((0, 80), (80, 64))[half]
        return WO.at[q, pl.ds(144 * piece + lo, n), :]

    own = (w2.at[:, pl.ds(96 * p, 96), :], wo.at[pl.ds(144 * p, 144), :])

    def quarter(d, k):
        return (j - k + 4) % 4 if d == 0 else (j + k) % 4

    def sends(d, k):
        return (j < 3) & (j >= k) if d == 0 else (j > 0) & (j + k <= 3)

    def gets(d, k):
        return j >= k + 1 if d == 0 else j + k + 1 <= 3

    def zcopy(d, k, a):
        q = quarter(d, k)
        if a == 2:
            src = emb if k == 0 else E.at[q]
            dst = E.at[q]
        else:
            src = own[a] if k == 0 else part(a, q, p)
            dst = part(a, q, p)
        return push(src, dst, zs.at[d, k, a], zr.at[d, k, a], me.z(1 if d == 0 else 3))

    def zgot(d, k, a):
        q = quarter(d, k + 1)
        dst = E.at[q] if a == 2 else part(a, q, p)
        return push(dst, dst, zs.at[d, k, a], zr.at[d, k, a], me.z(1))

    def zstart(k, arrays):
        for d in (0, 1):

            @pl.when(sends(d, k))
            def _():
                for a in arrays:
                    zcopy(d, k, a).start()

    def zwait(k, arrays):
        for d in (0, 1):

            @pl.when(gets(d, k))
            def _():
                for a in arrays:
                    zgot(d, k, a).wait_recv()

    def routes(d, k, a, stage):
        q = quarter(d, k + 1)
        if stage == 0:
            return [(part(a, q, p), me.px), (part(a, q, p), me.py), (part(a, q, p), me.pc)]
        if stage == 1:
            return [
                (part(a, q, me.py, 0), me.px),
                (part(a, q, me.px, 1), me.py),
                (part(a, q, me.px), me.pc),
                (part(a, q, me.py), me.pc),
            ]
        return [(part(a, q, me.pd), me.pc)]

    def arrivals(d, k, a, stage):
        q = quarter(d, k + 1)
        if stage == 0:
            return [part(a, q, me.px), part(a, q, me.py), part(a, q, me.pc)]
        if stage == 1:
            return [
                part(a, q, me.pd, 0),
                part(a, q, me.pd, 1),
                part(a, q, me.px + me.pc - p),
                part(a, q, me.py + me.pc - p),
            ]
        return [part(a, q, me.pd + me.pc - p)]

    def pstart(k, stage):
        for d in (0, 1):

            @pl.when(gets(d, k))
            def _():
                for a in (0, 1):
                    for i, (ref, dp) in enumerate(routes(d, k, a, stage)):
                        s = 3 * stage + i if stage < 2 else 7
                        push(ref, ref, ps.at[d, k, a, s], pr.at[d, k, a, s], me.at(dp)).start()

    def pwait(k, stage, which, send=False):
        for d in (0, 1):

            @pl.when(gets(d, k))
            def _():
                for a in (0, 1):
                    refs = [r for r, _ in routes(d, k, a, stage)] if send else arrivals(d, k, a, stage)
                    for i in which:
                        s = 3 * stage + i if stage < 2 else 7
                        c = push(refs[i], refs[i], ps.at[d, k, a, s], pr.at[d, k, a, s], me.at(me.pc))
                        c.wait_send() if send else c.wait_recv()

    locals_ = [
        pltpu.make_async_copy(emb, E.at[j], ls.at[0]),
        pltpu.make_async_copy(trow, TR.at[j], ls.at[1]),
        pltpu.make_async_copy(ids, IDS.at[p], ls.at[2]),
        pltpu.make_async_copy(w2, W2.at[j], ls.at[3]),
        pltpu.make_async_copy(wo, WO.at[j], ls.at[4]),
    ]
    small = [push(trow, TR.at[j], ts.at[k - 1], tr.at[k - 1], me.z(k)) for k in (1, 2, 3)]
    small += [push(ids, IDS.at[p], is_.at[k - 1], ir.at[k - 1], me.at((p + k) % 8)) for k in range(1, 8)]

    zstart(0, (0, 1))
    for c in small + locals_:
        c.start()
    zwait(0, (0, 1))
    zstart(1, (0, 1))
    pstart(0, 0)
    zstart(0, (2,))
    zwait(1, (0, 1))
    zstart(2, (0, 1))
    pwait(0, 0, (0, 1))
    pstart(0, 1)
    pstart(1, 0)
    zwait(0, (2,))
    zstart(1, (2,))
    zwait(2, (0, 1))
    pwait(0, 1, (0, 1))
    pstart(0, 2)
    pwait(1, 0, (0, 1))
    pstart(1, 1)
    pstart(2, 0)
    zwait(1, (2,))
    zstart(2, (2,))
    pwait(1, 1, (0, 1))
    pstart(1, 2)
    pwait(2, 0, (0, 1))
    pstart(2, 1)
    pwait(2, 1, (0, 1))
    pstart(2, 2)
    zwait(2, (2,))
    for k in range(3):
        pwait(k, 0, (2,))
        pwait(k, 1, (2, 3))
        pwait(k, 2, (0,))
        pwait(k, 0, (0, 1, 2), send=True)
        pwait(k, 1, (0, 1, 2, 3), send=True)
        pwait(k, 2, (0,), send=True)
        for d in (0, 1):

            @pl.when(sends(d, k))
            def _():
                for a in (0, 1, 2):
                    zcopy(d, k, a).wait_send()

    for c in small + locals_:
        c.wait()


def gather_all(emb, trow, ids, w2, wo):
    return pl.pallas_call(
        gather_kernel,
        out_shape=(
            jax.ShapeDtypeStruct((4,) + emb.shape, BF),
            jax.ShapeDtypeStruct((4,) + trow.shape, BF),
            jax.ShapeDtypeStruct((8,) + ids.shape, jnp.int32),
            jax.ShapeDtypeStruct((4,) + w2.shape, BF),
            jax.ShapeDtypeStruct((4,) + wo.shape, BF),
        ),
        in_specs=[ANY] * 5,
        out_specs=(ANY,) * 5,
        scratch_shapes=[
            DMA((2, 3, 3)),
            DMA((2, 3, 3)),
            DMA((3,)),
            DMA((3,)),
            DMA((7,)),
            DMA((7,)),
            DMA((2, 3, 2, 8)),
            DMA((2, 3, 2, 8)),
            DMA((5,)),
        ],
        compiler_params=params(0),
        name="gather_all",
    )(emb, trow, ids, w2, wo)


def exchange_kernel(x, out, send, recv, local):
    me = Place()
    meet([me.z(1), me.z(2), me.z(3)])
    mine = pltpu.make_async_copy(x.at[me.j], out.at[me.j], local)
    copies = [
        push(x.at[(me.j + k) % 4], out.at[me.j], send.at[k - 1], recv.at[k - 1], me.z(k)) for k in (1, 2, 3)
    ]
    for c in copies:
        c.start()
    mine.start()
    for c in copies:
        c.wait()
    mine.wait()


def exchange(x, cid, name):
    return pl.pallas_call(
        exchange_kernel,
        out_shape=jax.ShapeDtypeStruct(x.shape, x.dtype),
        in_specs=[ANY],
        out_specs=ANY,
        scratch_shapes=[DMA((3,)), DMA((3,)), DMA],
        compiler_params=params(cid),
        name=name,
    )(x)


class Line:
    def __init__(self, me, acc, up, down, sems):
        self.me, self.acc, self.up, self.down = me, acc, up, down
        self.us, self.ur, self.ds, self.dr = (sems.at[i] for i in range(4))

    def send(self, q, d):
        if d == 0:
            return push(self.acc(q), self.up.at[q], self.us.at[q], self.ur.at[q], self.me.z(1))
        return push(self.acc(q), self.down.at[q], self.ds.at[q], self.dr.at[q], self.me.z(3))

    def go(self, q, d):
        j, ref = self.me.j, self.acc(q)
        here = (j < q) if d == 0 else (j > q)
        inner = (j > 0) if d == 0 else (j < 3)
        got = self.up if d == 0 else self.down

        @pl.when(here & inner)
        def _():
            self.send(q, d).wait_recv()
            ref[...] = ref[...] + got[q]

        @pl.when(here)
        def _():
            self.send(q, d).start()

    def first(self):
        j = self.me.j

        @pl.when(j == 0)
        def _():
            for q in (3, 2, 1):
                self.send(q, 0).start()

        @pl.when(j == 3)
        def _():
            for q in (0, 1, 2):
                self.send(q, 1).start()

    def inner(self, steps):
        j = self.me.j
        for q, d in steps:
            got = self.up if d == 0 else self.down
            cond = ((j < q) & (j > 0)) if d == 0 else ((j > q) & (j < 3))

            @pl.when(cond)
            def _():
                c = self.send(q, d)
                c.wait_recv()
                ref = self.acc(q)
                ref[...] = ref[...] + got[q]
                c.start()

    def finish(self, out):
        j = self.me.j
        for q in range(4):

            @pl.when(j == q)
            def _():
                total = self.acc(q)[...].astype(F32)
                if q > 0:
                    self.send(q, 0).wait_recv()
                    total = total + self.up[q].astype(F32)
                if q < 3:
                    self.send(q, 1).wait_recv()
                    total = total + self.down[q].astype(F32)
                out[...] = total

            @pl.when(j < q)
            def _():
                self.send(q, 0).wait_send()

            @pl.when(j > q)
            def _():
                self.send(q, 1).wait_send()


OUTER = ((3, 0), (0, 1))
MIDDLE = ((2, 0), (1, 1))


class Unit:
    def __init__(self, me, src, acc, rc, rx, ry, rx2, ry2, sems, lsem):
        self.me, self.src, self.acc = me, src, acc
        self.rc, self.rx, self.ry, self.rx2, self.ry2 = rc, rx, ry, rx2, ry2
        self.s, self.r, self.lsem = sems.at[0], sems.at[1], lsem
        self.nq = acc.shape[0]

    def copies(self, stage):
        me, acc, s, r = self.me, self.acc, self.s, self.r
        lo, hi = pl.ds(0, 48), pl.ds(48, 48)
        if stage == 0:
            return [push(self.src.at[:, :, 1 - me.core], self.rc, s.at[0], r.at[0], me.at(me.pc))]
        if stage == 1:
            return [
                push(acc.at[:, me.md, lo], self.rx.at[:, 1], s.at[1], r.at[1], me.at(me.px)),
                push(acc.at[:, me.md, hi], self.ry.at[:, 1], s.at[2], r.at[2], me.at(me.py)),
                push(acc.at[:, me.mx, lo], self.rx.at[:, 0], s.at[3], r.at[3], me.at(me.px)),
                push(acc.at[:, me.my, hi], self.ry.at[:, 0], s.at[4], r.at[4], me.at(me.py)),
            ]
        return [
            push(acc.at[:, me.my, lo], self.ry2, s.at[5], r.at[5], me.at(me.py)),
            push(acc.at[:, me.mx, hi], self.rx2, s.at[6], r.at[6], me.at(me.px)),
        ]

    def load(self):
        return pltpu.make_async_copy(self.src.at[:, :, self.me.core], self.acc, self.lsem)

    def begin(self):
        self.copies(0)[0].start()
        self.load().start()

    def chip(self):
        self.load().wait()
        self.copies(0)[0].wait_recv()

        @pl.loop(0, self.nq)
        def _(q):
            for m in range(4):
                self.acc[q, m] = self.acc[q, m] + self.rc[q, m]

    def cross(self):
        for c in self.copies(1):
            c.start()

    def turn(self):
        me = self.me
        for c in self.copies(1):
            c.wait()

        @pl.loop(0, self.nq)
        def _(q):
            self.acc[q, me.my, 0:48] = self.acc[q, me.my, 0:48] + self.rx[q, 1]
            self.acc[q, me.mx, 48:96] = self.acc[q, me.mx, 48:96] + self.ry[q, 1]

        for c in self.copies(2):
            c.start()

        @pl.loop(0, self.nq)
        def _(q):
            self.acc[q, me.m, 0:48] = self.acc[q, me.m, 0:48] + self.rx[q, 0]
            self.acc[q, me.m, 48:96] = self.acc[q, me.m, 48:96] + self.ry[q, 0]

    def settle(self):
        me = self.me
        for c in self.copies(2):
            c.wait()

        @pl.loop(0, self.nq)
        def _(q):
            self.acc[q, me.m, 0:48] = self.acc[q, me.m, 0:48] + self.ry2[q]
            self.acc[q, me.m, 48:96] = self.acc[q, me.m, 48:96] + self.rx2[q]

        self.copies(0)[0].wait_send()

    def own(self, q):
        return self.acc.at[q, self.me.m]


def reduce_kernel(gn, dw, dwo, dqkv, o_gn, o_up, o_down, o_out, o_qkv, *scratch):
    me = Place()
    meet([me.z(1), me.z(2), me.z(3), me.at(me.px), me.at(me.py), me.at(me.pc)])
    it = iter(scratch)
    take = lambda n: [next(it) for _ in range(n)]
    gacc, gup, gdown, gsem, gl = take(5)
    sources = (dw.at[1], dw.at[0], dwo, dqkv)
    units, lines = [], []
    for i, src in enumerate(sources):
        acc, rc, rx, ry, rx2, ry2, sems, lsem = take(8)
        unit = Unit(me, src, acc, rc, rx, ry, rx2, ry2, sems, lsem)
        units.append(unit)
        if i < 3:
            up, down, sem = take(3)
            lines.append(Line(me, unit.own, up, down, sem))
    own = Line(me, lambda q: gacc.at[q], gup, gdown, gsem)
    load = pltpu.make_async_copy(gn, gacc, gl)
    load.start()
    for u in units:
        u.begin()
    load.wait()
    own.first()
    units[0].chip()
    units[0].cross()
    for u in units[1:]:
        u.chip()
    own.inner(OUTER)
    units[0].turn()
    units[1].cross()
    own.inner(MIDDLE)
    units[0].settle()
    lines[0].first()
    units[1].turn()
    units[2].cross()
    units[3].cross()
    own.inner(((3, 0), (0, 1))[:0])
    lines[0].inner(OUTER)
    units[1].settle()
    lines[1].first()
    units[2].turn()
    units[3].turn()
    lines[0].inner(MIDDLE)
    own.finish(o_gn)
    units[2].settle()
    lines[2].first()
    lines[1].inner(OUTER)
    units[3].settle()
    lines[2].inner(OUTER)
    lines[1].inner(MIDDLE)
    lines[2].inner(MIDDLE)
    lines[0].finish(o_down)
    lines[1].finish(o_up)
    lines[2].finish(o_out)
    o_qkv[...] = units[3].acc[0, me.m].astype(F32)


def reduce_all(gn, dw, dwo, dqkv):
    scratch = [
        pltpu.VMEM((4, 256, 768), BF),
        pltpu.VMEM((4, 256, 768), BF),
        pltpu.VMEM((4, 256, 768), BF),
        DMA((4, 4)),
        DMA,
    ]
    for i, (nq, w) in enumerate(((4, 768), (4, 768), (4, 256), (1, 640))):
        scratch += [
            pltpu.VMEM((nq, 4, 96, w), BF),
            pltpu.VMEM((nq, 4, 96, w), BF),
            pltpu.VMEM((nq, 2, 48, w), BF),
            pltpu.VMEM((nq, 2, 48, w), BF),
            pltpu.VMEM((nq, 48, w), BF),
            pltpu.VMEM((nq, 48, w), BF),
            DMA((2, 7)),
            DMA,
        ]
        if i < 3:
            scratch += [pltpu.VMEM((4, 96, w), BF), pltpu.VMEM((4, 96, w), BF), DMA((4, 4))]
    vm = pl.BlockSpec(memory_space=pltpu.VMEM)
    return pl.pallas_call(
        reduce_kernel,
        out_shape=(
            jax.ShapeDtypeStruct((256, 768), F32),
            jax.ShapeDtypeStruct((96, 768), F32),
            jax.ShapeDtypeStruct((96, 768), F32),
            jax.ShapeDtypeStruct((96, 256), F32),
            jax.ShapeDtypeStruct((96, 640), F32),
        ),
        in_specs=[ANY] * 4,
        out_specs=(vm,) * 5,
        scratch_shapes=scratch,
        compiler_params=params(3),
        name="reduce_all",
    )(gn, dw, dwo, dqkv)


def final_kernel(tp, vec, X, SP, SZ, vs, zs, zr, vzs, vzr, ps, pr, vps, vpr, ls):
    me = Place()
    p, j = me.p, me.j
    meet([me.z(1), me.z(2), me.z(3)] + [me.at((p + k) % 8) for k in range(1, 8)])
    small = [push(vec, SZ.at[j], vzs.at[k - 1], vzr.at[k - 1], me.z(k)) for k in (1, 2, 3)]
    big = [push(tp.at[(j + k) % 4], X.at[p, j], zs.at[k - 1], zr.at[k - 1], me.z(k)) for k in (1, 2, 3)]
    mine = pltpu.make_async_copy(tp.at[j], X.at[p, j], ls.at[0])
    mine_v = pltpu.make_async_copy(vec, SZ.at[j], ls.at[1])
    for c in small + big + [mine, mine_v]:
        c.start()
    for c in small + [mine_v]:
        c.wait()
    vs[...] = SZ[0] + SZ[1] + SZ[2] + SZ[3]
    out_v = [push(vs, SP.at[p], vps.at[k - 1], vpr.at[k - 1], me.at((p + k) % 8)) for k in range(1, 8)]
    own_v = pltpu.make_async_copy(vs, SP.at[p], ls.at[2])
    for c in out_v + [own_v]:
        c.start()
    for c in big + [mine]:
        c.wait()
    lo, hi = pl.ds(0, 2), pl.ds(2, 2)

    def to(ref, i, dp):
        return push(ref, ref, ps.at[i], pr.at[i], me.at(dp))

    first = [to(X.at[p], 0, me.px), to(X.at[p], 1, me.py), to(X.at[p], 2, me.pc)]
    for c in first:
        c.start()
    here = me.pc - p
    to(X.at[me.px], 0, me.px).wait_recv()
    to(X.at[me.py], 1, me.py).wait_recv()
    second = [
        to(X.at[me.py, lo], 3, me.px),
        to(X.at[me.px, hi], 4, me.py),
        to(X.at[me.px], 5, me.pc),
        to(X.at[me.py], 6, me.pc),
    ]
    for c in second:
        c.start()
    to(X.at[me.pd, lo], 3, me.px).wait_recv()
    to(X.at[me.pd, hi], 4, me.px).wait_recv()
    third = to(X.at[me.pd], 7, me.pc)
    third.start()
    to(X.at[me.pc], 2, me.pc).wait_recv()
    to(X.at[me.px + here], 5, me.pc).wait_recv()
    to(X.at[me.py + here], 6, me.pc).wait_recv()
    to(X.at[me.pd + here], 7, me.pc).wait_recv()
    for c in first + second + [third]:
        c.wait_send()
    for c in out_v + [own_v]:
        c.wait()


def final_exchange(tp, vec):
    return pl.pallas_call(
        final_kernel,
        out_shape=(
            jax.ShapeDtypeStruct((8,) + tp.shape, BF),
            jax.ShapeDtypeStruct((8, 8, D), F32),
        ),
        in_specs=[ANY] * 2,
        out_specs=(ANY,) * 2,
        scratch_shapes=[
            pltpu.VMEM((4, 8, D), F32),
            pltpu.VMEM((8, D), F32),
            DMA((3,)),
            DMA((3,)),
            DMA((3,)),
            DMA((3,)),
            DMA((8,)),
            DMA((8,)),
            DMA((7,)),
            DMA((7,)),
            DMA((3,)),
        ],
        compiler_params=params(4),
        name="final_exchange",
    )(tp, vec)


class Native:
    def __init__(self, ndp, nmp):
        self.ndp, self.nmp = ndp, nmp

    def gather_all(self, emb, trow, ids, w2, wo):
        over_mp = lambda a: lax.all_gather(a, "mp", axis=0, tiled=False)
        return (
            over_mp(emb),
            over_mp(trow),
            lax.all_gather(ids, "dp", axis=0, tiled=False),
            over_mp(w2),
            over_mp(wo),
        )

    def exchange(self, x, cid, name):
        return lax.all_to_all(x, "mp", split_axis=0, concat_axis=0, tiled=True)

    def reduce_all(self, gn, dw, dwo, dqkv):
        sum_mp = lambda a: lax.psum_scatter(a.astype(F32), "mp", scatter_dimension=0, tiled=True)
        sum_dp = lambda a: lax.psum_scatter(a, "dp", scatter_dimension=0, tiled=True)
        flat = lambda a: a.reshape(D, a.shape[-1])
        return (
            sum_mp(gn).reshape(gn.shape[1:]),
            sum_dp(flat(sum_mp(dw[0]))),
            sum_dp(flat(sum_mp(dw[1]))),
            sum_dp(flat(sum_mp(dwo[..., : D // self.nmp]))),
            sum_dp(flat(dqkv[..., : 3 * D // self.nmp].astype(F32))),
        )

    def final_exchange(self, tp, vec):
        x = lax.all_to_all(tp, "mp", split_axis=0, concat_axis=0, tiled=True)
        return (
            lax.all_gather(x, "dp", axis=0, tiled=False),
            lax.all_gather(lax.psum(vec, "mp"), "dp", axis=0, tiled=False),
        )


class Tuned:
    gather_all = staticmethod(gather_all)
    exchange = staticmethod(exchange)
    reduce_all = staticmethod(reduce_all)
    final_exchange = staticmethod(final_exchange)


def layer_norm(stream, gain, shift):
    average = jnp.mean(stream, axis=-1, keepdims=True)
    centered = stream - average
    variance = jnp.mean(centered * centered, axis=-1, keepdims=True)
    return centered * lax.rsqrt(variance + 1e-05) * gain + shift


def allowed_pairs(seg_query, segments, first_row):
    key_pos = jnp.arange(L)
    query_pos = first_row + jnp.arange(QBLK)
    same_text = seg_query[:, None] == segments[None, :]
    self_or_text = (seg_query[:, None] != 0) | (query_pos[:, None] == key_pos[None, :])
    return same_text & self_or_text


def attend_forward(queries, key_rows, value_rows, segments):
    outputs = []
    log_parts = []
    for block_index in range(L // QBLK):
        first_row = block_index * QBLK
        query_block = queries[first_row : first_row + QBLK]
        allowed = allowed_pairs(segments[first_row : first_row + QBLK], segments, first_row)
        scores = jnp.einsum("qhd,khd->hqk", query_block, key_rows, preferred_element_type=F32) * 0.125
        masked = jnp.where(allowed[None], scores, -1e30)
        highest = jnp.max(masked, axis=-1, keepdims=True)
        exponents = jnp.exp(masked - highest)
        totals = jnp.sum(exponents, axis=-1, keepdims=True)
        weights = (exponents / totals).astype(BF)
        outputs.append(jnp.einsum("hqk,khd->qhd", weights, value_rows, preferred_element_type=F32).astype(BF))
        log_parts.append((highest + jnp.log(totals))[..., 0])
    return (jnp.concatenate(outputs, axis=0), jnp.concatenate(log_parts, axis=1))


def attend_backward(queries, key_rows, value_rows, segments, log_sums, grad_heads):
    grad_keys = jnp.zeros(key_rows.shape, F32)
    grad_values = jnp.zeros(value_rows.shape, F32)
    grad_queries = []
    for block_index in range(L // QBLK):
        first_row = block_index * QBLK
        query_block = queries[first_row : first_row + QBLK]
        grad_block = grad_heads[first_row : first_row + QBLK]
        allowed = allowed_pairs(segments[first_row : first_row + QBLK], segments, first_row)
        scores = jnp.einsum("qhd,khd->hqk", query_block, key_rows, preferred_element_type=F32) * 0.125
        masked = jnp.where(allowed[None], scores, -1e30)
        probs = jnp.exp(masked - log_sums[:, first_row : first_row + QBLK, None])
        rounded = probs.astype(BF)
        grad_probs = jnp.einsum("qhd,khd->hqk", grad_block, value_rows, preferred_element_type=F32)
        inner = jnp.sum(probs * grad_probs, axis=-1, keepdims=True)
        grad_scores = (probs * (grad_probs - inner)).astype(BF)
        grad_queries.append(
            jnp.einsum("hqk,khd->qhd", grad_scores, key_rows, preferred_element_type=F32) * 0.125
        )
        grad_keys = (
            grad_keys
            + jnp.einsum("hqk,qhd->khd", grad_scores, query_block, preferred_element_type=F32) * 0.125
        )
        grad_values = grad_values + jnp.einsum("hqk,qhd->khd", rounded, grad_block, preferred_element_type=F32)
    return (
        jnp.concatenate(grad_queries, axis=0).astype(BF),
        grad_keys.astype(BF),
        grad_values.astype(BF),
    )


def dot(a, b):
    return jnp.dot(a, b, preferred_element_type=F32)


def contract_rows(left, right):
    return lax.dot_general(left, right, (((0,), (0,)), ((), ())), preferred_element_type=F32)


def contract_cols(left, right):
    return lax.dot_general(left, right, (((1,), (1,)), ((), ())), preferred_element_type=F32)


def fold(rows):
    half = rows.shape[-2] // 2
    return jnp.concatenate((rows[..., :half, :], rows[..., half:, :]), axis=-1)


def unfold(packed):
    width = packed.shape[-1] // 2
    return jnp.concatenate((packed[..., :width], packed[..., width:]), axis=-2)


def on_device(
    comm,
    token_ids,
    segment_ids,
    timesteps,
    token_table,
    time_table,
    ln1_gain,
    ln1_bias,
    w_qkv,
    w_out,
    attn_bias,
    ln2_gain,
    ln2_bias,
    w_up,
    w_down,
    mlp_bias,
    cotangent,
):
    group = lax.axis_size("mp")
    ndp = lax.axis_size("dp")
    member = lax.axis_index("mp")
    own_rows = L // group
    width = token_table.shape[1]
    heads_local = width // HD

    emb = fold(token_table[token_ids])
    time_row = lax.dynamic_slice_in_dim(time_table, timesteps[0], 1, 0)
    trow = jnp.broadcast_to(jnp.pad(time_row, ((0, 0), (0, 256 - width))), (16, 256))
    ids = token_ids.reshape(8, 128)
    w2 = jnp.stack((w_up, w_down))
    wo = w_out.reshape(width, 6, 128).transpose(1, 0, 2).reshape(6 * width, 128)
    E, TR, IDS, W2, WO = comm.gather_all(emb, trow, ids, w2, wo)

    time_full = TR[:, 0, :width].reshape(1, D).astype(F32)
    tokens = unfold(E).transpose(1, 0, 2).reshape(L, D)
    stream_all = tokens.astype(F32) + time_full
    stream_in = lax.dynamic_slice_in_dim(stream_all, member * own_rows, own_rows, 0)
    normed_one = layer_norm(stream_all, ln1_gain, ln1_bias).astype(BF)
    wq = w_qkv.transpose(1, 2, 0).reshape(3 * width, D)
    packed = contract_cols(normed_one, wq).astype(BF).reshape(L, 3, heads_local, HD)
    queries, key_rows, value_rows = packed[:, 0], packed[:, 1], packed[:, 2]
    attended, log_sums = attend_forward(queries, key_rows, value_rows, segment_ids)
    sent = fold(attended.reshape(group, own_rows, width))
    got = comm.exchange(sent, 1, "to_rows")

    att_own = unfold(got).transpose(1, 0, 2).reshape(own_rows, D)
    w_out_full = WO.reshape(group, 6, width, 128).transpose(0, 2, 1, 3).reshape(D, D)
    stream_mid = stream_in + dot(att_own, w_out_full) + attn_bias
    normed_two = layer_norm(stream_mid, ln2_gain, ln2_bias).astype(BF)
    own_segments = lax.dynamic_slice_in_dim(segment_ids, member * own_rows, own_rows, 0)
    grad_out = cotangent.astype(F32) * (own_segments != 0).astype(F32)[:, None]
    grad_mlp = grad_out.astype(BF)
    out = stream_mid + mlp_bias
    grad_norm_two = jnp.zeros((own_rows, D), F32)
    grads_up, grads_down = [], []
    for q in range(group):
        pre = dot(normed_two, W2[q, 0])
        act, back = jax.vjp(lambda v: jax.nn.gelu(v, approximate=True), pre)
        act = act.astype(BF)
        out = out + dot(act, W2[q, 1])
        grad_pre = back(contract_cols(grad_mlp, W2[q, 1]))[0].astype(BF)
        grad_norm_two = grad_norm_two + contract_cols(grad_pre, W2[q, 0])
        grads_up.append(contract_rows(normed_two, grad_pre).astype(BF))
        grads_down.append(contract_rows(grad_mlp, act).astype(BF))
    dw = jnp.stack((jnp.stack(grads_up), jnp.stack(grads_down)))
    norm_back_two = jax.vjp(layer_norm, stream_mid, ln2_gain, ln2_bias)[1]
    grad_mid_norm, grad_ln2_gain, grad_ln2_bias = norm_back_two(grad_norm_two)
    grad_mid = grad_out + grad_mid_norm
    grad_attn = grad_mid.astype(BF)
    dwo = contract_rows(grad_attn, att_own).astype(BF).reshape(D, group, width).transpose(1, 0, 2)
    dwo = jnp.pad(dwo, ((0, 0), (0, 0), (0, 256 - width)))
    grad_attended = contract_cols(grad_attn, w_out_full).astype(BF)
    sent = fold(grad_attended.reshape(own_rows, group, width).transpose(1, 0, 2))
    got = comm.exchange(sent, 2, "to_heads")

    grad_heads = unfold(got).reshape(L, heads_local, HD)
    grad_q, grad_k, grad_v = attend_backward(
        queries, key_rows, value_rows, segment_ids, log_sums, grad_heads
    )
    grad_packed = jnp.stack((grad_q, grad_k, grad_v), axis=1).reshape(L, 3 * width)
    dqkv = jnp.pad(contract_rows(normed_one, grad_packed).astype(BF), ((0, 0), (0, 640 - 3 * width)))
    gn = dot(grad_packed, wq).astype(BF).reshape(group, own_rows, D)

    pieces = lambda a: a.reshape(a.shape[:-2] + (ndp // 2, 2, D // ndp, a.shape[-1]))
    grad_norm_one, g_up, g_down, g_out, g_qkv = comm.reduce_all(
        gn, pieces(dw), pieces(dwo), pieces(dqkv)[None]
    )
    norm_back_one = jax.vjp(layer_norm, stream_in, ln1_gain, ln1_bias)[1]
    grad_in_norm, grad_ln1_gain, grad_ln1_bias = norm_back_one(grad_norm_one)
    input_grad = grad_mid + grad_in_norm
    tp = fold(input_grad.astype(BF).reshape(own_rows, group, width).transpose(1, 0, 2))
    step_row = jnp.where(member == 0, timesteps[0], 0).astype(F32)
    vec = jnp.stack(
        (
            grad_ln1_gain,
            grad_ln1_bias,
            jnp.sum(grad_mid, axis=0),
            grad_ln2_gain,
            grad_ln2_bias,
            jnp.sum(grad_out, axis=0),
            jnp.sum(input_grad, axis=0),
            jnp.broadcast_to(step_row, (D,)),
        )
    )
    X, SP = comm.final_exchange(tp, vec)
    rows_table = token_table.shape[0] // ndp
    columns = unfold(X).reshape(ndp * L, width)
    first = lax.axis_index("dp") * rows_table
    hot = (first + jnp.arange(rows_table))[:, None] == IDS.reshape(1, ndp * L)
    grad_token_table = dot(hot.astype(BF), columns)
    steps = SP[:, 7, 0].astype(jnp.int32)
    grad_time_table = jnp.zeros(time_table.shape[:1] + (D,), F32)
    at_row = jnp.arange(time_table.shape[0])[:, None]
    if ndp <= 8:
        for i in range(ndp):
            grad_time_table = grad_time_table + jnp.where(at_row == steps[i], SP[i, 6][None], 0.0)
    else:
        grad_time_table = grad_time_table.at[steps].add(SP[:, 6])
    sums = jnp.sum(SP[:, :6], axis=0)
    return (
        out.astype(BF),
        input_grad,
        grad_token_table,
        grad_time_table,
        sums[0],
        sums[1],
        g_qkv[:, : 3 * width].reshape(-1, 3, width),
        g_out[:, :width].T,
        sums[2],
        sums[3],
        sums[4],
        g_up,
        g_down.T,
        sums[5],
    )


def solution(mesh):
    placed = (
        P("dp"),
        P("dp"),
        P("dp"),
        P(None, "mp"),
        P(None, "mp"),
        P(),
        P(),
        P(None, None, "mp"),
        P("mp", None),
        P(),
        P(),
        P(),
        P(None, "mp"),
        P("mp", None),
        P(),
        P(("dp", "mp"), None),
    )
    ndp, nmp = mesh.shape["dp"], mesh.shape["mp"]
    comm = Tuned if (ndp, nmp) == (8, 4) else Native(ndp, nmp)
    return jax.shard_map(
        functools.partial(on_device, comm),
        mesh=mesh,
        in_specs=placed,
        out_specs=(
            P(("dp", "mp"), None),
            P(("dp", "mp"), None),
            P("dp", "mp"),
            P(),
            P(),
            P(),
            P("dp", None, "mp"),
            P("mp", "dp"),
            P(),
            P(),
            P(),
            P("dp", "mp"),
            P("mp", "dp"),
            P(),
        ),
        check_vma=False,
    )
```

time: 1000 us -> 433 us (0.43)
  waiting for transfers between devices: 725 us -> 0 us
  Pallas kernels: 0 us -> 244 us
  blocking collectives: 91.6 us -> 0 us
  local copies, waits for them, and re-layouts: 28.3 us -> 65 us
  matrix products: 89.9 us -> 68.9 us
  between operations: 15.6 us -> 2.85 us
    reduce_scatter x9 -> x0, waiting for transfers between devices: 389 us -> none  [the longest x2 117 us: block_forward(): lax.psum_scatter(jnp.dot(lax.slice_in_dim(attended_flat, 0, own_rows * la...]
    pallas_call x0 -> x5, Pallas kernels: none -> 244 us  [the longest x1 101 us: gather_all(): pl.pallas_call(gather_kernel, out_shape=(jax.ShapeDtypeStruct((4,) + emb....]
    all_gather x6 -> x0, waiting for transfers between devices: 178 us -> none  [the longest x2 69.5 us: block_forward(): gathered_one = lax.all_gather(normed_one, 'mp', axis=0, tiled=True)]
    psum x1 -> x0, waiting for transfers between devices: 143 us -> none  [on_device(): lax.psum((grad_time_table, grad_ln1_gain, grad_ln1_bias, grad_attn_bias,...]
    all_to_all x2 -> x0, blocking collectives: 51.2 us -> none  [the longest x1 26.2 us: on_device(): lax.all_to_all(embedded.reshape(tokens_all, local_width), 'mp', split_axi...]
    psum x1 -> x0, blocking collectives: 40.3 us -> none  [on_device(): lax.psum((grad_time_table, grad_ln1_gain, grad_ln1_bias, grad_attn_bias,...]
    unnamed x18 -> x0, waiting for transfers between devices: 14.7 us -> none
    sub x2 -> x0, matrix products: 12.1 us -> none  [attend_forward(): exponents = jnp.exp(masked - highest)]
  transfers between devices with their start and end apart: 17 -> 0, of which waited for: 17 -> 0; matrix products, arithmetic and copies ran while one was open for 6% -> 0% of each run, Pallas kernels for 0% -> 0%
where the time goes in v1:
time: 433 us; the launch traced here: 425 us
  Pallas kernels  244 us (56%)
  matrix products  68.9 us (16%)
  local copies, waits for them, and re-layouts  65 us (15%)
  other arithmetic  45 us (10%)
    pallas_call x1, Pallas kernels, gather_all(): pl.pallas_call(gather_kernel, out_shape=(jax.ShapeDtypeStruct((4,) + emb....  101 us
    pallas_call x1, Pallas kernels, reduce_all(): pl.pallas_call(reduce_kernel, out_shape=(jax.ShapeDtypeStruct((256, 768),...  89.6 us
    pallas_call x1, Pallas kernels, final_exchange(): pl.pallas_call(final_kernel, out_shape=(jax.ShapeDtypeStruct((8,) + tp.sh...  30.2 us
    dot_general x11, matrix products, dot(): return jnp.dot(a, b, preferred_element_type=F32)  27 us
    pallas_call x2, Pallas kernels, exchange(): pl.pallas_call(exchange_kernel, out_shape=jax.ShapeDtypeStruct(x.shape, x...  22.7 us
    unnamed x130, local copies, waits for them, and re-layouts  17.1 us
    dot_general x2, matrix products, attend_backward(): jnp.einsum('hqk,qhd->khd', rounded, grad_block, preferred_element_type=F32)  9.07 us
    dot_general x10, matrix products, contract_cols(): lax.dot_general(left, right, (((1,), (1,)), ((), ())), preferred_element_...  9.01 us

profile of v1, /device:TPU:0, one launch (start us, length us, event | category | flops | bytes accessed | tf_op | source)
XLA Modules:
  0.0 425.4 jit_solution(13266219850653073775)
XLA Ops:
  0.7 6.0 %copy.42 = bf16[8192,192]{1,0:T(8,128)(2,1)} copy(bf16[8192,192]{0,1:T(8,128)(2,1)} %param.19) | data formatting | bytes 6291456 | tf_op args[3]
  6.7 6.3 %gather_fusion = bf16[1024,192]{1,0:T(8,128)(2,1)S(1)} fusion(bf16[8192,192]{1,0:T(8,128)(2,1)} %copy.42, s32[1024]{0:T(1024)S(1)} %fusion.140), kind=kCustom, calls=%fused_computation | custom fusion | bytes 790528 | tf_op jit(solution)/shard_map/gather | solution.py:762
  16.2 2.9 pad_maximum_fusion.1.w2
  20.2 101.1 %gather_all.1 = (bf16[4,512,384]{2,1,0:T(8,128)(2,1)}, bf16[4,16,256]{2,1,0:T(8,128)(2,1)}, s32[8,8,128]{2,1,0:T(8,128)}, bf16[4,2,768,768]{3,2,1,0:T(8,128)(2,1)}, bf16[4,1152,128]{2,1,0:T(8,128)(2,1)}) custom-call(bf16[512,384]{1,0:T(8,128)(2,1)} %pad_maximum_fusion.4.emb, bf16[16,256]{1,0:T(8,128)(2,1)} %broadcast_in_dim.212.trow, s32[8,128]{1,0:T(8,128)} %bitcast.267, ...), custom_call_target="tpu_custom_call" | custom-call | tf_op jit(solution)/shard_map/gather_all/pallas_call | solution.py:220
  122.2 2.0 fusion.157
  125.8 3.0 fusion.24
  128.8 3.9 copy.46
  132.7 2.5 convolution_convert_fusion.2
  135.2 1.9 fusion.26
  137.1 1.4 fusion.166
  138.6 1.5 fusion.5
  141.3 1.5 fusion.75
  142.7 1.4 fusion.167
  144.2 1.5 fusion.4
  146.8 1.5 fusion.74
  154.3 10.7 %to_rows.1 = bf16[4,128,384]{2,1,0:T(8,128)(2,1)} custom-call(bf16[4,128,384]{2,1,0:T(8,128)(2,1)} %pad_maximum_fusion.6.x), custom_call_target="tpu_custom_call" | custom-call | tf_op jit(solution)/shard_map/to_rows/pallas_call | solution.py:263
  167.3 3.2 copy.50
  170.5 2.4 convert_bitcast_fusion
  172.9 5.4 %copy.44 = f32[1024,4,192]{0,2,1:T(8,128)} copy(f32[1024,4,192]{2,0,1:T(8,128)} %convert_bitcast_fusion) | data formatting | bytes 6291456 | tf_op jit(solution)/shard_map/convert_element_type | solution.py:772
  180.7 2.2 fusion.168
  183.4 1.9 fusion.68
  185.3 2.2 convolution_add_fusion.7
  187.5 1.8 fusion.61
  189.3 2.2 convolution_add_fusion.6
  191.5 1.7 fusion.55
  194.5 1.4 fusion.34
  206.5 12.0 %to_heads.1 = bf16[4,128,384]{2,1,0:T(8,128)(2,1)} custom-call(bf16[4,128,384]{2,1,0:T(8,128)(2,1)} %pad_maximum_fusion.7.x), custom_call_target="tpu_custom_call" | custom-call | tf_op jit(solution)/shard_map/to_heads/pallas_call | solution.py:263
  221.8 4.8 %fusion.16 = f32[3,64,1024]{2,1,0:T(8,128)} fusion(bf16[512,3,64]{0,2,1:T(8,128)(2,1)S(1)} %slice.244, f32[3,512,1024]{2,1,0:T(8,128)} %copy-done.1, f32[3,512]{1,0:T(4,128)S(1)} %log_add_fusion), kind=kOutput, calls=%fused_computation.33 | convolution fusion | flops 204472320 | bytes 7280640 | tf_op jit(solution)/shard_map/hqk,qhd->khd/dot_general | solution.py:706
  226.9 4.3 %fusion.39 = bf16[1024,1,3,64]{0,3,2,1:T(8,128)(2,1)S(1)} fusion(f32[3,64,1024]{2,1,0:T(8,128)} %fusion.16, bf16[512,3,64]{0,2,1:T(8,128)(2,1)S(1)} %slice.242, f32[3,512,1024]{2,1,0:T(8,128)} %copy-done.2, f32[3,512]{1,0:T(4,128)S(1)} %log_add_fusion.1), kind=kOutput, calls=%fused_computation.77 | convolution fusion | flops 204865536 | bytes 7673856 | tf_op jit(solution)/shard_map/hqk,qhd->khd/dot_general | solution.py:706
  231.2 3.9 multiply_reduce_fusion.1
  235.2 1.4 multiply_convert_fusion.1
  237.3 1.9 multiply_reduce_fusion
  239.2 1.8 multiply_convert_fusion
  244.0 2.6 convolution_convert_fusion
  252.2 4.7 %maximum_maximum_fusion.dw = bf16[2,4,4,2,96,768]{5,4,3,2,1,0:T(8,128)(2,1)} fusion(bf16[1,1,4,2,96,768]{5,4,3,2,1,0:T(8,128)(2,1)S(1)} %bitcast.251, bf16[1,1,4,2,96,768]{5,4,3,2,1,0:T(8,128)(2,1)S(1)} %bitcast.252, bf16[1,1,4,2,96,768]{5,4,3,2,1,0:T(8,128)(2,1)S(1)} %bitcast.253, bf16[1,1,4,2,96,768]{5,4,3,2,1,0:T(8,128)(2,1)S(1)} %bitcast.254, ...), kind=kLoop, calls=%fused_computation.5 | loop fusion | flops 33030144 | bytes 18874368 | tf_op jit(solution)/shard_map/stack | solution.py:801
  256.9 1.6 convolution_convert_fusion.1
  258.5 2.5 copy.55
  261.0 3.0 pad.13
  264.0 2.1 convolution_convert_fusion.11
  266.1 2.2 copy.65
  268.3 2.2 pad.14.clone
  270.6 89.6 %reduce_all.1 = (f32[256,768]{1,0:T(8,128)}, f32[96,768]{1,0:T(8,128)}, f32[96,768]{1,0:T(8,128)}, f32[96,256]{1,0:T(8,128)}, f32[96,640]{1,0:T(8,128)}) custom-call(bf16[4,256,768]{2,1,0:T(8,128)(2,1)} %bitcast.243, bf16[2,4,4,2,96,768]{5,4,3,2,1,0:T(8,128)(2,1)} %maximum_maximum_fusion.dw, bf16[4,4,2,96,256]{4,3,2,1,0:T(8,128)(2,1)} %bitcast.219, ...), custom_call_target="tpu_custom_call" | custom-call | tf_op jit(solution)/shard_map/reduce_all/pallas_call | solution.py:510
  360.6 1.5 multiply_reduce_fusion.3
  365.0 30.2 %final_exchange.1 = (bf16[8,4,128,384]{3,2,1,0:T(8,128)(2,1)}, f32[8,8,768]{2,1,0:T(8,128)}) custom-call(bf16[4,128,384]{2,1,0:T(8,128)(2,1)} %pad_maximum_fusion.8.tp, f32[8,768]{1,0:T(8,128)} %stack.90.vec), custom_call_target="tpu_custom_call" | custom-call | tf_op jit(solution)/shard_map/final_exchange/pallas_call | solution.py:580
  395.2 3.5 fusion.156
  398.7 2.9 pad_maximum_fusion
  401.6 9.9 %fusion = f32[1024,192]{0,1:T(8,128)} fusion(bf16[8192,192]{1,0:T(8,128)(2,1)} %bitcast.227, s32[8192]{0:T(1024)S(1)} %bitcast.268, s32[1024]{0:T(1024)S(1)} %iota_add_fusion), kind=kOutput, calls=%fused_computation.1 | convolution fusion | flops 3229614080 | bytes 3969024 | tf_op jit(solution)/shard_map/dot_general | solution.py:715
  417.5 3.9 select_add_fusion
  (240 shorter events, 56.5 us)
Async XLA Ops:
  0.6 120.7 %copy-start = (bf16[768,3,192]{0,2,1:T(8,128)(2,1)S(1)}, bf16[768,3,192]{0,2,1:T(8,128)(2,1)}, u32[]{:S(2)}) copy-start(bf16[768,3,192]{0,2,1:T(8,128)(2,1)} %param.23) | copy-start | bytes 2654212
  0.7 6.0 %copy-start.41 = (s32[1024]{0:T(1024)S(1)}, s32[1024]{0:T(1024)}, u32[]{:S(2)}) copy-start(s32[1024]{0:T(1024)} %param.16) | copy-start | bytes 12292
  6.7 9.5 %copy-start.21 = (bf16[768,768]{1,0:T(8,128)(2,1)S(1)}, bf16[768,768]{1,0:T(8,128)(2,1)}, u32[]{:S(2)}) copy-start(bf16[768,768]{1,0:T(8,128)(2,1)} %param.29) | copy-start | bytes 3538948
  13.0 6.1 %copy-start.34 = (bf16[192,768]{1,0:T(8,128)(2,1)S(1)}, bf16[192,768]{1,0:T(8,128)(2,1)}, u32[]{:S(2)}) copy-start(bf16[192,768]{1,0:T(8,128)(2,1)} %param.24) | copy-start | bytes 884740
  19.1 102.2 %copy-start.49 = (f32[768]{0:T(1024)S(1)}, f32[768]{0:T(1024)}, u32[]{:S(2)}) copy-start(f32[768]{0:T(1024)} %param.22) | copy-start | bytes 9220
  19.1 102.3 %copy-start.39 = (f32[768]{0:T(1024)S(1)}, f32[768]{0:T(1024)}, u32[]{:S(2)}) copy-start(f32[768]{0:T(1024)} %param.21) | copy-start | bytes 9220
  132.7 2.5 copy-start.38
  135.2 10.5 %copy-start.3 = (bf16[1024,576]{0,1:T(8,128)(2,1)}, bf16[1024,576]{0,1:T(8,128)(2,1)S(1)}, u32[]{:S(2)}) copy-start(bf16[1024,576]{0,1:T(8,128)(2,1)S(1)} %convolution_convert_fusion.2) | copy-start | bytes 3538948
  138.6 2.7 copy-start.1
  144.2 2.6 copy-start.2
  178.3 2.4 copy-start.8
  178.3 2.4 copy-start.51
  179.6 3.5 copy-start.40
  179.6 3.5 copy-start.46
  180.7 4.6 %copy-start.52 = (f32[768]{0:T(1024)S(1)}, f32[768]{0:T(1024)}, u32[]{:S(2)}) copy-start(f32[768]{0:T(1024)} %param.30) | copy-start | bytes 9220
  180.7 12.6 %slice-start.4 = ((s8[9437184]{0:T(1024)(128)(4,1)}), s8[4194304]{0:T(1024)(128)(4,1)S(1)}, s32[]{:S(2)}) async-start(s8[9437184]{0:T(1024)(128)(4,1)} %bitcast.217), calls=%async_computation.4 | async-start | bytes 8388608
  183.3 9.9 %slice-start.5 = ((s8[9437184]{0:T(1024)(128)(4,1)}), s8[4194304]{0:T(1024)(128)(4,1)S(1)}, s32[]{:S(2)}) async-start(s8[9437184]{0:T(1024)(128)(4,1)} %bitcast.217), calls=%async_computation.5 | async-start | bytes 8388608
  185.3 10.6 %copy-start.22 = (f32[256,768]{1,0:T(8,128)}, f32[256,768]{1,0:T(8,128)S(1)}, u32[]{:S(2)}) copy-start(f32[256,768]{1,0:T(8,128)S(1)} %fusion.68) | copy-start | bytes 2359300
  187.5 5.8 %slice-start.6 = ((s8[9437184]{0:T(1024)(128)(4,1)}), s8[1048576]{0:T(1024)(128)(4,1)S(1)}, s32[]{:S(2)}) async-start(s8[9437184]{0:T(1024)(128)(4,1)} %bitcast.217), calls=%async_computation.6 | async-start | bytes 2097152
  189.3 7.9 %copy-start.24 = (f32[256,768]{1,0:T(8,128)}, f32[256,768]{1,0:T(8,128)S(1)}, u32[]{:S(2)}) copy-start(f32[256,768]{1,0:T(8,128)S(1)} %fusion.61) | copy-start | bytes 2359300
  193.3 5.5 %copy-start.26 = (f32[256,768]{1,0:T(8,128)}, f32[256,768]{1,0:T(8,128)S(1)}, u32[]{:S(2)}) copy-start(f32[256,768]{1,0:T(8,128)S(1)} %fusion.55) | copy-start | bytes 2359300
  194.0 2.0 copy-start.11
  194.5 5.7 %copy-start.28 = (f32[256,768]{1,0:T(8,128)}, f32[256,768]{1,0:T(8,128)S(1)}, u32[]{:S(2)}) copy-start(f32[256,768]{1,0:T(8,128)S(1)} %fusion.49) | copy-start | bytes 2359300
  195.9 7.0 %copy-start.42 = (f32[256]{0:T(256)}, f32[256]{0:T(256)S(1)}, u32[]{:S(2)}) copy-start(f32[256]{0:T(256)S(1)} %compare_convert_fusion) | copy-start | bytes 3076
  226.9 4.3 %copy-start.4 = (bf16[1024,576]{0,1:T(8,128)(2,1)S(1)}, bf16[1024,576]{0,1:T(8,128)(2,1)}, u32[]{:S(2)}) copy-start(bf16[1024,576]{0,1:T(8,128)(2,1)} %copy-done.3) | copy-start | bytes 3538948
  226.9 8.2 %slice-start.2 = ((s8[6291456]{0:T(1024)(128)(4,1)}), s8[4194304]{0:T(1024)(128)(4,1)S(1)}, s32[]{:S(2)}) async-start(s8[6291456]{0:T(1024)(128)(4,1)} %bitcast.215), calls=%async_computation.2 | async-start | bytes 8388608
  231.2 4.0 slice-start.3
  231.2 6.1 %slice-start = ((s8[6291456]{0:T(1024)(128)(4,1)}), s8[4194304]{0:T(1024)(128)(4,1)S(1)}, s32[]{:S(2)}) async-start(s8[6291456]{0:T(1024)(128)(4,1)} %bitcast.213), calls=%async_computation | async-start | bytes 8388608
  235.2 2.1 slice-start.1
  244.0 2.6 copy-start.19
  244.0 2.6 copy-start.12
  244.0 2.6 copy-start.29
  244.0 2.6 copy-start.43
  246.6 1.9 copy-start.25
  249.3 1.8 copy-start.16
  252.2 4.8 %copy-start.9 = (bf16[256,4,192]{0,2,1:T(8,128)(2,1)S(1)}, bf16[256,4,192]{0,2,1:T(8,128)(2,1)}, u32[]{:S(2)}) copy-start(bf16[256,4,192]{0,2,1:T(8,128)(2,1)} %copy.49) | copy-start | bytes 1179652
  252.2 4.8 %copy-start.45 = (f32[256]{0:T(256)S(1)}, f32[256]{0:T(256)}, u32[]{:S(2)}) copy-start(f32[256]{0:T(256)} %copy-done.44) | copy-start | bytes 3076
  261.0 3.0 copy-start.7
  261.0 3.0 copy-start.20
  360.2 1.9 copy-start.6
  362.5 1.8 copy-start.47
  362.8 35.9 %copy-start.5 = (f32[256,768]{1,0:T(8,128)}, f32[256,768]{1,0:T(8,128)S(1)}, u32[]{:S(2)}) copy-start(f32[256,768]{1,0:T(8,128)S(1)} %get-tuple-element.155) | copy-start | bytes 2359300
  398.7 2.9 copy-start.50
  401.6 9.9 %copy-start.35 = (f32[8,8,768]{2,1,0:T(8,128)S(1)}, f32[8,8,768]{2,1,0:T(8,128)}, u32[]{:S(2)}) copy-start(f32[8,8,768]{2,1,0:T(8,128)} %get-tuple-element.33) | copy-start | bytes 589828
  411.6 10.5 %copy-start.36 = (f32[96,640]{1,0:T(8,128)S(1)}, f32[96,640]{1,0:T(8,128)}, u32[]{:S(2)}) copy-start(f32[96,640]{1,0:T(8,128)} %get-tuple-element.34) | copy-start | bytes 737284
  411.6 11.5 %copy-start.37 = (f32[96,256]{1,0:T(8,128)S(1)}, f32[96,256]{1,0:T(8,128)}, u32[]{:S(2)}) copy-start(f32[96,256]{1,0:T(8,128)} %get-tuple-element.35) | copy-start | bytes 294916
  411.6 12.3 %copy-start.33 = (f32[96,768]{1,0:T(8,128)S(1)}, f32[96,768]{1,0:T(8,128)}, u32[]{:S(2)}) copy-start(f32[96,768]{1,0:T(8,128)} %get-tuple-element.165) | copy-start | bytes 884740
  411.6 13.0 %copy-start.32 = (f32[96,768]{1,0:T(8,128)S(1)}, f32[96,768]{1,0:T(8,128)}, u32[]{:S(2)}) copy-start(f32[96,768]{1,0:T(8,128)} %get-tuple-element.37) | copy-start | bytes 884740
  (12 other events, 16.5 us)

commit v2 on v1

--- a/solution.py
+++ b/solution.py
@@ -15,7 +15,25 @@
 F32 = jnp.float32
 MESH = pl.DeviceIdType.MESH
 ANY = pl.BlockSpec(memory_space=pl.ANY)
+VM = pl.BlockSpec(memory_space=pltpu.VMEM)
 DMA = pltpu.SemaphoreType.DMA
+EPS = 1e-05
+
+
+def shape(dims, dtype):
+    return jax.ShapeDtypeStruct(dims, dtype)
+
+
+def dot(a, b):
+    return jnp.dot(a, b, preferred_element_type=F32)
+
+
+def contract_rows(left, right):
+    return lax.dot_general(left, right, (((0,), (0,)), ((), ())), preferred_element_type=F32)
+
+
+def contract_cols(left, right):
+    return lax.dot_general(left, right, (((1,), (1,)), ((), ())), preferred_element_type=F32)
 
 
 class Place:
@@ -53,222 +71,531 @@
 
 
 def params(cid):
-    return pltpu.CompilerParams(collective_id=cid, has_side_effects=True, vmem_limit_bytes=56 << 20)
-
-
-def gather_kernel(emb, trow, ids, w2, wo, E, TR, IDS, W2, WO, zs, zr, ts, tr, is_, ir, ps, pr, ls):
+    return pltpu.CompilerParams(collective_id=cid, has_side_effects=True, vmem_limit_bytes=60 << 20)
+
+
+def head_mask(width, h):
+    lane = lax.broadcasted_iota(jnp.int32, (1, width), 1)
+    return ((lane >= HD * h) & (lane < HD * h + HD)).astype(F32)
+
+
+def fold(rows):
+    half = rows.shape[-2] // 2
+    return jnp.concatenate((rows[..., :half, :], rows[..., half:, :]), axis=-1)
+
+
+def unfold(packed):
+    width = packed.shape[-1] // 2
+    return jnp.concatenate((packed[..., :width], packed[..., width:]), axis=-2)
+
+
+CH = 32
+
+
+def allowed(segc, sq, b, c):
+    key = CH * c + lax.broadcasted_iota(jnp.int32, (CH, 256), 0)
+    query = 256 * b + lax.broadcasted_iota(jnp.int32, (CH, 256), 1)
+    return ((segc[CH * c : CH * c + CH, :] == sq) & (sq != 0)) | (key == query)
+
+
+def lanes(b):
+    return pl.ds(pl.multiple_of(256 * b, 256), 256)
+
+
+def groups(x):
+    return x.reshape(CH // 8, 8, 256)
+
+
+class Weights:
+    def __init__(self, me, shards, W2, WO, zs, zr, ps, pr):
+        self.me, self.shards, self.W2, self.WO = me, shards, W2, WO
+        self.zs, self.zr, self.ps, self.pr = zs, zr, ps, pr
+
+    def zpart(self, a, q, piece, ref=None):
+        if a < 2:
+            rows = pl.ds(96 * piece, 96)
+            return self.W2.at[q, a, rows, :] if ref is None else ref.at[rows, :]
+        base = 192 * q if ref is None else 0
+        return (self.WO if ref is None else ref).at[
+            pl.ds(base + 48 * (piece // 2), 48), pl.ds(384 * (piece % 2), 384)
+        ]
+
+    def part(self, a, q, piece, half=None):
+        if a == 0:
+            lo, n = (0, 96) if half is None else (48 * half, 48)
+            return self.W2.at[q, :, pl.ds(96 * piece + lo, n), :]
+        lo, n = (0, 48) if half is None else ((0, 32), (32, 16))[half]
+        return self.WO.at[pl.ds(192 * q + 48 * (piece // 2) + lo, n), pl.ds(384 * (piece % 2), 384)]
+
+    def quarter(self, d, k):
+        j = self.me.j
+        return (j - k + 4) % 4 if d == 0 else (j + k) % 4
+
+    def sends(self, d, k):
+        j = self.me.j
+        return (j < 3) & (j >= k) if d == 0 else (j > 0) & (j + k <= 3)
+
+    def gets(self, d, k):
+        j = self.me.j
+        return j >= k + 1 if d == 0 else j + k + 1 <= 3
+
+    def zcopy(self, d, k, a):
+        p, q = self.me.p, self.quarter(d, k)
+        src = self.zpart(a, q, p, self.shards[a]) if k == 0 else self.zpart(a, q, p)
+        return push(src, self.zpart(a, q, p), self.zs.at[d, k, a], self.zr.at[d, k, a], self.me.z(1 if d == 0 else 3))
+
+    def zgot(self, d, k, a):
+        dst = self.zpart(a, self.quarter(d, k + 1), self.me.p)
+        return push(dst, dst, self.zs.at[d, k, a], self.zr.at[d, k, a], self.me.z(1))
+
+    def zstart(self, k, arrays):
+        for d in (0, 1):
+
+            @pl.when(self.sends(d, k))
+            def _():
+                for a in arrays:
+                    self.zcopy(d, k, a).start()
+
+    def zwait(self, k, arrays):
+        for d in (0, 1):
+
+            @pl.when(self.gets(d, k))
+            def _():
+                for a in arrays:
+                    self.zgot(d, k, a).wait_recv()
+
+    def routes(self, d, k, a, stage):
+        me, q = self.me, self.quarter(d, k + 1)
+        if stage == 0:
+            return [(self.part(a, q, me.p), me.px), (self.part(a, q, me.p), me.py), (self.part(a, q, me.p), me.pc)]
+        if stage == 1:
+            return [
+                (self.part(a, q, me.py, 0), me.px),
+                (self.part(a, q, me.px, 1), me.py),
+                (self.part(a, q, me.px), me.pc),
+                (self.part(a, q, me.py), me.pc),
+            ]
+        return [(self.part(a, q, me.pd), me.pc)]
+
+    def arrivals(self, d, k, a, stage):
+        me, q = self.me, self.quarter(d, k + 1)
+        c = me.pc - me.p
+        if stage == 0:
+            return [self.part(a, q, me.px), self.part(a, q, me.py), self.part(a, q, me.pc)]
+        if stage == 1:
+            return [
+                self.part(a, q, me.pd, 0),
+                self.part(a, q, me.pd, 1),
+                self.part(a, q, me.px + c),
+                self.part(a, q, me.py + c),
+            ]
+        return [self.part(a, q, me.pd + c)]
+
+    def pstart(self, k, stage):
+        for d in (0, 1):
+
+            @pl.when(self.gets(d, k))
+            def _():
+                for a in (0, 1):
+                    for i, (ref, dp) in enumerate(self.routes(d, k, a, stage)):
+                        s = 3 * stage + i if stage < 2 else 7
+                        push(ref, ref, self.ps.at[d, k, a, s], self.pr.at[d, k, a, s], self.me.at(dp)).start()
+
+    def pwait(self, k, stage, which, send=False):
+        for d in (0, 1):
+
+            @pl.when(self.gets(d, k))
+            def _():
+                for a in (0, 1):
+                    if send:
+                        refs = [r for r, _ in self.routes(d, k, a, stage)]
+                    else:
+                        refs = self.arrivals(d, k, a, stage)
+                    for i in which:
+                        s = 3 * stage + i if stage < 2 else 7
+                        c = push(refs[i], refs[i], self.ps.at[d, k, a, s], self.pr.at[d, k, a, s], self.me.at(self.me.pc))
+                        c.wait_send() if send else c.wait_recv()
+
+    def finish(self):
+        for k in range(3):
+            self.pwait(k, 0, (2,))
+            self.pwait(k, 1, (2, 3))
+            self.pwait(k, 2, (0,))
+            self.pwait(k, 0, (0, 1, 2), send=True)
+            self.pwait(k, 1, (0, 1, 2, 3), send=True)
+            self.pwait(k, 2, (0,), send=True)
+            for d in (0, 1):
+
+                @pl.when(self.sends(d, k))
+                def _():
+                    for a in (0, 1, 2):
+                        self.zcopy(d, k, a).wait_send()
+
+
+def front_kernel(
+    emb, trow, ids, segc, segr, par, wq, w_up, w_down, w_out,
+    qm_o, k_o, v_o, kt_o, n1_o, x_o, lse_o, att_o, IDS, W2, WO,
+    E, TR, vt, s, pb, ot, sendb, attg, own2, own_o,
+    es, er, ts, tr, is_, ir, zs, zr, ps, pr, as_, ar, ls,
+):
     me = Place()
     p, j = me.p, me.j
-    plane = [me.at((p + k) % 8) for k in range(1, 8)]
-    meet([me.z(1), me.z(2), me.z(3)] + plane)
-
-    def part(a, q, piece, half=None):
-        if a == 0:
-            lo, n = (0, 96) if half is None else (48 * half, 48)
-            return W2.at[q, :, pl.ds(96 * piece + lo, n), :]
-        lo, n = (0, 144) if half is None else ((0, 80), (80, 64))[half]
-        return WO.at[q, pl.ds(144 * piece + lo, n), :]
-
-    own = (w2.at[:, pl.ds(96 * p, 96), :], wo.at[pl.ds(144 * p, 144), :])
-
-    def quarter(d, k):
-        return (j - k + 4) % 4 if d == 0 else (j + k) % 4
-
-    def sends(d, k):
-        return (j < 3) & (j >= k) if d == 0 else (j > 0) & (j + k <= 3)
-
-    def gets(d, k):
-        return j >= k + 1 if d == 0 else j + k + 1 <= 3
-
-    def zcopy(d, k, a):
-        q = quarter(d, k)
-        if a == 2:
-            src = emb if k == 0 else E.at[q]
-            dst = E.at[q]
-        else:
-            src = own[a] if k == 0 else part(a, q, p)
-            dst = part(a, q, p)
-        return push(src, dst, zs.at[d, k, a], zr.at[d, k, a], me.z(1 if d == 0 else 3))
-
-    def zgot(d, k, a):
-        q = quarter(d, k + 1)
-        dst = E.at[q] if a == 2 else part(a, q, p)
-        return push(dst, dst, zs.at[d, k, a], zr.at[d, k, a], me.z(1))
-
-    def zstart(k, arrays):
+    meet([me.z(1), me.z(2), me.z(3)] + [me.at((p + k) % 8) for k in range(1, 8)])
+    w = Weights(me, (own2.at[0], own2.at[1], own_o), W2, WO, zs, zr, ps, pr)
+
+    def ecopy(d, k):
+        q = w.quarter(d, k)
+        return (emb if k == 0 else E.at[q], E.at[q], es.at[d, k], er.at[d, k], me.z(1 if d == 0 else 3))
+
+    def estart(k):
         for d in (0, 1):
 
-            @pl.when(sends(d, k))
+            @pl.when(w.sends(d, k))
             def _():
-                for a in arrays:
-                    zcopy(d, k, a).start()
-
-    def zwait(k, arrays):
+                push(*ecopy(d, k)).start()
+
+    def ewait(k):
         for d in (0, 1):
 
-            @pl.when(gets(d, k))
+            @pl.when(w.gets(d, k))
             def _():
-                for a in arrays:
-                    zgot(d, k, a).wait_recv()
-
-    def routes(d, k, a, stage):
-        q = quarter(d, k + 1)
-        if stage == 0:
-            return [(part(a, q, p), me.px), (part(a, q, p), me.py), (part(a, q, p), me.pc)]
-        if stage == 1:
-            return [
-                (part(a, q, me.py, 0), me.px),
-                (part(a, q, me.px, 1), me.py),
-                (part(a, q, me.px), me.pc),
-                (part(a, q, me.py), me.pc),
-            ]
-        return [(part(a, q, me.pd), me.pc)]
-
-    def arrivals(d, k, a, stage):
-        q = quarter(d, k + 1)
-        if stage == 0:
-            return [part(a, q, me.px), part(a, q, me.py), part(a, q, me.pc)]
-        if stage == 1:
-            return [
-                part(a, q, me.pd, 0),
-                part(a, q, me.pd, 1),
-                part(a, q, me.px + me.pc - p),
-                part(a, q, me.py + me.pc - p),
-            ]
-        return [part(a, q, me.pd + me.pc - p)]
-
-    def pstart(k, stage):
-        for d in (0, 1):
-
-            @pl.when(gets(d, k))
-            def _():
-                for a in (0, 1):
-                    for i, (ref, dp) in enumerate(routes(d, k, a, stage)):
-                        s = 3 * stage + i if stage < 2 else 7
-                        push(ref, ref, ps.at[d, k, a, s], pr.at[d, k, a, s], me.at(dp)).start()
-
-    def pwait(k, stage, which, send=False):
-        for d in (0, 1):
-
-            @pl.when(gets(d, k))
-            def _():
-                for a in (0, 1):
-                    refs = [r for r, _ in routes(d, k, a, stage)] if send else arrivals(d, k, a, stage)
-                    for i in which:
-                        s = 3 * stage + i if stage < 2 else 7
-                        c = push(refs[i], refs[i], ps.at[d, k, a, s], pr.at[d, k, a, s], me.at(me.pc))
-                        c.wait_send() if send else c.wait_recv()
-
-    locals_ = [
+                dst = E.at[w.quarter(d, k + 1)]
+                push(dst, dst, es.at[d, k], er.at[d, k], me.z(1)).wait_recv()
+
+    here = [
         pltpu.make_async_copy(emb, E.at[j], ls.at[0]),
         pltpu.make_async_copy(trow, TR.at[j], ls.at[1]),
         pltpu.make_async_copy(ids, IDS.at[p], ls.at[2]),
-        pltpu.make_async_copy(w2, W2.at[j], ls.at[3]),
-        pltpu.make_async_copy(wo, WO.at[j], ls.at[4]),
+    ]
+    load = [
+        pltpu.make_async_copy(w_up, own2.at[0], ls.at[3]),
+        pltpu.make_async_copy(w_down, own2.at[1], ls.at[4]),
+        pltpu.make_async_copy(w_out, own_o, ls.at[5]),
+    ]
+    keep = [
+        pltpu.make_async_copy(own2, W2.at[j], ls.at[3]),
+        pltpu.make_async_copy(own_o, WO.at[pl.ds(192 * j, 192), :], ls.at[5]),
     ]
     small = [push(trow, TR.at[j], ts.at[k - 1], tr.at[k - 1], me.z(k)) for k in (1, 2, 3)]
-    small += [push(ids, IDS.at[p], is_.at[k - 1], ir.at[k - 1], me.at((p + k) % 8)) for k in range(1, 8)]
-
-    zstart(0, (0, 1))
-    for c in small + locals_:
+    small_ids = [push(ids, IDS.at[p], is_.at[k - 1], ir.at[k - 1], me.at((p + k) % 8)) for k in range(1, 8)]
+
+    estart(0)
+    for c in load + small + here + small_ids:
         c.start()
-    zwait(0, (0, 1))
-    zstart(1, (0, 1))
-    pstart(0, 0)
-    zstart(0, (2,))
-    zwait(1, (0, 1))
-    zstart(2, (0, 1))
-    pwait(0, 0, (0, 1))
-    pstart(0, 1)
-    pstart(1, 0)
-    zwait(0, (2,))
-    zstart(1, (2,))
-    zwait(2, (0, 1))
-    pwait(0, 1, (0, 1))
-    pstart(0, 2)
-    pwait(1, 0, (0, 1))
-    pstart(1, 1)
-    pstart(2, 0)
-    zwait(1, (2,))
-    zstart(2, (2,))
-    pwait(1, 1, (0, 1))
-    pstart(1, 2)
-    pwait(2, 0, (0, 1))
-    pstart(2, 1)
-    pwait(2, 1, (0, 1))
-    pstart(2, 2)
-    zwait(2, (2,))
+    for c in load:
+        c.wait()
+    for c in keep:
+        c.start()
+    w.zstart(0, (0,))
+    ewait(0)
+    estart(1)
+    w.zstart(0, (1,))
+    ewait(1)
+    estart(2)
+    w.zstart(0, (2,))
+    w.zwait(0, (0,))
+    w.zstart(1, (0,))
+    w.zwait(0, (1, 2))
+    w.zstart(1, (1, 2))
+    w.pstart(0, 0)
+    ewait(2)
+    for c in small:
+        c.wait()
+    here[0].wait()
+    here[1].wait()
+
+    time_row = jnp.concatenate([TR[q].astype(F32)[0:1, 0:192] for q in range(4)], axis=1)
+    gain, shift = par[0:1, :], par[1:2, :]
+    for r in range(4):
+        h, o = r // 2, 256 * (r % 2)
+        rows = slice(256 * r, 256 * r + 256)
+        x = jnp.concatenate([E[q, o : o + 256, 192 * h : 192 * h + 192] for q in range(4)], axis=1)
+        x = x.astype(F32) + time_row
+        centered = x - jnp.mean(x, axis=1, keepdims=True)
+        variance = jnp.mean(centered * centered, axis=1, keepdims=True)
+        normed = (centered * lax.rsqrt(variance + EPS) * gain + shift).astype(BF)
+        n1_o[rows, :] = normed
+
+        @pl.when(j == r)
+        def _():
+            x_o[...] = x
+
+        q = contract_cols(normed, wq[0:192, :]).astype(BF).astype(F32) * 0.125
+        for i in range(3):
+            qm_o[i, rows, :] = (q * head_mask(192, i)).astype(BF)
+        k_o[rows, :] = contract_cols(normed, wq[192:384, :]).astype(BF)
+        v_o[rows, :] = contract_cols(normed, wq[384:576, :]).astype(BF)
+        kt_o[:, rows] = contract_cols(wq[192:384, :], normed).astype(BF)
+        vt[:, rows] = contract_cols(wq[384:576, :], normed).astype(BF)
+
+    def att_copy(b):
+        return push(sendb.at[b], attg.at[j], as_.at[b], ar.at[j], (p, b))
+
+    def step0():
+        w.zwait(1, (0,))
+        w.zstart(2, (0,))
+
+    def step1():
+        w.pwait(0, 0, (0, 1))
+        w.pstart(0, 1)
+
+    def step2():
+        w.zwait(1, (1, 2))
+        w.zstart(2, (1, 2))
+        w.pstart(1, 0)
+
+    def step3():
+        w.pwait(0, 1, (0, 1))
+        w.pstart(0, 2)
+
+    def step4():
+        w.pwait(1, 0, (0, 1))
+        w.pstart(1, 1)
+
+    def step5():
+        w.zwait(2, (0, 1, 2))
+        w.pstart(2, 0)
+
+    steps = {0: step0, 2: step1, 4: step2, 6: step3, 10: step4, 11: step5}
+
+    def slot(i, n):
+        for k, step in {k: v for k, v in steps.items() if k % 3 == n}.items():
+            pl.when(i == k // 3)(step)
+
+    @pl.loop(0, 4)
+    def _(i):
+        b = (j + 1 + i) % 4
+        sq = segr[0:1, lanes(b)]
+        for h in range(3):
+            s[h] = contract_cols(k_o[...], qm_o[h, lanes(b), :])
+        slot(i, 0)
+        top = [jnp.full((8, 256), -jnp.inf, F32)] * 3
+        for c in range(L // CH):
+            rows = slice(CH * c, CH * c + CH)
+            ok = allowed(segc, sq, b, c)
+            for h in range(3):
+                x = jnp.where(ok, s[h, rows, :], -1e30)
+                s[h, rows, :] = x
+                top[h] = jnp.maximum(top[h], jnp.max(groups(x), axis=0))
+        top = [jnp.max(m, axis=0, keepdims=True) for m in top]
+        slot(i, 1)
+        total = [jnp.zeros((8, 256), F32)] * 3
+        for c in range(L // CH):
+            rows = slice(CH * c, CH * c + CH)
+            for h in range(3):
+                e = jnp.exp(s[h, rows, :] - top[h])
+                pb[h, rows, :] = e.astype(BF)
+                total[h] = total[h] + jnp.sum(groups(e), axis=0)
+        for h in range(3):
+            t = jnp.sum(total[h], axis=0, keepdims=True)
+            lse_o[3 * b + h] = top[h] + jnp.log(t)
+            part = slice(64 * h, 64 * h + 64)
+            ot[part, :] = dot(vt[part, :], pb[h]) * (1.0 / t)
+        sendb[b] = fold(ot[...].T.astype(BF))
+
+        @pl.when(b != j)
+        def _():
+            att_copy(b).start()
+
+        slot(i, 2)
+
+    attg[j] = sendb[j]
+    w.pwait(1, 1, (0, 1))
+    w.pstart(1, 2)
+    for q in range(4):
+
+        @pl.when(j != q)
+        def _():
+            push(attg.at[q], attg.at[q], as_.at[q], ar.at[q], me.z(1)).wait_recv()
+
+    att_o[...] = jnp.concatenate([unfold(attg[q]) for q in range(4)], axis=1)
+    w.pwait(2, 0, (0, 1))
+    w.pstart(2, 1)
+    w.pwait(2, 1, (0, 1))
+    w.pstart(2, 2)
+    for b in range(4):
+
+        @pl.when(j != b)
+        def _():
+            att_copy(b).wait_send()
+
     for k in range(3):
-        pwait(k, 0, (2,))
-        pwait(k, 1, (2, 3))
-        pwait(k, 2, (0,))
-        pwait(k, 0, (0, 1, 2), send=True)
-        pwait(k, 1, (0, 1, 2, 3), send=True)
-        pwait(k, 2, (0,), send=True)
         for d in (0, 1):
 
-            @pl.when(sends(d, k))
+            @pl.when(w.sends(d, k))
             def _():
-                for a in (0, 1, 2):
-                    zcopy(d, k, a).wait_send()
-
-    for c in small + locals_:
+                push(*ecopy(d, k)).wait_send()
+
+    w.finish()
+    for c in small_ids + here[2:] + keep:
         c.wait()
 
 
-def gather_all(emb, trow, ids, w2, wo):
+def front(emb, trow, ids, segc, segr, par, wq, w_up, w_down, w_out):
     return pl.pallas_call(
-        gather_kernel,
+        front_kernel,
         out_shape=(
-            jax.ShapeDtypeStruct((4,) + emb.shape, BF),
-            jax.ShapeDtypeStruct((4,) + trow.shape, BF),
-            jax.ShapeDtypeStruct((8,) + ids.shape, jnp.int32),
-            jax.ShapeDtypeStruct((4,) + w2.shape, BF),
-            jax.ShapeDtypeStruct((4,) + wo.shape, BF),
+            shape((3, L, 192), BF),
+            shape((L, 192), BF),
+            shape((L, 192), BF),
+            shape((192, L), BF),
+            shape((L, D), BF),
+            shape((256, D), F32),
+            shape((12, 1, 256), F32),
+            shape((256, D), BF),
+            shape((8, 8, 128), jnp.int32),
+            shape((4, 2, D, D), BF),
+            shape((D, D), BF),
         ),
-        in_specs=[ANY] * 5,
-        out_specs=(ANY,) * 5,
+        in_specs=[ANY] * 3 + [VM] * 4 + [ANY] * 3,
+        out_specs=(VM,) * 8 + (ANY,) * 3,
         scratch_shapes=[
-            DMA((2, 3, 3)),
-            DMA((2, 3, 3)),
+            pltpu.VMEM((4, 512, 384), BF),
+            pltpu.VMEM((4, 16, 256), BF),
+            pltpu.VMEM((192, L), BF),
+            pltpu.VMEM((3, L, 256), F32),
+            pltpu.VMEM((3, L, 256), BF),
+            pltpu.VMEM((192, 256), F32),
+            pltpu.VMEM((4, 128, 384), BF),
+            pltpu.VMEM((4, 128, 384), BF),
+            pltpu.VMEM((2, D, D), BF),
+            pltpu.VMEM((192, D), BF),
+            DMA((2, 3)),
+            DMA((2, 3)),
             DMA((3,)),
             DMA((3,)),
             DMA((7,)),
             DMA((7,)),
+            DMA((2, 3, 3)),
+            DMA((2, 3, 3)),
             DMA((2, 3, 2, 8)),
             DMA((2, 3, 2, 8)),
-            DMA((5,)),
+            DMA((4,)),
+            DMA((4,)),
+            DMA((6,)),
         ],
         compiler_params=params(0),
-        name="gather_all",
-    )(emb, trow, ids, w2, wo)
-
-
-def exchange_kernel(x, out, send, recv, local):
-    me = Place()
-    meet([me.z(1), me.z(2), me.z(3)])
-    mine = pltpu.make_async_copy(x.at[me.j], out.at[me.j], local)
-    copies = [
-        push(x.at[(me.j + k) % 4], out.at[me.j], send.at[k - 1], recv.at[k - 1], me.z(k)) for k in (1, 2, 3)
-    ]
-    for c in copies:
-        c.start()
-    mine.start()
-    for c in copies:
-        c.wait()
-    mine.wait()
-
-
-def exchange(x, cid, name):
+        name="front",
+    )(emb, trow, ids, segc, segr, par, wq, w_up, w_down, w_out)
+
+
+def norm_stats(x):
+    centered = x - jnp.mean(x, axis=1, keepdims=True)
+    scale = lax.rsqrt(jnp.mean(centered * centered, axis=1, keepdims=True) + EPS)
+    return centered * scale, scale
+
+
+def norm_back(grad, gain, hat, scale):
+    t = grad * gain
+    return scale * (t - jnp.mean(t, axis=1, keepdims=True) - hat * jnp.mean(t * hat, axis=1, keepdims=True))
+
+
+def rows_sum(x):
+    return jnp.sum(x, axis=0, keepdims=True)
+
+
+def mid_kernel(
+    att, x, wo, w2, cot, segc, par,
+    out_o, gmid_o, gatt_o, dw_o, dwo_o, vec_o,
+    sm, hat, sc, n2, n2t, gmt, gm, acc, gn2,
+):
+    q = pl.program_id(0)
+
+    @pl.when(q == 0)
+    def _():
+        mid = x[...] + dot(att[...], wo[...]) + par[2:3, :]
+        sm[...] = mid
+        h, scale = norm_stats(mid)
+        hat[...] = h
+        sc[...] = scale
+        normed = (h * par[3:4, :] + par[4:5, :]).astype(BF)
+        n2[...] = normed
+        n2t[...] = normed.astype(F32).T.astype(BF)
+        valid = (segc[...] != 0).astype(F32)
+        grad = cot[...].astype(F32) * valid
+        gm[...] = grad.astype(BF)
+        gmt[...] = grad.T.astype(BF)
+        acc[...] = mid + par[5:6, :]
+        gn2[...] = jnp.zeros_like(gn2)
+
+    up, down = w2[0, 0], w2[0, 1]
+    pre = dot(n2[...], up)
+    c = 0.7978845608028654
+    cubic = c * (pre + 0.044715 * pre * pre * pre)
+    t = jnp.tanh(cubic)
+    act = (0.5 * pre * (1.0 + t)).astype(BF)
+    slope = 0.5 * (1.0 + t) + 0.5 * pre * (1.0 - t * t) * (c * (1.0 + 3 * 0.044715 * pre * pre))
+    acc[...] += dot(act, down)
+    grad_pre = (contract_cols(gm[...], down) * slope).astype(BF)
+    gn2[...] += contract_cols(grad_pre, up)
+    dw_o[0, 0] = dot(n2t[...], grad_pre).astype(BF)
+    dw_o[1, 0] = dot(gmt[...], act).astype(BF)
+
+    @pl.when(q == 3)
+    def _():
+        out_o[...] = acc[...].astype(BF)
+        grad = cot[...].astype(F32) * (segc[...] != 0).astype(F32)
+        gn, h = gn2[...], hat[...]
+        gmid = grad + norm_back(gn, par[3:4, :], h, sc[...])
+        gmid_o[...] = gmid
+        vec_o[...] = jnp.zeros_like(vec_o)
+        vec_o[2:3, :] = rows_sum(gmid)
+        vec_o[3:4, :] = rows_sum(gn * h)
+        vec_o[4:5, :] = rows_sum(gn)
+        vec_o[5:6, :] = rows_sum(grad)
+        ga = gmid.astype(BF)
+        gatt_o[...] = contract_cols(ga, wo[...]).astype(BF)
+        full = dot(gmid.T.astype(BF), att[...]).astype(BF)
+        for i in range(4):
+            dwo_o[i, :, 0:192] = full[:, 192 * i : 192 * i + 192]
+            dwo_o[i, :, 192:256] = jnp.zeros((D, 64), BF)
+
+
+def mid(att, x, wo, w2, cot, segc, par):
+    whole = lambda a: pl.BlockSpec(a.shape, lambda q: (0,) * a.ndim)
+    keep = lambda *dims: pl.BlockSpec(dims, lambda q: (0,) * len(dims))
     return pl.pallas_call(
-        exchange_kernel,
-        out_shape=jax.ShapeDtypeStruct(x.shape, x.dtype),
-        in_specs=[ANY],
-        out_specs=ANY,
-        scratch_shapes=[DMA((3,)), DMA((3,)), DMA],
-        compiler_params=params(cid),
-        name=name,
-    )(x)
+        mid_kernel,
+        grid=(4,),
+        out_shape=(
+            shape((256, D), BF),
+            shape((256, D), F32),
+            shape((256, D), BF),
+            shape((2, 4, D, D), BF),
+            shape((4, D, 256), BF),
+            shape((8, D), F32),
+        ),
+        in_specs=[
+            whole(att),
+            whole(x),
+            whole(wo),
+            pl.BlockSpec((1, 2, D, D), lambda q: (q, 0, 0, 0)),
+            whole(cot),
+            whole(segc),
+            whole(par),
+        ],
+        out_specs=(
+            keep(256, D),
+            keep(256, D),
+            keep(256, D),
+            pl.BlockSpec((2, 1, D, D), lambda q: (0, q, 0, 0)),
+            keep(4, D, 256),
+            keep(8, D),
+        ),
+        scratch_shapes=[
+            pltpu.VMEM((256, D), F32),
+            pltpu.VMEM((256, D), F32),
+            pltpu.VMEM((256, 1), F32),
+            pltpu.VMEM((256, D), BF),
+            pltpu.VMEM((D, 256), BF),
+            pltpu.VMEM((D, 256), BF),
+            pltpu.VMEM((256, D), BF),
+            pltpu.VMEM((256, D), F32),
+            pltpu.VMEM((256, D), F32),
+        ],
+        compiler_params=pltpu.CompilerParams(vmem_limit_bytes=60 << 20, dimension_semantics=("arbitrary",)),
+        name="mid",
+    )(att, x, wo, w2, cot, segc, par)
 
 
 class Line:
@@ -281,46 +608,26 @@
             return push(self.acc(q), self.up.at[q], self.us.at[q], self.ur.at[q], self.me.z(1))
         return push(self.acc(q), self.down.at[q], self.ds.at[q], self.dr.at[q], self.me.z(3))
 
-    def go(self, q, d):
-        j, ref = self.me.j, self.acc(q)
-        here = (j < q) if d == 0 else (j > q)
-        inner = (j > 0) if d == 0 else (j < 3)
-        got = self.up if d == 0 else self.down
-
-        @pl.when(here & inner)
-        def _():
-            self.send(q, d).wait_recv()
-            ref[...] = ref[...] + got[q]
-
-        @pl.when(here)
+    def end(self, q, d):
+        @pl.when(self.me.j == (0 if d == 0 else 3))
         def _():
             self.send(q, d).start()
 
     def first(self):
-        j = self.me.j
-
-        @pl.when(j == 0)
-        def _():
-            for q in (3, 2, 1):
-                self.send(q, 0).start()
-
-        @pl.when(j == 3)
-        def _():
-            for q in (0, 1, 2):
-                self.send(q, 1).start()
+        for q in (3, 2, 1):
+            self.end(q, 0)
+        for q in (0, 1, 2):
+            self.end(q, 1)
 
     def inner(self, steps):
-        j = self.me.j
-        for q, d in steps:
-            got = self.up if d == 0 else self.down
-            cond = ((j < q) & (j > 0)) if d == 0 else ((j > q) & (j < 3))
-
-            @pl.when(cond)
+        for q, d, j in steps:
+
+            @pl.when(self.me.j == j)
             def _():
                 c = self.send(q, d)
                 c.wait_recv()
                 ref = self.acc(q)
-                ref[...] = ref[...] + got[q]
+                ref[...] = ref[...] + (self.up if d == 0 else self.down)[q]
                 c.start()
 
     def finish(self, out):
@@ -338,6 +645,10 @@
                     total = total + self.down[q].astype(F32)
                 out[...] = total
 
+    def close(self):
+        j = self.me.j
+        for q in range(4):
+
             @pl.when(j < q)
             def _():
                 self.send(q, 0).wait_send()
@@ -347,8 +658,8 @@
                 self.send(q, 1).wait_send()
 
 
-OUTER = ((3, 0), (0, 1))
-MIDDLE = ((2, 0), (1, 1))
+NEAR = ((3, 0, 1), (0, 1, 2))
+FAR = ((3, 0, 2), (0, 1, 1), (2, 0, 1), (1, 1, 2))
 
 
 class Unit:
@@ -397,16 +708,20 @@
 
     def turn(self):
         me = self.me
-        for c in self.copies(1):
+        first = self.copies(1)
+        for c in first[:2]:
             c.wait()
+        second = self.copies(2)
 
         @pl.loop(0, self.nq)
         def _(q):
             self.acc[q, me.my, 0:48] = self.acc[q, me.my, 0:48] + self.rx[q, 1]
             self.acc[q, me.mx, 48:96] = self.acc[q, me.mx, 48:96] + self.ry[q, 1]
 
-        for c in self.copies(2):
+        for c in second:
             c.start()
+        for c in first[2:]:
+            c.wait()
 
         @pl.loop(0, self.nq)
         def _(q):
@@ -429,13 +744,25 @@
         return self.acc.at[q, self.me.m]
 
 
-def reduce_kernel(gn, dw, dwo, dqkv, o_gn, o_up, o_down, o_out, o_qkv, *scratch):
+SHAPES = ((4, 768), (4, 768), (4, 256), (3, 256))
+
+
+def back_kernel(
+    gatt, qm, k, v, kt, lse, n1, wq, x, gmid, segc, segr, par, vec, IDS, step, dw, dwo,
+    o_in, o_tok, o_up, o_down, o_out, o_qkv, o_sp,
+    *scratch,
+):
     me = Place()
-    meet([me.z(1), me.z(2), me.z(3), me.at(me.px), me.at(me.py), me.at(me.pc)])
+    p, j = me.p, me.j
+    meet([me.z(1), me.z(2), me.z(3)] + [me.at((p + i) % 8) for i in range(1, 8)])
     it = iter(scratch)
     take = lambda n: [next(it) for _ in range(n)]
-    gacc, gup, gdown, gsem, gl = take(5)
-    sources = (dw.at[1], dw.at[0], dwo, dqkv)
+    sendb, gbuf, dom, s, dp, pb, dsb, dqt, dqn, dk, dv, gn = take(12)
+    as_, ar = take(2)
+    gacc, gup, gdown, gsem = take(4)
+    qk, tb, X, hot, vbuf, SZ, vs = take(7)
+    vzs, vzr, ts, tr, ps, pr, vps, vpr, ls = take(9)
+    sources = (dw.at[1], dw.at[0], dwo, qk)
     units, lines = [], []
     for i, src in enumerate(sources):
         acc, rc, rx, ry, rx2, ry2, sems, lsem = take(8)
@@ -445,55 +772,265 @@
             up, down, sem = take(3)
             lines.append(Line(me, unit.own, up, down, sem))
     own = Line(me, lambda q: gacc.at[q], gup, gdown, gsem)
-    load = pltpu.make_async_copy(gn, gacc, gl)
-    load.start()
-    for u in units:
+
+    def to_heads(d):
+        return push(sendb.at[d], gbuf.at[j], as_.at[d], ar.at[j], (p, d))
+
+    for d in range(4):
+        sendb[d] = fold(gatt[:, 192 * d : 192 * d + 192])
+
+        @pl.when(j != d)
+        def _():
+            to_heads(d).start()
+
+    gbuf[j] = sendb[j]
+    for u in units[:3]:
         u.begin()
-    load.wait()
-    own.first()
-    units[0].chip()
-    units[0].cross()
-    for u in units[1:]:
-        u.chip()
-    own.inner(OUTER)
-    units[0].turn()
-    units[1].cross()
-    own.inner(MIDDLE)
+    dk[...] = jnp.zeros_like(dk)
+    dv[...] = jnp.zeros_like(dv)
+
+    def step0():
+        units[0].chip()
+        units[0].cross()
+
+    def step1():
+        units[1].chip()
+
+    def step2():
+        units[2].chip()
+
+    def step3():
+        units[0].turn()
+        units[1].cross()
+
+    steps = {0: step0, 1: step1, 2: step2, 11: step3}
+
+    def slot(i, n):
+        for c, fn in {c: fn for c, fn in steps.items() if c % 3 == n}.items():
+            pl.when(i == c // 3)(fn)
+
+    @pl.loop(0, 4)
+    def _(i):
+        b = (j + i) % 4
+        sq = segr[0:1, lanes(b)]
+
+        @pl.when(i > 0)
+        def _():
+            push(gbuf.at[b], gbuf.at[b], as_.at[b], ar.at[b], me.z(1)).wait_recv()
+
+        do = unfold(gbuf[b]).astype(F32)
+        for h in range(3):
+            dom[h] = (do * head_mask(192, h)).astype(BF)
+            s[h] = contract_cols(k[...], qm[h, lanes(b), :])
+            dp[h] = contract_cols(v[...], dom[h])
+        slot(i, 0)
+        ls_ = [lse[3 * b + h] for h in range(3)]
+        inner = [jnp.zeros((8, 256), F32)] * 3
+        for c in range(L // CH):
+            rows = slice(CH * c, CH * c + CH)
+            ok = allowed(segc, sq, b, c)
+            for h in range(3):
+                e = jnp.exp(jnp.where(ok, s[h, rows, :], -1e30) - ls_[h])
+                s[h, rows, :] = e
+                pb[rows, 256 * h : 256 * h + 256] = e.astype(BF)
+                inner[h] = inner[h] + jnp.sum(groups(e * dp[h, rows, :]), axis=0)
+        inner = [jnp.sum(a, axis=0, keepdims=True) for a in inner]
+        slot(i, 1)
+        for c in range(L // CH):
+            rows = slice(CH * c, CH * c + CH)
+            for h in range(3):
+                grad = s[h, rows, :] * (dp[h, rows, :] - inner[h])
+                dsb[rows, 256 * h : 256 * h + 256] = grad.astype(BF)
+        dv[...] += dot(pb[...], dom[...].reshape(768, 192))
+        dk[...] += dot(dsb[...], qm[:, lanes(b), :].reshape(768, 192))
+        for h in range(3):
+            part = slice(64 * h, 64 * h + 64)
+            dqt[part, lanes(b)] = dot(kt[part, :], dsb[:, 256 * h : 256 * h + 256]) * 0.125
+        slot(i, 2)
+
+    for q, starts in ((3, ((3, 0),)), (0, ((0, 1),)), (2, ((2, 0),)), (1, ((1, 1), (1, 0), (2, 1)))):
+        rows = slice(256 * q, 256 * q + 256)
+        dq = dqt[:, rows].T.astype(BF)
+        dqn[rows, :] = dq
+        total = dot(dq, wq[0:192, :]) + dot(dk[rows, :].astype(BF), wq[192:384, :])
+        gacc[q] = (total + dot(dv[rows, :].astype(BF), wq[384:576, :])).astype(BF)
+        for block, d in starts:
+            own.end(block, d)
+    for i, grad in enumerate((dqn[...], dk[...].astype(BF), dv[...].astype(BF))):
+        full = contract_rows(n1[...], grad).astype(BF)
+        for piece in range(8):
+            qk[i, piece // 2, piece % 2, :, 0:192] = full[96 * piece : 96 * piece + 96, :]
+            qk[i, piece // 2, piece % 2, :, 192:256] = jnp.zeros((96, 64), BF)
+    units[3].begin()
+    own.inner(NEAR)
+    units[3].chip()
     units[0].settle()
-    lines[0].first()
+    own.inner(FAR)
     units[1].turn()
     units[2].cross()
     units[3].cross()
-    own.inner(((3, 0), (0, 1))[:0])
-    lines[0].inner(OUTER)
+    own.finish(gn)
+    lines[0].first()
+
+    hat, scale = norm_stats(x[...])
+    grad = gn[...]
+    dx = gmid[...] + norm_back(grad, par[0:1, :], hat, scale)
+    o_in[...] = dx
+    dxb = dx.astype(BF)
+
+    def to_columns(d):
+        return push(tb.at[d], X.at[p, j], ts.at[d], tr.at[j], (p, d))
+
+    for d in range(4):
+        tb[d] = fold(dxb[:, 192 * d : 192 * d + 192])
+
+        @pl.when(j != d)
+        def _():
+            to_columns(d).start()
+
+    X[p, j] = tb[j]
+    vbuf[...] = vec[...]
+    vbuf[0:1, :] = rows_sum(grad * hat)
+    vbuf[1:2, :] = rows_sum(grad)
+    vbuf[6:7, :] = rows_sum(dx)
+    first = jnp.where(j == 0, step[0], 0).astype(F32)
+    vbuf[7:8, :] = jnp.full((1, D), 1.0, F32) * first
+    small = [push(vbuf, SZ.at[j], vzs.at[i - 1], vzr.at[i - 1], me.z(i)) for i in (1, 2, 3)]
+    for c in small:
+        c.start()
+    SZ[j] = vbuf[...]
     units[1].settle()
     lines[1].first()
+    lines[0].inner(NEAR)
+    for c in small:
+        c.wait()
+    vs[...] = SZ[0] + SZ[1] + SZ[2] + SZ[3]
+    out_v = [push(vs, o_sp.at[p], vps.at[i - 1], vpr.at[i - 1], me.at((p + i) % 8)) for i in range(1, 8)]
+    for c in out_v:
+        c.start()
+    o_sp[p] = vs[...]
+
+    for q in range(4):
+
+        @pl.when(j != q)
+        def _():
+            push(X.at[p, q], X.at[p, q], ts.at[q], tr.at[q], me.z(1)).wait_recv()
+
+    half = (pl.ds(0, 2), pl.ds(2, 2))
+
+    def to(ref, i, dev):
+        return push(ref, ref, ps.at[i], pr.at[i], me.at(dev))
+
+    first_hop = [to(X.at[p], 0, me.px), to(X.at[p], 1, me.py), to(X.at[p], 2, me.pc)]
+    for c in first_hop:
+        c.start()
+
+    def table(d, start=False):
+        vocab = 1024 * p + lax.broadcasted_iota(jnp.int32, (1024, 128), 0)
+        for g in range(8):
+            hot[:, 128 * g : 128 * g + 128] = (vocab == IDS[d, g : g + 1, :]).astype(F32).astype(BF)
+        rows = jnp.concatenate([unfold(X[d, q]) for q in range(4)], axis=0)
+        part = dot(hot[...], rows)
+        if start:
+            o_tok[...] = part
+        else:
+            o_tok[...] += part
+
+    here = me.pc - p
+    table(p, start=True)
+    to(X.at[me.pc], 2, me.pc).wait_recv()
+    to(X.at[me.px], 0, me.px).wait_recv()
+    to(X.at[me.py], 1, me.py).wait_recv()
+    second = [
+        to(X.at[me.py, half[0]], 3, me.px),
+        to(X.at[me.px, half[1]], 4, me.py),
+        to(X.at[me.px], 5, me.pc),
+        to(X.at[me.py], 6, me.pc),
+    ]
+    for c in second:
+        c.start()
+    table(me.pc)
     units[2].turn()
     units[3].turn()
-    lines[0].inner(MIDDLE)
-    own.finish(o_gn)
+    table(me.px)
+    lines[0].inner(FAR)
+    lines[1].inner(NEAR)
+    table(me.py)
+    to(X.at[me.pd, half[0]], 3, me.px).wait_recv()
+    to(X.at[me.pd, half[1]], 4, me.px).wait_recv()
+    third = to(X.at[me.pd], 7, me.pc)
+    third.start()
     units[2].settle()
     lines[2].first()
-    lines[1].inner(OUTER)
     units[3].settle()
-    lines[2].inner(OUTER)
-    lines[1].inner(MIDDLE)
-    lines[2].inner(MIDDLE)
+    table(me.pd)
+    to(X.at[me.px + here], 5, me.pc).wait_recv()
+    table(me.px + here)
+    lines[1].inner(FAR)
+    lines[2].inner(NEAR)
+    to(X.at[me.py + here], 6, me.pc).wait_recv()
+    table(me.py + here)
+    lines[2].inner(FAR)
+    to(X.at[me.pd + here], 7, me.pc).wait_recv()
+    table(me.pd + here)
     lines[0].finish(o_down)
     lines[1].finish(o_up)
     lines[2].finish(o_out)
-    o_qkv[...] = units[3].acc[0, me.m].astype(F32)
-
-
-def reduce_all(gn, dw, dwo, dqkv):
+    for i in range(3):
+        o_qkv[i] = units[3].acc[i, me.m].astype(F32)
+    for c in out_v:
+        c.wait()
+    for c in first_hop + second + [third]:
+        c.wait_send()
+    for d in range(4):
+
+        @pl.when(j != d)
+        def _():
+            to_heads(d).wait_send()
+            to_columns(d).wait_send()
+
+    for line in lines + [own]:
+        line.close()
+
+
+def back(gatt, qm, k, v, kt, lse, n1, wq, x, gmid, segc, segr, par, vec, ids, step, dw, dwo):
     scratch = [
-        pltpu.VMEM((4, 256, 768), BF),
-        pltpu.VMEM((4, 256, 768), BF),
-        pltpu.VMEM((4, 256, 768), BF),
+        pltpu.VMEM((4, 128, 384), BF),
+        pltpu.VMEM((4, 128, 384), BF),
+        pltpu.VMEM((3, 256, 192), BF),
+        pltpu.VMEM((3, L, 256), F32),
+        pltpu.VMEM((3, L, 256), F32),
+        pltpu.VMEM((L, 768), BF),
+        pltpu.VMEM((L, 768), BF),
+        pltpu.VMEM((192, L), F32),
+        pltpu.VMEM((L, 192), BF),
+        pltpu.VMEM((L, 192), F32),
+        pltpu.VMEM((L, 192), F32),
+        pltpu.VMEM((256, D), F32),
+        DMA((4,)),
+        DMA((4,)),
+        pltpu.VMEM((4, 256, D), BF),
+        pltpu.VMEM((4, 256, D), BF),
+        pltpu.VMEM((4, 256, D), BF),
         DMA((4, 4)),
-        DMA,
+        pltpu.VMEM((3, 4, 2, 96, 256), BF),
+        pltpu.VMEM((4, 128, 384), BF),
+        pltpu.VMEM((8, 4, 128, 384), BF),
+        pltpu.VMEM((1024, 1024), BF),
+        pltpu.VMEM((8, D), F32),
+        pltpu.VMEM((4, 8, D), F32),
+        pltpu.VMEM((8, D), F32),
+        DMA((3,)),
+        DMA((3,)),
+        DMA((4,)),
+        DMA((4,)),
+        DMA((8,)),
+        DMA((8,)),
+        DMA((7,)),
+        DMA((7,)),
+        DMA((2,)),
     ]
-    for i, (nq, w) in enumerate(((4, 768), (4, 768), (4, 256), (1, 640))):
+    for i, (nq, w) in enumerate(SHAPES):
         scratch += [
             pltpu.VMEM((nq, 4, 96, w), BF),
             pltpu.VMEM((nq, 4, 96, w), BF),
@@ -506,102 +1043,23 @@
         ]
         if i < 3:
             scratch += [pltpu.VMEM((4, 96, w), BF), pltpu.VMEM((4, 96, w), BF), DMA((4, 4))]
-    vm = pl.BlockSpec(memory_space=pltpu.VMEM)
     return pl.pallas_call(
-        reduce_kernel,
+        back_kernel,
         out_shape=(
-            jax.ShapeDtypeStruct((256, 768), F32),
-            jax.ShapeDtypeStruct((96, 768), F32),
-            jax.ShapeDtypeStruct((96, 768), F32),
-            jax.ShapeDtypeStruct((96, 256), F32),
-            jax.ShapeDtypeStruct((96, 640), F32),
+            shape((256, D), F32),
+            shape((1024, 192), F32),
+            shape((96, D), F32),
+            shape((96, D), F32),
+            shape((96, 256), F32),
+            shape((3, 96, 256), F32),
+            shape((8, 8, D), F32),
         ),
-        in_specs=[ANY] * 4,
-        out_specs=(vm,) * 5,
+        in_specs=[VM] * 15 + [pl.BlockSpec(memory_space=pltpu.SMEM)] + [ANY] * 2,
+        out_specs=(VM,) * 7,
         scratch_shapes=scratch,
-        compiler_params=params(3),
-        name="reduce_all",
-    )(gn, dw, dwo, dqkv)
-
-
-def final_kernel(tp, vec, X, SP, SZ, vs, zs, zr, vzs, vzr, ps, pr, vps, vpr, ls):
-    me = Place()
-    p, j = me.p, me.j
-    meet([me.z(1), me.z(2), me.z(3)] + [me.at((p + k) % 8) for k in range(1, 8)])
-    small = [push(vec, SZ.at[j], vzs.at[k - 1], vzr.at[k - 1], me.z(k)) for k in (1, 2, 3)]
-    big = [push(tp.at[(j + k) % 4], X.at[p, j], zs.at[k - 1], zr.at[k - 1], me.z(k)) for k in (1, 2, 3)]
-    mine = pltpu.make_async_copy(tp.at[j], X.at[p, j], ls.at[0])
-    mine_v = pltpu.make_async_copy(vec, SZ.at[j], ls.at[1])
-    for c in small + big + [mine, mine_v]:
-        c.start()
-    for c in small + [mine_v]:
-        c.wait()
-    vs[...] = SZ[0] + SZ[1] + SZ[2] + SZ[3]
-    out_v = [push(vs, SP.at[p], vps.at[k - 1], vpr.at[k - 1], me.at((p + k) % 8)) for k in range(1, 8)]
-    own_v = pltpu.make_async_copy(vs, SP.at[p], ls.at[2])
-    for c in out_v + [own_v]:
-        c.start()
-    for c in big + [mine]:
-        c.wait()
-    lo, hi = pl.ds(0, 2), pl.ds(2, 2)
-
-    def to(ref, i, dp):
-        return push(ref, ref, ps.at[i], pr.at[i], me.at(dp))
-
-    first = [to(X.at[p], 0, me.px), to(X.at[p], 1, me.py), to(X.at[p], 2, me.pc)]
-    for c in first:
-        c.start()
-    here = me.pc - p
-    to(X.at[me.px], 0, me.px).wait_recv()
-    to(X.at[me.py], 1, me.py).wait_recv()
-    second = [
-        to(X.at[me.py, lo], 3, me.px),
-        to(X.at[me.px, hi], 4, me.py),
-        to(X.at[me.px], 5, me.pc),
-        to(X.at[me.py], 6, me.pc),
-    ]
-    for c in second:
-        c.start()
-    to(X.at[me.pd, lo], 3, me.px).wait_recv()
-    to(X.at[me.pd, hi], 4, me.px).wait_recv()
-    third = to(X.at[me.pd], 7, me.pc)
-    third.start()
-    to(X.at[me.pc], 2, me.pc).wait_recv()
-    to(X.at[me.px + here], 5, me.pc).wait_recv()
-    to(X.at[me.py + here], 6, me.pc).wait_recv()
-    to(X.at[me.pd + here], 7, me.pc).wait_recv()
-    for c in first + second + [third]:
-        c.wait_send()
-    for c in out_v + [own_v]:
-        c.wait()
-
-
-def final_exchange(tp, vec):
-    return pl.pallas_call(
-        final_kernel,
-        out_shape=(
-            jax.ShapeDtypeStruct((8,) + tp.shape, BF),
-            jax.ShapeDtypeStruct((8, 8, D), F32),
-        ),
-        in_specs=[ANY] * 2,
-        out_specs=(ANY,) * 2,
-        scratch_shapes=[
-            pltpu.VMEM((4, 8, D), F32),
-            pltpu.VMEM((8, D), F32),
-            DMA((3,)),
-            DMA((3,)),
-            DMA((3,)),
-            DMA((3,)),
-            DMA((8,)),
-            DMA((8,)),
-            DMA((7,)),
-            DMA((7,)),
-            DMA((3,)),
-        ],
-        compiler_params=params(4),
-        name="final_exchange",
-    )(tp, vec)
-
+        compiler_params=params(1),
+        name="back",
+    )(gatt, qm, k, v, kt, lse, n1, wq, x, gmid, segc, segr, par, vec, ids, step, dw, dwo)
 
 class Native:
     def __init__(self, ndp, nmp):
@@ -638,13 +1096,6 @@
             lax.all_gather(x, "dp", axis=0, tiled=False),
             lax.all_gather(lax.psum(vec, "mp"), "dp", axis=0, tiled=False),
         )
-
-
-class Tuned:
-    gather_all = staticmethod(gather_all)
-    exchange = staticmethod(exchange)
-    reduce_all = staticmethod(reduce_all)
-    final_exchange = staticmethod(final_exchange)
 
 
 def layer_norm(stream, gain, shift):
@@ -711,29 +1162,7 @@
     )
 
 
-def dot(a, b):
-    return jnp.dot(a, b, preferred_element_type=F32)
-
-
-def contract_rows(left, right):
-    return lax.dot_general(left, right, (((0,), (0,)), ((), ())), preferred_element_type=F32)
-
-
-def contract_cols(left, right):
-    return lax.dot_general(left, right, (((1,), (1,)), ((), ())), preferred_element_type=F32)
-
-
-def fold(rows):
-    half = rows.shape[-2] // 2
-    return jnp.concatenate((rows[..., :half, :], rows[..., half:, :]), axis=-1)
-
-
-def unfold(packed):
-    width = packed.shape[-1] // 2
-    return jnp.concatenate((packed[..., :width], packed[..., width:]), axis=-2)
-
-
-def on_device(
+def on_device_native(
     comm,
     token_ids,
     segment_ids,
@@ -871,6 +1300,43 @@
     )
 
 
+def on_device_tuned(
+    token_ids, segment_ids, timesteps, token_table, time_table, ln1_gain, ln1_bias, w_qkv, w_out, attn_bias,
+    ln2_gain, ln2_bias, w_up, w_down, mlp_bias, cotangent,
+):
+    group, ndp = 4, 8
+    member = lax.axis_index("mp")
+    own_rows, width = 256, 192
+    emb = fold(token_table[token_ids])
+    time_row = lax.dynamic_slice_in_dim(time_table, timesteps[0], 1, 0)
+    trow = jnp.broadcast_to(jnp.pad(time_row, ((0, 0), (0, 256 - width))), (16, 256))
+    ids = token_ids.reshape(8, 128)
+    wq = w_qkv.transpose(1, 2, 0).reshape(3 * width, D)
+    segc, segr = segment_ids.reshape(L, 1), segment_ids.reshape(1, L)
+    par = jnp.stack((ln1_gain, ln1_bias, attn_bias, ln2_gain, ln2_bias, mlp_bias))
+    qm, k, v, kt, normed_one, stream_in, lse, att_own, IDS, W2, WO = front(
+        emb, trow, ids, segc, segr, par, wq, w_up, w_down, w_out
+    )
+    segc_own = lax.dynamic_slice_in_dim(segc, member * own_rows, own_rows, 0)
+    out, grad_mid, grad_attended, dw, dwo, vec = mid(att_own, stream_in, WO, W2, cotangent, segc_own, par)
+    pieces = lambda a: a.reshape(a.shape[:-2] + (ndp // 2, 2, D // ndp, a.shape[-1]))
+    input_grad, grad_token_table, g_up, g_down, g_out, g_qkv, SP = back(
+        grad_attended, qm, k, v, kt, lse, normed_one, wq, stream_in, grad_mid, segc, segr, par, vec, IDS, timesteps,
+        pieces(dw), pieces(dwo),
+    )
+    steps = SP[:, 7, 0].astype(jnp.int32)
+    grad_time_table = jnp.zeros(time_table.shape[:1] + (D,), F32)
+    at_row = jnp.arange(time_table.shape[0])[:, None]
+    for i in range(ndp):
+        grad_time_table = grad_time_table + jnp.where(at_row == steps[i], SP[i, 6][None], 0.0)
+    sums = jnp.sum(SP[:, :6], axis=0)
+    return (
+        out, input_grad, grad_token_table, grad_time_table, sums[0], sums[1],
+        g_qkv[:, :, :width].transpose(1, 0, 2), g_out[:, :width].T, sums[2], sums[3], sums[4], g_up, g_down.T,
+        sums[5],
+    )
+
+
 def solution(mesh):
     placed = (
         P("dp"),
@@ -891,9 +1357,8 @@
         P(("dp", "mp"), None),
     )
     ndp, nmp = mesh.shape["dp"], mesh.shape["mp"]
-    comm = Tuned if (ndp, nmp) == (8, 4) else Native(ndp, nmp)
     return jax.shard_map(
-        functools.partial(on_device, comm),
+        on_device_tuned if (ndp, nmp) == (8, 4) else functools.partial(on_device_native, Native(ndp, nmp)),
         mesh=mesh,
         in_specs=placed,
         out_specs=(

time: 433 us -> 257 us (0.59); the launches traced: 425 us -> 256 us
  matrix products: 68.9 us -> 0 us
  local copies, waits for them, and re-layouts: 65 us -> 31.3 us
  Pallas kernels: 244 us -> 211 us
  other arithmetic: 45 us -> 12.3 us
    dot_general x43 -> x0, matrix products: 68.9 us -> none  [the longest x11 27 us: dot(): return jnp.dot(a, b, preferred_element_type=F32)]
    pallas_call x5 -> x3, Pallas kernels: 244 us -> 211 us  [the longest x1 110 us: back(): pl.pallas_call(back_kernel, out_shape=(shape((256, D), F32), shape((1024,...]
    convert_element_type x5 -> x0, local copies, waits for them, and re-layouts: 10.5 us -> none  [the longest x1 5.41 us: on_device(): stream_all = tokens.astype(F32) + time_full]
    convert_element_type x10 -> x1, other arithmetic: 10.3 us -> 0.77 us  [on_device_tuned(): steps = SP[:, 7, 0].astype(jnp.int32)]
    slice x12 -> x3, local copies, waits for them, and re-layouts: 10.8 us -> 2.19 us  [the longest x1 1 us: on_device_tuned(): SP[i, 6][None]]
    another operation x3 -> x0, other arithmetic: 7.75 us -> none  [the longest x1 4.74 us: on_device(): dw = jnp.stack((jnp.stack(grads_up), jnp.stack(grads_down)))]
    reshape x10 -> x1, local copies, waits for them, and re-layouts: 8.79 us -> 1.71 us  [on_device_tuned(): segc, segr = (segment_ids.reshape(L, 1), segment_ids.reshape(1, L))]
    reduce_sum x12 -> x1, other arithmetic: 7.69 us -> 0.95 us  [on_device_tuned(): sums = jnp.sum(SP[:, :6], axis=0)]
where the time goes in v2:
time: 257 us; the launch traced here: 256 us
  Pallas kernels  211 us (82%)
  local copies, waits for them, and re-layouts  31.3 us (12%)
  other arithmetic  12.3 us (5%)
    pallas_call x1, Pallas kernels, back(): pl.pallas_call(back_kernel, out_shape=(shape((256, D), F32), shape((1024,...  110 us
    pallas_call x1, Pallas kernels, front(): pl.pallas_call(front_kernel, out_shape=(shape((3, L, 192), BF), shape((L,...  84 us
    pallas_call x1, Pallas kernels, mid(): pl.pallas_call(mid_kernel, grid=(4,), out_shape=(shape((256, D), BF), sha...  16.5 us
    unnamed x14, local copies, waits for them, and re-layouts  11.4 us
    gather x1, local copies, waits for them, and re-layouts, on_device_tuned(): emb = fold(token_table[token_ids])  6.19 us
    eq x4, other arithmetic, on_device_tuned(): at_row == steps[i]  5.19 us

profile of v2, /device:TPU:0, one launch (start us, length us, event | category | flops | bytes accessed | tf_op | source)
XLA Modules:
  0.0 255.9 jit_solution(4504236923688446104)
XLA Ops:
  0.6 0.0 copy-start
  1.4 0.8 dynamic-slice.3
  2.1 0.7 stack.21
  2.8 0.7 stack.22
  3.5 0.7 stack.23
  4.2 0.7 stack.24
  4.9 0.7 stack.25
  5.6 0.7 stack.26
  6.3 0.7 fusion
  7.0 0.6 stack.27.par
  7.6 0.0 copy-done
  7.6 0.1 constant_dynamic-slice_fusion
  7.7 0.1 pad_reduce_fusion
  7.8 0.6 broadcast_in_dim.126.trow
  8.4 0.8 copy.35.segc
  9.2 1.7 copy.34.segc
  10.9 5.9 %copy.33 = bf16[8192,192]{1,0:T(8,128)(2,1)} copy(bf16[8192,192]{0,1:T(8,128)(2,1)} %param.19) | data formatting | bytes 6291456 | tf_op args[3]
  16.8 6.2 %gather_fusion = bf16[1024,192]{1,0:T(8,128)(2,1)S(1)} fusion(bf16[8192,192]{1,0:T(8,128)(2,1)} %copy.33, s32[1024]{0:T(1024)S(1)} %fusion), kind=kCustom, calls=%fused_computation | custom fusion | bytes 790528 | tf_op jit(solution)/shard_map/gather | solution.py:1310
  23.1 0.9 pad_maximum_fusion.emb
  24.0 84.0 %front.1 = (bf16[3,1024,192]{2,1,0:T(8,128)(2,1)}, bf16[1024,192]{1,0:T(8,128)(2,1)}, bf16[1024,192]{1,0:T(8,128)(2,1)}, bf16[192,1024]{1,0:T(8,128)(2,1)}, bf16...) custom-call(bf16[512,384]{1,0:T(8,128)(2,1)} %pad_maximum_fusion.emb, ...), custom_call_target="tpu_custom_call" | custom-call | tf_op jit(solution)/shard_map/front/pallas_call | solution.py:435
  108.0 16.5 %mid.1 = (bf16[256,768]{1,0:T(8,128)(2,1)}, f32[256,768]{1,0:T(8,128)}, bf16[256,768]{1,0:T(8,128)(2,1)}, bf16[2,4,768,768]{3,2,1,0:T(8,128)(2,1)}, bf16[4,768,256]{2,1,0:T(8,128)(2,1)}, /*index=5*/f32[8,768]{1,0:T(8,128)}) custom-call(bf16[256,768]{1,0:T(8,128)(2,1)} %get-tuple-element.38.att, f32[256,768]{1,0:T(8,128)} %get-tuple-element.39.x, ...), custom_call_target="tpu_custom_call" | custom-call | tf_op jit(solution)/shard_map/mid/pallas_call | solution.py:557
  124.5 110.2 %back.1 = (f32[256,768]{1,0:T(8,128)}, f32[1024,192]{1,0:T(8,128)}, f32[96,768]{1,0:T(8,128)}, f32[96,768]{1,0:T(8,128)}, f32[96,256]{1,0:T(8,128)}, /*index=5*/f32[3,96,256]{2,1,0:T(8,128)}, f32[8,8,768]{2,1,0:T(8,128)}) custom-call(bf16[256,768]{1,0:T(8,128)(2,1)} %get-tuple-element.43.gatt, bf16[3,1024,192]{2,1,0:T(8,128)(2,1)} %get-tuple-element.44.qm, ...), custom_call_target="tpu_custom_call" | custom-call | tf_op jit(solution)/shard_map/back/pallas_call | solution.py:1046
  234.8 0.8 slice_convert_fusion
  235.5 0.5 fusion.2
  236.1 1.3 iota_compare_fusion.6
  237.4 1.3 iota_compare_fusion
  238.7 1.3 iota_compare_fusion.2
  240.0 1.3 iota_compare_fusion.4
  241.3 0.9 slice_reduce_fusion
  242.3 0.0 copy-start.1
  242.3 1.0 slice_reduce_fusion.14
  243.3 0.6 slice_reduce_fusion.1
  243.9 0.9 slice_bitcast_fusion.1
  244.8 0.7 copy.38
  245.6 1.7 slice_bitcast_fusion
  247.3 0.0 copy-start.3
  247.3 2.5 copy.37
  249.7 0.0 copy-start.2
  249.7 3.8 %select_add_fusion = f32[1000,768]{1,0:T(8,128)} fusion(f32[768]{0:T(1024)S(1)} %get-tuple-element.91, f32[768]{0:T(1024)S(1)} %get-tuple-element.92, f32[768]{0:T(1024)S(1)} %get-tuple-element.93, f32[768]{0:T(1024)S(1)} %get-tuple-element.94, f32[768]{0:T(1024)S(1)} %get-tuple-element.95, f32[768]{0:T(1024)S(1)} %get-tuple-element.96, ...), kind=kLoop, calls=%fused_computation.1 | loop fusion | flops 11520000 | bytes 3104576 | tf_op jit(solution)/shard_map/add | solution.py:1331
  253.6 0.0 copy-done.1
  253.6 0.9 copy.43
  254.5 0.0 copy-done.3
  254.5 0.7 copy.44
  255.2 0.0 copy-done.2
  255.2 0.7 copy.45
  (1 shorter events, 0.0 us)
Async XLA Ops:
  0.6 7.0 %copy-start = (bf16[1000,192]{0,1:T(8,128)(2,1)S(1)}, bf16[1000,192]{0,1:T(8,128)(2,1)}, u32[]{:S(2)}) copy-start(bf16[1000,192]{0,1:T(8,128)(2,1)} %param.20) | copy-start | bytes 1152004
  242.3 11.3 %copy-start.1 = (f32[256,768]{1,0:T(8,128)S(1)}, f32[256,768]{1,0:T(8,128)}, u32[]{:S(2)}) copy-start(f32[256,768]{1,0:T(8,128)} %get-tuple-element.137) | copy-start | bytes 2359300
  247.3 7.2 %copy-start.3 = (f32[96,768]{1,0:T(8,128)S(1)}, f32[96,768]{1,0:T(8,128)}, u32[]{:S(2)}) copy-start(f32[96,768]{1,0:T(8,128)} %get-tuple-element.147) | copy-start | bytes 884740
  249.7 5.5 %copy-start.2 = (f32[96,768]{1,0:T(8,128)S(1)}, f32[96,768]{1,0:T(8,128)}, u32[]{:S(2)}) copy-start(f32[96,768]{1,0:T(8,128)} %get-tuple-element.61) | copy-start | bytes 884740

commit v3 on v2

--- a/solution.py
+++ b/solution.py
@@ -92,10 +92,18 @@
 CH = 32
 
 
+def line_of(ref):
+    return ref[...].reshape(1, ref.shape[0])
+
+
+def across(row):
+    return jnp.broadcast_to(row, (128, row.shape[1])).T
+
+
 def allowed(segc, sq, b, c):
     key = CH * c + lax.broadcasted_iota(jnp.int32, (CH, 256), 0)
     query = 256 * b + lax.broadcasted_iota(jnp.int32, (CH, 256), 1)
-    return ((segc[CH * c : CH * c + CH, :] == sq) & (sq != 0)) | (key == query)
+    return ((segc[CH * c : CH * c + CH, :] == sq) & (sq != 0.0)) | (key == query)
 
 
 def lanes(b):
@@ -104,6 +112,13 @@
 
 def groups(x):
     return x.reshape(CH // 8, 8, 256)
+
+
+def write_segments(seg, segr, segc):
+    row = line_of(seg).astype(F32)
+    segr[...] = row
+    for i in range(8):
+        segc[128 * i : 128 * i + 128, :] = across(row[:, 128 * i : 128 * i + 128])[:, 0:1]
 
 
 class Weights:
@@ -233,83 +248,111 @@
 
 
 def front_kernel(
-    emb, trow, ids, segc, segr, par, wq, w_up, w_down, w_out,
-    qm_o, k_o, v_o, kt_o, n1_o, x_o, lse_o, att_o, IDS, W2, WO,
-    E, TR, vt, s, pb, ot, sendb, attg, own2, own_o,
+    ids, seg, step, ids8, tabt, timet, g1, b1, wq, w_up, w_down, w_out,
+    qm_o, k_o, v_o, kt_o, n1_o, x_o, lse_o, att_o, segr, segc, IDS, W2, WO,
+    tab, hot, eb, E, tb, TR, vt, s, pb, ot, sendb, attg, own2, own_o,
     es, er, ts, tr, is_, ir, zs, zr, ps, pr, as_, ar, ls,
 ):
     me = Place()
     p, j = me.p, me.j
-    meet([me.z(1), me.z(2), me.z(3)] + [me.at((p + k) % 8) for k in range(1, 8)])
-    w = Weights(me, (own2.at[0], own2.at[1], own_o), W2, WO, zs, zr, ps, pr)
-
-    def ecopy(d, k):
-        q = w.quarter(d, k)
-        return (emb if k == 0 else E.at[q], E.at[q], es.at[d, k], er.at[d, k], me.z(1 if d == 0 else 3))
-
-    def estart(k):
-        for d in (0, 1):
-
-            @pl.when(w.sends(d, k))
-            def _():
-                push(*ecopy(d, k)).start()
-
-    def ewait(k):
-        for d in (0, 1):
-
-            @pl.when(w.gets(d, k))
-            def _():
-                dst = E.at[w.quarter(d, k + 1)]
-                push(dst, dst, es.at[d, k], er.at[d, k], me.z(1)).wait_recv()
-
-    here = [
-        pltpu.make_async_copy(emb, E.at[j], ls.at[0]),
-        pltpu.make_async_copy(trow, TR.at[j], ls.at[1]),
-        pltpu.make_async_copy(ids, IDS.at[p], ls.at[2]),
-    ]
+    fetch = pltpu.make_async_copy(tabt, tab, ls.at[0])
+    fetch.start()
     load = [
         pltpu.make_async_copy(w_up, own2.at[0], ls.at[3]),
         pltpu.make_async_copy(w_down, own2.at[1], ls.at[4]),
         pltpu.make_async_copy(w_out, own_o, ls.at[5]),
     ]
+    for c in load:
+        c.start()
+    write_segments(seg, segr, segc)
+    lane = lax.broadcasted_iota(jnp.int32, (192, 1000), 1)
+    column = jnp.sum(jnp.where(lane == step[0], timet[...].astype(F32), 0.0), axis=1, keepdims=True)
+    tb[:, 0:192] = jnp.broadcast_to(column, (192, 128)).T[0:16, :].astype(BF)
+    meet([me.z(1), me.z(2), me.z(3)] + [me.at((p + k) % 8) for k in range(1, 8)])
+    w = Weights(me, (own2.at[0], own2.at[1], own_o), W2, WO, zs, zr, ps, pr)
+
+    def ecopy(d, k, c):
+        q = w.quarter(d, k)
+        dev = me.z(1 if d == 0 else 3)
+        return push(eb.at[c] if k == 0 else E.at[q, c], E.at[q, c], es.at[d, k, c], er.at[d, k, c], dev)
+
+    def estart(k, c):
+        for d in (0, 1):
+
+            @pl.when(w.sends(d, k))
+            def _():
+                ecopy(d, k, c).start()
+
+    def ewait(k, c):
+        for d in (0, 1):
+
+            @pl.when(w.gets(d, k))
+            def _():
+                dst = E.at[w.quarter(d, k + 1), c]
+                push(dst, dst, es.at[d, k, c], er.at[d, k, c], me.z(1)).wait_recv()
+
+    here = [pltpu.make_async_copy(ids8, IDS.at[p], ls.at[2])]
     keep = [
         pltpu.make_async_copy(own2, W2.at[j], ls.at[3]),
         pltpu.make_async_copy(own_o, WO.at[pl.ds(192 * j, 192), :], ls.at[5]),
     ]
-    small = [push(trow, TR.at[j], ts.at[k - 1], tr.at[k - 1], me.z(k)) for k in (1, 2, 3)]
-    small_ids = [push(ids, IDS.at[p], is_.at[k - 1], ir.at[k - 1], me.at((p + k) % 8)) for k in range(1, 8)]
-
-    estart(0)
-    for c in load + small + here + small_ids:
-        c.start()
+    small = [push(tb, TR.at[j], ts.at[k - 1], tr.at[k - 1], me.z(k)) for k in (1, 2, 3)]
+    small_ids = [push(ids8, IDS.at[p], is_.at[k - 1], ir.at[k - 1], me.at((p + k) % 8)) for k in range(1, 8)]
+    ids_row = line_of(ids).astype(F32)
+
+    def embed(c):
+        token = across(ids_row[:, 256 * c : 256 * c + 256])
+        s[0, 0:256, 0:192] = jnp.zeros((256, 192), F32)
+
+        @pl.loop(0, 4)
+        def _(v):
+            base = (2048 * v).astype(F32)
+            for i in range(16):
+                word = lax.broadcasted_iota(jnp.int32, (256, 128), 1).astype(F32) + (base + 128.0 * i)
+                hot[:, 128 * i : 128 * i + 128] = (token == word).astype(F32).astype(BF)
+            s[0, 0:256, 0:192] += contract_cols(hot[...], tab[:, pl.ds(pl.multiple_of(2048 * v, 2048), 2048)])
+
+        eb[c] = fold(s[0, 0:256, 0:192].astype(BF))
+        estart(0, c)
+
+    fetch.wait()
     for c in load:
         c.wait()
-    for c in keep:
+    w.zstart(0, (0,))
+    embed(0)
+    for c in small + here + small_ids + keep:
         c.start()
-    w.zstart(0, (0,))
-    ewait(0)
-    estart(1)
+    embed(1)
+    embed(2)
+    ewait(0, 0)
+    estart(1, 0)
+    embed(3)
     w.zstart(0, (1,))
-    ewait(1)
-    estart(2)
+    ewait(0, 1)
+    estart(1, 1)
+    ewait(0, 2)
+    estart(1, 2)
+    ewait(1, 0)
+    estart(2, 0)
+    ewait(0, 3)
+    estart(1, 3)
+    ewait(1, 1)
+    estart(2, 1)
+    w.zwait(0, (0,))
     w.zstart(0, (2,))
-    w.zwait(0, (0,))
+    ewait(1, 2)
+    estart(2, 2)
     w.zstart(1, (0,))
-    w.zwait(0, (1, 2))
-    w.zstart(1, (1, 2))
-    w.pstart(0, 0)
-    ewait(2)
     for c in small:
         c.wait()
-    here[0].wait()
-    here[1].wait()
-
+    E[j] = eb[...]
+    TR[j] = tb[...]
     time_row = jnp.concatenate([TR[q].astype(F32)[0:1, 0:192] for q in range(4)], axis=1)
-    gain, shift = par[0:1, :], par[1:2, :]
-    for r in range(4):
-        h, o = r // 2, 256 * (r % 2)
+    gain, shift = line_of(g1), line_of(b1)
+
+    def norm_qkv(r):
         rows = slice(256 * r, 256 * r + 256)
-        x = jnp.concatenate([E[q, o : o + 256, 192 * h : 192 * h + 192] for q in range(4)], axis=1)
+        x = jnp.concatenate([unfold(E[q, r]) for q in range(4)], axis=1)
         x = x.astype(F32) + time_row
         centered = x - jnp.mean(x, axis=1, keepdims=True)
         variance = jnp.mean(centered * centered, axis=1, keepdims=True)
@@ -327,6 +370,20 @@
         v_o[rows, :] = contract_cols(normed, wq[384:576, :]).astype(BF)
         kt_o[:, rows] = contract_cols(wq[192:384, :], normed).astype(BF)
         vt[:, rows] = contract_cols(wq[384:576, :], normed).astype(BF)
+
+    ewait(2, 0)
+    norm_qkv(0)
+    ewait(1, 3)
+    estart(2, 3)
+    w.zwait(0, (1, 2))
+    w.zstart(1, (1, 2))
+    w.pstart(0, 0)
+    ewait(2, 1)
+    norm_qkv(1)
+    ewait(2, 2)
+    norm_qkv(2)
+    ewait(2, 3)
+    norm_qkv(3)
 
     def att_copy(b):
         return push(sendb.at[b], attg.at[j], as_.at[b], ar.at[j], (p, b))
@@ -424,14 +481,15 @@
 
             @pl.when(w.sends(d, k))
             def _():
-                push(*ecopy(d, k)).wait_send()
+                for c in range(4):
+                    ecopy(d, k, c).wait_send()
 
     w.finish()
-    for c in small_ids + here[2:] + keep:
+    for c in small_ids + here + keep:
         c.wait()
 
 
-def front(emb, trow, ids, segc, segr, par, wq, w_up, w_down, w_out):
+def front(ids, seg, step, ids8, tabt, timet, g1, b1, wq, w_up, w_down, w_out):
     return pl.pallas_call(
         front_kernel,
         out_shape=(
@@ -443,14 +501,20 @@
             shape((256, D), F32),
             shape((12, 1, 256), F32),
             shape((256, D), BF),
+            shape((1, L), F32),
+            shape((L, 1), F32),
             shape((8, 8, 128), jnp.int32),
             shape((4, 2, D, D), BF),
             shape((D, D), BF),
         ),
-        in_specs=[ANY] * 3 + [VM] * 4 + [ANY] * 3,
-        out_specs=(VM,) * 8 + (ANY,) * 3,
+        in_specs=[VM] * 2 + [pl.BlockSpec(memory_space=pltpu.SMEM)] + [ANY] * 2 + [VM] * 4 + [ANY] * 3,
+        out_specs=(VM,) * 10 + (ANY,) * 3,
         scratch_shapes=[
-            pltpu.VMEM((4, 512, 384), BF),
+            pltpu.VMEM((192, 8192), BF),
+            pltpu.VMEM((256, 2048), BF),
+            pltpu.VMEM((4, 128, 384), BF),
+            pltpu.VMEM((4, 4, 128, 384), BF),
+            pltpu.VMEM((16, 256), BF),
             pltpu.VMEM((4, 16, 256), BF),
             pltpu.VMEM((192, L), BF),
             pltpu.VMEM((3, L, 256), F32),
@@ -460,8 +524,8 @@
             pltpu.VMEM((4, 128, 384), BF),
             pltpu.VMEM((2, D, D), BF),
             pltpu.VMEM((192, D), BF),
-            DMA((2, 3)),
-            DMA((2, 3)),
+            DMA((2, 3, 4)),
+            DMA((2, 3, 4)),
             DMA((3,)),
             DMA((3,)),
             DMA((7,)),
@@ -476,7 +540,7 @@
         ],
         compiler_params=params(0),
         name="front",
-    )(emb, trow, ids, segc, segr, par, wq, w_up, w_down, w_out)
+    )(ids, seg, step, ids8, tabt, timet, g1, b1, wq, w_up, w_down, w_out)
 
 
 def norm_stats(x):
@@ -495,27 +559,32 @@
 
 
 def mid_kernel(
-    att, x, wo, w2, cot, segc, par,
+    att, x, wo, w2, cot, segr, pa, pg, pb, pm,
     out_o, gmid_o, gatt_o, dw_o, dwo_o, vec_o,
     sm, hat, sc, n2, n2t, gmt, gm, acc, gn2,
 ):
     q = pl.program_id(0)
+    own = pl.ds(pl.multiple_of(256 * lax.axis_index("mp"), 256), 256)
+
+    def masked():
+        valid = across((segr[:, own] != 0.0).astype(F32))[:, 0:1]
+        return cot[...].astype(F32) * valid
+
 
     @pl.when(q == 0)
     def _():
-        mid = x[...] + dot(att[...], wo[...]) + par[2:3, :]
+        mid = x[...] + dot(att[...], wo[...]) + line_of(pa)
         sm[...] = mid
         h, scale = norm_stats(mid)
         hat[...] = h
         sc[...] = scale
-        normed = (h * par[3:4, :] + par[4:5, :]).astype(BF)
+        normed = (h * line_of(pg) + line_of(pb)).astype(BF)
         n2[...] = normed
         n2t[...] = normed.astype(F32).T.astype(BF)
-        valid = (segc[...] != 0).astype(F32)
-        grad = cot[...].astype(F32) * valid
+        grad = masked()
         gm[...] = grad.astype(BF)
         gmt[...] = grad.T.astype(BF)
-        acc[...] = mid + par[5:6, :]
+        acc[...] = mid + line_of(pm)
         gn2[...] = jnp.zeros_like(gn2)
 
     up, down = w2[0, 0], w2[0, 1]
@@ -534,9 +603,9 @@
     @pl.when(q == 3)
     def _():
         out_o[...] = acc[...].astype(BF)
-        grad = cot[...].astype(F32) * (segc[...] != 0).astype(F32)
+        grad = masked()
         gn, h = gn2[...], hat[...]
-        gmid = grad + norm_back(gn, par[3:4, :], h, sc[...])
+        gmid = grad + norm_back(gn, line_of(pg), h, sc[...])
         gmid_o[...] = gmid
         vec_o[...] = jnp.zeros_like(vec_o)
         vec_o[2:3, :] = rows_sum(gmid)
@@ -551,7 +620,7 @@
             dwo_o[i, :, 192:256] = jnp.zeros((D, 64), BF)
 
 
-def mid(att, x, wo, w2, cot, segc, par):
+def mid(att, x, wo, w2, cot, segr, pa, pg, pb, pm):
     whole = lambda a: pl.BlockSpec(a.shape, lambda q: (0,) * a.ndim)
     keep = lambda *dims: pl.BlockSpec(dims, lambda q: (0,) * len(dims))
     return pl.pallas_call(
@@ -571,8 +640,11 @@
             whole(wo),
             pl.BlockSpec((1, 2, D, D), lambda q: (q, 0, 0, 0)),
             whole(cot),
-            whole(segc),
-            whole(par),
+            whole(segr),
+            whole(pa),
+            whole(pg),
+            whole(pb),
+            whole(pm),
         ],
         out_specs=(
             keep(256, D),
@@ -595,7 +667,7 @@
         ],
         compiler_params=pltpu.CompilerParams(vmem_limit_bytes=60 << 20, dimension_semantics=("arbitrary",)),
         name="mid",
-    )(att, x, wo, w2, cot, segc, par)
+    )(att, x, wo, w2, cot, segr, pa, pg, pb, pm)
 
 
 class Line:
@@ -748,8 +820,8 @@
 
 
 def back_kernel(
-    gatt, qm, k, v, kt, lse, n1, wq, x, gmid, segc, segr, par, vec, IDS, step, dw, dwo,
-    o_in, o_tok, o_up, o_down, o_out, o_qkv, o_sp,
+    gatt, qm, k, v, kt, lse, n1, wq, x, gmid, segc, segr, g1, vec, IDS, step, dw, dwo,
+    h_in, h_tok, h_up, h_down, h_out, h_qkv, h_sp,
     *scratch,
 ):
     me = Place()
@@ -758,6 +830,7 @@
     it = iter(scratch)
     take = lambda n: [next(it) for _ in range(n)]
     sendb, gbuf, dom, s, dp, pb, dsb, dqt, dqn, dk, dv, gn = take(12)
+    o_in, o_tok, o_up, o_down, o_out, o_qkv, o_sp, hs = take(8)
     as_, ar = take(2)
     gacc, gup, gdown, gsem = take(4)
     qk, tb, X, hot, vbuf, SZ, vs = take(7)
@@ -773,6 +846,13 @@
             lines.append(Line(me, unit.own, up, down, sem))
     own = Line(me, lambda q: gacc.at[q], gup, gdown, gsem)
 
+    homes = [
+        pltpu.make_async_copy(src, dst, hs.at[i])
+        for i, (src, dst) in enumerate(
+            ((o_in, h_in), (o_tok, h_tok), (o_up, h_up), (o_down, h_down), (o_out, h_out), (o_qkv, h_qkv), (o_sp, h_sp))
+        )
+    ]
+
     def to_heads(d):
         return push(sendb.at[d], gbuf.at[j], as_.at[d], ar.at[j], (p, d))
 
@@ -794,16 +874,13 @@
         units[0].cross()
 
     def step1():
+        units[2].chip()
+        units[2].cross()
+
+    def step2():
         units[1].chip()
 
-    def step2():
-        units[2].chip()
-
-    def step3():
-        units[0].turn()
-        units[1].cross()
-
-    steps = {0: step0, 1: step1, 2: step2, 11: step3}
+    steps = {0: step0, 2: step1, 4: step2}
 
     def slot(i, n):
         for c, fn in {c: fn for c, fn in steps.items() if c % 3 == n}.items():
@@ -856,6 +933,9 @@
         gacc[q] = (total + dot(dv[rows, :].astype(BF), wq[384:576, :])).astype(BF)
         for block, d in starts:
             own.end(block, d)
+    units[0].turn()
+    units[2].turn()
+    units[1].cross()
     for i, grad in enumerate((dqn[...], dk[...].astype(BF), dv[...].astype(BF))):
         full = contract_rows(n1[...], grad).astype(BF)
         for piece in range(8):
@@ -864,18 +944,20 @@
     units[3].begin()
     own.inner(NEAR)
     units[3].chip()
+    units[3].cross()
     units[0].settle()
+    lines[0].first()
     own.inner(FAR)
+    units[2].settle()
     units[1].turn()
-    units[2].cross()
-    units[3].cross()
+    units[3].turn()
     own.finish(gn)
-    lines[0].first()
 
     hat, scale = norm_stats(x[...])
     grad = gn[...]
-    dx = gmid[...] + norm_back(grad, par[0:1, :], hat, scale)
+    dx = gmid[...] + norm_back(grad, line_of(g1), hat, scale)
     o_in[...] = dx
+    homes[0].start()
     dxb = dx.astype(BF)
 
     def to_columns(d):
@@ -899,31 +981,9 @@
     for c in small:
         c.start()
     SZ[j] = vbuf[...]
-    units[1].settle()
-    lines[1].first()
-    lines[0].inner(NEAR)
-    for c in small:
-        c.wait()
-    vs[...] = SZ[0] + SZ[1] + SZ[2] + SZ[3]
-    out_v = [push(vs, o_sp.at[p], vps.at[i - 1], vpr.at[i - 1], me.at((p + i) % 8)) for i in range(1, 8)]
-    for c in out_v:
-        c.start()
-    o_sp[p] = vs[...]
-
-    for q in range(4):
-
-        @pl.when(j != q)
-        def _():
-            push(X.at[p, q], X.at[p, q], ts.at[q], tr.at[q], me.z(1)).wait_recv()
-
-    half = (pl.ds(0, 2), pl.ds(2, 2))
-
-    def to(ref, i, dev):
+
+    def hop(ref, i, dev):
         return push(ref, ref, ps.at[i], pr.at[i], me.at(dev))
-
-    first_hop = [to(X.at[p], 0, me.px), to(X.at[p], 1, me.py), to(X.at[p], 2, me.pc)]
-    for c in first_hop:
-        c.start()
 
     def table(d, start=False):
         vocab = 1024 * p + lax.broadcasted_iota(jnp.int32, (1024, 128), 0)
@@ -936,52 +996,103 @@
         else:
             o_tok[...] += part
 
+    sent = []
     here = me.pc - p
+
+    def spread(i):
+        q = (j + i) % 4
+        if i > 0:
+            push(X.at[p, q], X.at[p, q], ts.at[q], tr.at[q], me.z(1)).wait_recv()
+        for c in (hop(X.at[p, q], 2 * q, me.px), hop(X.at[p, q], 2 * q + 1, me.py)):
+            c.start()
+            sent.append(c)
+
+    def on_x(q):
+        return hop(X.at[me.py, q], 8 + q, me.px)
+
+    def on_y(q):
+        return hop(X.at[me.px, q], 8 + q, me.py)
+
+    def corner(i):
+        q = (j + i) % 4
+        hop(X.at[me.px, q], 2 * q, me.px).wait_recv()
+        hop(X.at[me.py, q], 2 * q + 1, me.py).wait_recv()
+
+        @pl.when(q < 2)
+        def _():
+            on_x(q).start()
+
+        @pl.when(q >= 2)
+        def _():
+            on_y(q).start()
+
+    def to_core(d, i):
+        c = hop(X.at[d], i, me.pc)
+        c.start()
+        sent.append(c)
+
+    spread(0)
+    lines[0].inner(NEAR)
+    units[1].settle()
+    lines[1].first()
+    spread(1)
+    spread(3)
+    lines[2].first()
+    corner(0)
+    for c in small:
+        c.wait()
+    vs[...] = SZ[0] + SZ[1] + SZ[2] + SZ[3]
+    out_v = [push(vs, o_sp.at[p], vps.at[i - 1], vpr.at[i - 1], me.at((p + i) % 8)) for i in range(1, 8)]
+    for c in out_v:
+        c.start()
+    o_sp[p] = vs[...]
+    lines[0].inner(FAR)
+    spread(2)
+    to_core(p, 12)
+    corner(1)
+    corner(3)
     table(p, start=True)
-    to(X.at[me.pc], 2, me.pc).wait_recv()
-    to(X.at[me.px], 0, me.px).wait_recv()
-    to(X.at[me.py], 1, me.py).wait_recv()
-    second = [
-        to(X.at[me.py, half[0]], 3, me.px),
-        to(X.at[me.px, half[1]], 4, me.py),
-        to(X.at[me.px], 5, me.pc),
-        to(X.at[me.py], 6, me.pc),
-    ]
-    for c in second:
-        c.start()
+    lines[1].inner(NEAR)
+    corner(2)
+    to_core(me.px, 13)
+    to_core(me.py, 14)
+    units[3].settle()
+    lines[2].inner(NEAR)
+    hop(X.at[me.pc], 12, me.pc).wait_recv()
     table(me.pc)
-    units[2].turn()
-    units[3].turn()
+    lines[1].inner(FAR)
     table(me.px)
-    lines[0].inner(FAR)
-    lines[1].inner(NEAR)
+    for q in range(4):
+        hop(X.at[me.pd, q], 8 + q, me.px).wait_recv()
+    to_core(me.pd, 15)
+    lines[2].inner(FAR)
     table(me.py)
-    to(X.at[me.pd, half[0]], 3, me.px).wait_recv()
-    to(X.at[me.pd, half[1]], 4, me.px).wait_recv()
-    third = to(X.at[me.pd], 7, me.pc)
-    third.start()
-    units[2].settle()
-    lines[2].first()
-    units[3].settle()
     table(me.pd)
-    to(X.at[me.px + here], 5, me.pc).wait_recv()
+    hop(X.at[me.px + here], 13, me.pc).wait_recv()
     table(me.px + here)
-    lines[1].inner(FAR)
-    lines[2].inner(NEAR)
-    to(X.at[me.py + here], 6, me.pc).wait_recv()
+    hop(X.at[me.py + here], 14, me.pc).wait_recv()
     table(me.py + here)
-    lines[2].inner(FAR)
-    to(X.at[me.pd + here], 7, me.pc).wait_recv()
+    hop(X.at[me.pd + here], 15, me.pc).wait_recv()
     table(me.pd + here)
+    homes[1].start()
     lines[0].finish(o_down)
+    homes[3].start()
+    lines[2].finish(o_out)
+    homes[4].start()
     lines[1].finish(o_up)
-    lines[2].finish(o_out)
+    homes[2].start()
     for i in range(3):
         o_qkv[i] = units[3].acc[i, me.m].astype(F32)
+    homes[5].start()
     for c in out_v:
         c.wait()
-    for c in first_hop + second + [third]:
+    homes[6].start()
+    for c in homes:
+        c.wait()
+    for c in sent:
         c.wait_send()
+    for q in range(4):
+        on_x(q).wait_send() if q < 2 else on_y(q).wait_send()
     for d in range(4):
 
         @pl.when(j != d)
@@ -993,7 +1104,7 @@
         line.close()
 
 
-def back(gatt, qm, k, v, kt, lse, n1, wq, x, gmid, segc, segr, par, vec, ids, step, dw, dwo):
+def back(gatt, qm, k, v, kt, lse, n1, wq, x, gmid, segc, segr, g1, vec, ids, step, dw, dwo):
     scratch = [
         pltpu.VMEM((4, 128, 384), BF),
         pltpu.VMEM((4, 128, 384), BF),
@@ -1007,6 +1118,14 @@
         pltpu.VMEM((L, 192), F32),
         pltpu.VMEM((L, 192), F32),
         pltpu.VMEM((256, D), F32),
+        pltpu.VMEM((256, D), F32),
+        pltpu.VMEM((1024, 192), F32),
+        pltpu.VMEM((96, D), F32),
+        pltpu.VMEM((96, D), F32),
+        pltpu.VMEM((96, 256), F32),
+        pltpu.VMEM((3, 96, 256), F32),
+        pltpu.VMEM((8, 8, D), F32),
+        DMA((7,)),
         DMA((4,)),
         DMA((4,)),
         pltpu.VMEM((4, 256, D), BF),
@@ -1024,8 +1143,8 @@
         DMA((3,)),
         DMA((4,)),
         DMA((4,)),
-        DMA((8,)),
-        DMA((8,)),
+        DMA((16,)),
+        DMA((16,)),
         DMA((7,)),
         DMA((7,)),
         DMA((2,)),
@@ -1055,11 +1174,57 @@
             shape((8, 8, D), F32),
         ),
         in_specs=[VM] * 15 + [pl.BlockSpec(memory_space=pltpu.SMEM)] + [ANY] * 2,
-        out_specs=(VM,) * 7,
+        out_specs=(ANY,) * 7,
         scratch_shapes=scratch,
         compiler_params=params(1),
         name="back",
-    )(gatt, qm, k, v, kt, lse, n1, wq, x, gmid, segc, segr, par, vec, ids, step, dw, dwo)
+    )(gatt, qm, k, v, kt, lse, n1, wq, x, gmid, segc, segr, g1, vec, ids, step, dw, dwo)
+
+
+def tail_kernel(sp, din, tok, up, down, wout, qkv, *outs):
+    o_time, o_din, o_tok, o_up, o_down, o_out, o_qkv = outs[:7]
+    i = pl.program_id(0)
+    row = (200 * i + lax.broadcasted_iota(jnp.int32, (200, D), 0)).astype(F32)
+    total = jnp.zeros((200, D), F32)
+    for d in range(8):
+        total = total + jnp.where(row == sp[d, 7:8, :], sp[d, 6:7, :], 0.0)
+    o_time[...] = total
+
+    @pl.when(i == 0)
+    def _():
+        sums = sp[0]
+        for d in range(1, 8):
+            sums = sums + sp[d]
+        for n, ref in enumerate(outs[7:]):
+            ref[...] = sums[n : n + 1, :].reshape(D)
+        o_din[...] = din[...]
+        o_tok[...] = tok[...].T
+        o_up[...] = up[...]
+        o_down[...] = down[...]
+        o_out[...] = wout[...].T[0:192, :]
+        o_qkv[...] = qkv[:, :, 0:192]
+
+
+def tail(*args):
+    whole = lambda a: pl.BlockSpec(a.shape, lambda i: (0,) * len(a.shape))
+    outs = (
+        shape((256, D), F32),
+        shape((192, 1024), F32),
+        shape((96, D), F32),
+        shape((96, D), F32),
+        shape((192, 96), F32),
+        shape((3, 96, 192), F32),
+    ) + (shape((D,), F32),) * 6
+    return pl.pallas_call(
+        tail_kernel,
+        grid=(5,),
+        out_shape=(shape((1000, D), F32),) + outs,
+        in_specs=[whole(a) for a in args],
+        out_specs=(pl.BlockSpec((200, D), lambda i: (i, 0)),) + tuple(whole(a) for a in outs),
+        compiler_params=pltpu.CompilerParams(vmem_limit_bytes=63 << 20, dimension_semantics=("arbitrary",)),
+        name="tail",
+    )(*args)
+
 
 class Native:
     def __init__(self, ndp, nmp):
@@ -1304,36 +1469,26 @@
     token_ids, segment_ids, timesteps, token_table, time_table, ln1_gain, ln1_bias, w_qkv, w_out, attn_bias,
     ln2_gain, ln2_bias, w_up, w_down, mlp_bias, cotangent,
 ):
-    group, ndp = 4, 8
-    member = lax.axis_index("mp")
-    own_rows, width = 256, 192
-    emb = fold(token_table[token_ids])
-    time_row = lax.dynamic_slice_in_dim(time_table, timesteps[0], 1, 0)
-    trow = jnp.broadcast_to(jnp.pad(time_row, ((0, 0), (0, 256 - width))), (16, 256))
-    ids = token_ids.reshape(8, 128)
+    ndp, width = 8, 192
+    ids8 = token_ids.reshape(8, 128)
     wq = w_qkv.transpose(1, 2, 0).reshape(3 * width, D)
-    segc, segr = segment_ids.reshape(L, 1), segment_ids.reshape(1, L)
-    par = jnp.stack((ln1_gain, ln1_bias, attn_bias, ln2_gain, ln2_bias, mlp_bias))
-    qm, k, v, kt, normed_one, stream_in, lse, att_own, IDS, W2, WO = front(
-        emb, trow, ids, segc, segr, par, wq, w_up, w_down, w_out
+    qm, k, v, kt, normed_one, stream_in, lse, att_own, segr, segc, IDS, W2, WO = front(
+        token_ids, segment_ids, timesteps, ids8, token_table.T, time_table.T, ln1_gain, ln1_bias, wq, w_up, w_down, w_out
     )
-    segc_own = lax.dynamic_slice_in_dim(segc, member * own_rows, own_rows, 0)
-    out, grad_mid, grad_attended, dw, dwo, vec = mid(att_own, stream_in, WO, W2, cotangent, segc_own, par)
+    out, grad_mid, grad_attended, dw, dwo, vec = mid(
+        att_own, stream_in, WO, W2, cotangent, segr, attn_bias, ln2_gain, ln2_bias, mlp_bias
+    )
     pieces = lambda a: a.reshape(a.shape[:-2] + (ndp // 2, 2, D // ndp, a.shape[-1]))
     input_grad, grad_token_table, g_up, g_down, g_out, g_qkv, SP = back(
-        grad_attended, qm, k, v, kt, lse, normed_one, wq, stream_in, grad_mid, segc, segr, par, vec, IDS, timesteps,
+        grad_attended, qm, k, v, kt, lse, normed_one, wq, stream_in, grad_mid, segc, segr, ln1_gain, vec, IDS, timesteps,
         pieces(dw), pieces(dwo),
     )
-    steps = SP[:, 7, 0].astype(jnp.int32)
-    grad_time_table = jnp.zeros(time_table.shape[:1] + (D,), F32)
-    at_row = jnp.arange(time_table.shape[0])[:, None]
-    for i in range(ndp):
-        grad_time_table = grad_time_table + jnp.where(at_row == steps[i], SP[i, 6][None], 0.0)
-    sums = jnp.sum(SP[:, :6], axis=0)
+    o_time, o_in, o_tok, o_up, o_down, o_out, o_qkv, *sums = tail(
+        SP, input_grad, grad_token_table, g_up, g_down, g_out, g_qkv
+    )
     return (
-        out, input_grad, grad_token_table, grad_time_table, sums[0], sums[1],
-        g_qkv[:, :, :width].transpose(1, 0, 2), g_out[:, :width].T, sums[2], sums[3], sums[4], g_up, g_down.T,
-        sums[5],
+        out, o_in, o_tok.T, o_time, sums[0], sums[1], o_qkv.transpose(1, 0, 2), o_out, sums[2], sums[3], sums[4],
+        o_up, o_down.T, sums[5],
     )
 
 

time: 257 us -> 202 us (0.79)
  local copies, waits for them, and re-layouts: 31.3 us -> 0 us
  other arithmetic: 12.3 us -> 0 us
  Pallas kernels: 211 us -> 199 us
    pallas_call x1, Pallas kernels: 110 us -> 92.4 us  [back(): pl.pallas_call(back_kernel, out_shape=(shape((256, D), F32), shape((1024,...]
    unnamed x14 -> x0, local copies, waits for them, and re-layouts: 11.4 us -> none
    pallas_call x0 -> x1, Pallas kernels: none -> 7.04 us  [tail(): pl.pallas_call(tail_kernel, grid=(5,), out_shape=(shape((1000, D), F32),)...]
    gather x1 -> x0, local copies, waits for them, and re-layouts: 6.19 us -> none  [on_device_tuned(): emb = fold(token_table[token_ids])]
    another operation x8 -> x0, local copies, waits for them, and re-layouts: 5.54 us -> none  [the longest x7 4.77 us: on_device_tuned(): jnp.stack((ln1_gain, ln1_bias, attn_bias, ln2_gain, ln2_bias, mlp_bias))]
    eq x4 -> x0, other arithmetic: 5.19 us -> none  [on_device_tuned(): at_row == steps[i]]
    add x1 -> x0, other arithmetic: 3.85 us -> none  [on_device_tuned(): grad_time_table + jnp.where(at_row == steps[i], SP[i, 6][None], 0.0)]
    transpose x2 -> x0, local copies, waits for them, and re-layouts: 2.59 us -> none  [the longest x1 1.69 us: on_device_tuned(): g_qkv[:, :, :width].transpose(1, 0, 2)]
where the time goes in v3:
time: 202 us; the launch traced here: 201 us
  Pallas kernels  199 us (99%)
    pallas_call x1, Pallas kernels, back(): pl.pallas_call(back_kernel, out_shape=(shape((256, D), F32), shape((1024,...  92.4 us
    pallas_call x1, Pallas kernels, front(): pl.pallas_call(front_kernel, out_shape=(shape((3, L, 192), BF), shape((L,...  83.3 us
    pallas_call x1, Pallas kernels, mid(): pl.pallas_call(mid_kernel, grid=(4,), out_shape=(shape((256, D), BF), sha...  16.6 us
    pallas_call x1, Pallas kernels, tail(): pl.pallas_call(tail_kernel, grid=(5,), out_shape=(shape((1000, D), F32),)...  7.04 us

profile of v3, /device:TPU:0, one launch (start us, length us, event | category | flops | bytes accessed | tf_op | source)
XLA Modules:
  0.0 200.9 jit_solution(4534517570646763908)
XLA Ops:
  1.3 83.3 %front.1 = (bf16[3,1024,192]{2,1,0:T(8,128)(2,1)}, bf16[1024,192]{1,0:T(8,128)(2,1)}, bf16[1024,192]{1,0:T(8,128)(2,1)}, bf16[192,1024]{1,0:T(8,128)(2,1)}, bf16...) custom-call(s32[1024]{0:T(1024)} %ids.1, ...), custom_call_target="tpu_custom_call" | custom-call | tf_op jit(solution)/shard_map/front/pallas_call | solution.py:493
  84.6 16.6 %mid.1 = (bf16[256,768]{1,0:T(8,128)(2,1)}, f32[256,768]{1,0:T(8,128)}, bf16[256,768]{1,0:T(8,128)(2,1)}, bf16[2,4,768,768]{3,2,1,0:T(8,128)(2,1)}, bf16[4,768,256]{2,1,0:T(8,128)(2,1)}, /*index=5*/f32[8,768]{1,0:T(8,128)}) custom-call(bf16[256,768]{1,0:T(8,128)(2,1)} %get-tuple-element.53.att, f32[256,768]{1,0:T(8,128)} %get-tuple-element.54.x, ...), custom_call_target="tpu_custom_call" | custom-call | tf_op jit(solution)/shard_map/mid/pallas_call | solution.py:626
  101.3 92.4 %back.1 = (f32[256,768]{1,0:T(8,128)}, f32[1024,192]{1,0:T(8,128)}, f32[96,768]{1,0:T(8,128)}, f32[96,768]{1,0:T(8,128)}, f32[96,256]{1,0:T(8,128)}, /*index=5*/f32[3,96,256]{2,1,0:T(8,128)}, f32[8,8,768]{2,1,0:T(8,128)}) custom-call(bf16[256,768]{1,0:T(8,128)(2,1)} %get-tuple-element.59.gatt, bf16[3,1024,192]{2,1,0:T(8,128)(2,1)} %get-tuple-element.60.qm, ...), custom_call_target="tpu_custom_call" | custom-call | tf_op jit(solution)/shard_map/back/pallas_call | solution.py:1165
  193.7 7.0 %tail.1 = (f32[1000,768]{1,0:T(8,128)}, f32[256,768]{1,0:T(8,128)}, f32[192,1024]{1,0:T(8,128)}, f32[96,768]{1,0:T(8,128)}, f32[96,768]{1,0:T(8,128)}, /*index=5...) custom-call(f32[8,8,768]{2,1,0:T(8,128)} %get-tuple-element.72.sp, ...), custom_call_target="tpu_custom_call" | custom-call | tf_op jit(solution)/shard_map/tail/pallas_call | solution.py:1218

commit v4 on v3

--- a/solution.py
+++ b/solution.py
@@ -122,23 +122,19 @@
 
 
 class Weights:
-    def __init__(self, me, shards, W2, WO, zs, zr, ps, pr):
-        self.me, self.shards, self.W2, self.WO = me, shards, W2, WO
+    def __init__(self, me, W2, WO, zs, zr, ps, pr):
+        self.me, self.W2, self.WO = me, W2, WO
         self.zs, self.zr, self.ps, self.pr = zs, zr, ps, pr
 
-    def zpart(self, a, q, piece, ref=None):
+    def zpart(self, a, q, piece):
         if a < 2:
-            rows = pl.ds(96 * piece, 96)
-            return self.W2.at[q, a, rows, :] if ref is None else ref.at[rows, :]
-        base = 192 * q if ref is None else 0
-        return (self.WO if ref is None else ref).at[
-            pl.ds(base + 48 * (piece // 2), 48), pl.ds(384 * (piece % 2), 384)
-        ]
+            return self.W2.at[q, a, pl.ds(96 * piece, 96), :]
+        return self.WO.at[pl.ds(192 * q + 48 * (piece // 2), 48), pl.ds(384 * (piece % 2), 384)]
 
     def part(self, a, q, piece, half=None):
-        if a == 0:
+        if a < 2:
             lo, n = (0, 96) if half is None else (48 * half, 48)
-            return self.W2.at[q, :, pl.ds(96 * piece + lo, n), :]
+            return self.W2.at[q, a, pl.ds(96 * piece + lo, n), :]
         lo, n = (0, 48) if half is None else ((0, 32), (32, 16))[half]
         return self.WO.at[pl.ds(192 * q + 48 * (piece // 2) + lo, n), pl.ds(384 * (piece % 2), 384)]
 
@@ -156,8 +152,8 @@
 
     def zcopy(self, d, k, a):
         p, q = self.me.p, self.quarter(d, k)
-        src = self.zpart(a, q, p, self.shards[a]) if k == 0 else self.zpart(a, q, p)
-        return push(src, self.zpart(a, q, p), self.zs.at[d, k, a], self.zr.at[d, k, a], self.me.z(1 if d == 0 else 3))
+        part = self.zpart(a, q, p)
+        return push(part, part, self.zs.at[d, k, a], self.zr.at[d, k, a], self.me.z(1 if d == 0 else 3))
 
     def zgot(self, d, k, a):
         dst = self.zpart(a, self.quarter(d, k + 1), self.me.p)
@@ -170,6 +166,26 @@
             def _():
                 for a in arrays:
                     self.zcopy(d, k, a).start()
+
+    def spread(self, k, a):
+        self.zwait(k, (a,))
+        self.pstart(k, 0, (a,))
+
+    def turn(self, k, a):
+        self.pwait(k, 0, (0, 1), (a,))
+        self.pstart(k, 1, (a,))
+
+    def last(self, k, a):
+        self.pwait(k, 1, (0, 1), (a,))
+        self.pstart(k, 2, (a,))
+
+    def zown(self, k):
+        for d in (0, 1):
+            last = self.me.j == (k if d == 0 else 3 - k)
+
+            @pl.when(self.sends(d, 0) & last)
+            def _():
+                self.zcopy(d, 0, 1).start()
 
     def zwait(self, k, arrays):
         for d in (0, 1):
@@ -206,39 +222,58 @@
             ]
         return [self.part(a, q, me.pd + c)]
 
-    def pstart(self, k, stage):
+    def pstart(self, k, stage, arrays):
         for d in (0, 1):
 
             @pl.when(self.gets(d, k))
             def _():
-                for a in (0, 1):
+                for a in arrays:
                     for i, (ref, dp) in enumerate(self.routes(d, k, a, stage)):
                         s = 3 * stage + i if stage < 2 else 7
                         push(ref, ref, self.ps.at[d, k, a, s], self.pr.at[d, k, a, s], self.me.at(dp)).start()
 
-    def pwait(self, k, stage, which, send=False):
+    def pwait(self, k, stage, which, arrays, send=False):
         for d in (0, 1):
 
             @pl.when(self.gets(d, k))
             def _():
+                for a in arrays:
+                    self.one(d, k, stage, which, a, send)
+
+    def one(self, d, k, stage, which, a, send=False):
+        if send:
+            refs = [r for r, _ in self.routes(d, k, a, stage)]
+        else:
+            refs = self.arrivals(d, k, a, stage)
+        for i in which:
+            s = 3 * stage + i if stage < 2 else 7
+            c = push(refs[i], refs[i], self.ps.at[d, k, a, s], self.pr.at[d, k, a, s], self.me.at(self.me.pc))
+            c.wait_send() if send else c.wait_recv()
+
+    def rest(self, step):
+        for d, k, devices in NEEDS[step]:
+            here = self.me.j == devices[0]
+            for other in devices[1:]:
+                here = here | (self.me.j == other)
+
+            @pl.when(here)
+            def _():
                 for a in (0, 1):
-                    if send:
-                        refs = [r for r, _ in self.routes(d, k, a, stage)]
-                    else:
-                        refs = self.arrivals(d, k, a, stage)
-                    for i in which:
-                        s = 3 * stage + i if stage < 2 else 7
-                        c = push(refs[i], refs[i], self.ps.at[d, k, a, s], self.pr.at[d, k, a, s], self.me.at(self.me.pc))
-                        c.wait_send() if send else c.wait_recv()
+                    self.one(d, k, 0, (2,), a)
+                    self.one(d, k, 1, (2, 3), a)
+                    self.one(d, k, 2, (0,), a)
+
+    def out_rest(self):
+        for k in range(3):
+            self.pwait(k, 0, (2,), (2,))
+            self.pwait(k, 1, (2, 3), (2,))
+            self.pwait(k, 2, (0,), (2,))
 
     def finish(self):
         for k in range(3):
-            self.pwait(k, 0, (2,))
-            self.pwait(k, 1, (2, 3))
-            self.pwait(k, 2, (0,))
-            self.pwait(k, 0, (0, 1, 2), send=True)
-            self.pwait(k, 1, (0, 1, 2, 3), send=True)
-            self.pwait(k, 2, (0,), send=True)
+            self.pwait(k, 0, (0, 1, 2), (0, 1, 2), send=True)
+            self.pwait(k, 1, (0, 1, 2, 3), (0, 1, 2), send=True)
+            self.pwait(k, 2, (0,), (0, 1, 2), send=True)
             for d in (0, 1):
 
                 @pl.when(self.sends(d, k))
@@ -247,29 +282,60 @@
                         self.zcopy(d, k, a).wait_send()
 
 
+NEEDS = {
+    1: ((0, 0, (1, 2, 3)), (1, 0, (0,))),
+    2: ((1, 1, (0,)), (1, 0, (1, 2)), (0, 1, (3,))),
+    3: ((1, 2, (0,)), (1, 1, (1,)), (0, 1, (2,)), (0, 2, (3,))),
+}
+ORDER = ((0, 1, 2, 3), (1, 0, 2, 3), (2, 1, 3, 0), (3, 2, 1, 0))
+
+
+def quarter_at(j, i):
+    total = 0
+    for n in range(4):
+        for m in range(4):
+            total = total + ORDER[n][m] * ((j == n) & (i == m)).astype(jnp.int32)
+    return total
+
+
 def front_kernel(
-    ids, seg, step, ids8, tabt, timet, g1, b1, wq, w_up, w_down, w_out,
-    qm_o, k_o, v_o, kt_o, n1_o, x_o, lse_o, att_o, segr, segc, IDS, W2, WO,
-    tab, hot, eb, E, tb, TR, vt, s, pb, ot, sendb, attg, own2, own_o,
-    es, er, ts, tr, is_, ir, zs, zr, ps, pr, as_, ar, ls,
+    ids, seg, step, ids8, tabt, h_timet, g1, b1, h_wq, w_up, w_down, w_out, h_cot, pa, pg, pb2, pm,
+    h_qm, h_k, h_v, h_kt, h_n1, h_x, h_lse, h_segr, h_segc, h_gmid, h_gatt, h_vec, h_out, IDS, dw_o, dwo_o,
+    qm_o, k_o, v_o, kt_o, n1_o, x_o, lse_o, segr, segc, gmid_o, gatt_o, vec_o, out_o, wq, cot, timet,
+    W2, WO, tab, hot, eb, E, tb, TR, vt, s, pb, ot, sendb, attg,
+    att, hat, n2, n2t, gmt, gm, acc, gn2, stage, rc, accb, wst, wrc, wacc,
+    es, er, ts, tr, is_, ir, zs, zr, ps, pr, as_, ar, ls, cs, cr, ws, wr, hs, os,
 ):
     me = Place()
     p, j = me.p, me.j
     fetch = pltpu.make_async_copy(tabt, tab, ls.at[0])
+    fetch_time = pltpu.make_async_copy(h_timet, timet, ls.at[1])
+    later = [pltpu.make_async_copy(h_wq, wq, ls.at[6]), pltpu.make_async_copy(h_cot, cot, ls.at[7])]
+    fetch_time.start()
     fetch.start()
+    pairs = (
+        (qm_o, h_qm), (k_o, h_k), (v_o, h_v), (kt_o, h_kt), (n1_o, h_n1), (x_o, h_x), (lse_o, h_lse), (segr, h_segr),
+        (segc, h_segc), (gmid_o, h_gmid), (gatt_o, h_gatt), (vec_o, h_vec), (out_o, h_out),
+    )
+    homes = [pltpu.make_async_copy(src, dst, os.at[i]) for i, (src, dst) in enumerate(pairs)]
     load = [
-        pltpu.make_async_copy(w_up, own2.at[0], ls.at[3]),
-        pltpu.make_async_copy(w_down, own2.at[1], ls.at[4]),
-        pltpu.make_async_copy(w_out, own_o, ls.at[5]),
+        pltpu.make_async_copy(w_up, W2.at[j, 0], ls.at[3]),
+        pltpu.make_async_copy(w_down, W2.at[j, 1], ls.at[4]),
+        pltpu.make_async_copy(w_out, WO.at[pl.ds(192 * j, 192), :], ls.at[5]),
     ]
     for c in load:
         c.start()
+    for c in later:
+        c.start()
     write_segments(seg, segr, segc)
+    homes[7].start()
+    homes[8].start()
+    fetch_time.wait()
     lane = lax.broadcasted_iota(jnp.int32, (192, 1000), 1)
     column = jnp.sum(jnp.where(lane == step[0], timet[...].astype(F32), 0.0), axis=1, keepdims=True)
     tb[:, 0:192] = jnp.broadcast_to(column, (192, 128)).T[0:16, :].astype(BF)
     meet([me.z(1), me.z(2), me.z(3)] + [me.at((p + k) % 8) for k in range(1, 8)])
-    w = Weights(me, (own2.at[0], own2.at[1], own_o), W2, WO, zs, zr, ps, pr)
+    w = Weights(me, W2, WO, zs, zr, ps, pr)
 
     def ecopy(d, k, c):
         q = w.quarter(d, k)
@@ -292,10 +358,6 @@
                 push(dst, dst, es.at[d, k, c], er.at[d, k, c], me.z(1)).wait_recv()
 
     here = [pltpu.make_async_copy(ids8, IDS.at[p], ls.at[2])]
-    keep = [
-        pltpu.make_async_copy(own2, W2.at[j], ls.at[3]),
-        pltpu.make_async_copy(own_o, WO.at[pl.ds(192 * j, 192), :], ls.at[5]),
-    ]
     small = [push(tb, TR.at[j], ts.at[k - 1], tr.at[k - 1], me.z(k)) for k in (1, 2, 3)]
     small_ids = [push(ids8, IDS.at[p], is_.at[k - 1], ir.at[k - 1], me.at((p + k) % 8)) for k in range(1, 8)]
     ids_row = line_of(ids).astype(F32)
@@ -318,35 +380,41 @@
     fetch.wait()
     for c in load:
         c.wait()
-    w.zstart(0, (0,))
+    w.zstart(0, (2, 0))
     embed(0)
-    for c in small + here + small_ids + keep:
+    for c in small + here + small_ids:
         c.start()
     embed(1)
+    w.spread(0, 2)
+    w.zstart(1, (2,))
     embed(2)
     ewait(0, 0)
     estart(1, 0)
+    w.spread(0, 0)
     embed(3)
-    w.zstart(0, (1,))
+    w.zown(0)
     ewait(0, 1)
     estart(1, 1)
+    w.spread(1, 2)
+    w.zstart(2, (2,))
     ewait(0, 2)
     estart(1, 2)
     ewait(1, 0)
     estart(2, 0)
     ewait(0, 3)
     estart(1, 3)
+    w.zown(1)
     ewait(1, 1)
     estart(2, 1)
-    w.zwait(0, (0,))
-    w.zstart(0, (2,))
+    w.spread(2, 2)
     ewait(1, 2)
     estart(2, 2)
-    w.zstart(1, (0,))
     for c in small:
         c.wait()
     E[j] = eb[...]
     TR[j] = tb[...]
+    for c in later:
+        c.wait()
     time_row = jnp.concatenate([TR[q].astype(F32)[0:1, 0:192] for q in range(4)], axis=1)
     gain, shift = line_of(g1), line_of(b1)
 
@@ -371,49 +439,58 @@
         kt_o[:, rows] = contract_cols(wq[192:384, :], normed).astype(BF)
         vt[:, rows] = contract_cols(wq[384:576, :], normed).astype(BF)
 
+    ewait(1, 3)
+    estart(2, 3)
+    w.zown(2)
+    w.zstart(1, (0,))
     ewait(2, 0)
     norm_qkv(0)
-    ewait(1, 3)
-    estart(2, 3)
-    w.zwait(0, (1, 2))
-    w.zstart(1, (1, 2))
-    w.pstart(0, 0)
+    for k in range(3):
+        w.turn(k, 2)
+    w.turn(0, 0)
     ewait(2, 1)
     norm_qkv(1)
+    for k in range(3):
+        w.last(k, 2)
+    w.last(0, 0)
     ewait(2, 2)
     norm_qkv(2)
     ewait(2, 3)
     norm_qkv(3)
+    for c in homes[:6]:
+        c.start()
+    w.spread(0, 1)
+    w.zstart(1, (1,))
 
     def att_copy(b):
         return push(sendb.at[b], attg.at[j], as_.at[b], ar.at[j], (p, b))
 
     def step0():
-        w.zwait(1, (0,))
+        w.spread(1, 0)
         w.zstart(2, (0,))
 
     def step1():
-        w.pwait(0, 0, (0, 1))
-        w.pstart(0, 1)
+        w.turn(0, 1)
 
     def step2():
-        w.zwait(1, (1, 2))
-        w.zstart(2, (1, 2))
-        w.pstart(1, 0)
+        w.spread(1, 1)
+        w.zstart(2, (1,))
 
     def step3():
-        w.pwait(0, 1, (0, 1))
-        w.pstart(0, 2)
+        w.turn(1, 0)
+        w.last(0, 1)
 
     def step4():
-        w.pwait(1, 0, (0, 1))
-        w.pstart(1, 1)
+        w.spread(2, 0)
 
     def step5():
-        w.zwait(2, (0, 1, 2))
-        w.pstart(2, 0)
-
-    steps = {0: step0, 2: step1, 4: step2, 6: step3, 10: step4, 11: step5}
+        w.turn(1, 1)
+        w.last(1, 0)
+
+    def step6():
+        w.spread(2, 1)
+
+    steps = {1: step0, 3: step1, 4: step2, 6: step3, 8: step4, 10: step5, 11: step6}
 
     def slot(i, n):
         for k, step in {k: v for k, v in steps.items() if k % 3 == n}.items():
@@ -456,20 +533,118 @@
 
         slot(i, 2)
 
+    homes[6].start()
     attg[j] = sendb[j]
-    w.pwait(1, 1, (0, 1))
-    w.pstart(1, 2)
+    w.out_rest()
     for q in range(4):
 
         @pl.when(j != q)
         def _():
             push(attg.at[q], attg.at[q], as_.at[q], ar.at[q], me.z(1)).wait_recv()
 
-    att_o[...] = jnp.concatenate([unfold(attg[q]) for q in range(4)], axis=1)
-    w.pwait(2, 0, (0, 1))
-    w.pstart(2, 1)
-    w.pwait(2, 1, (0, 1))
-    w.pstart(2, 2)
+    w.last(1, 1)
+    w.turn(2, 0)
+    att[...] = jnp.concatenate([unfold(attg[q]) for q in range(4)], axis=1)
+    mid = x_o[...] + dot(att[...], WO[...]) + line_of(pa)
+    h0, scale = norm_stats(mid)
+    hat[...] = h0
+    normed = h0 * line_of(pg) + line_of(pb2)
+    n2[...] = normed.astype(BF)
+    n2t[...] = normed.T.astype(BF)
+    valid = across((segr[:, lanes(j)] != 0.0).astype(F32))[:, 0:1]
+    gmid_o[...] = cot[...].astype(F32) * valid
+    gm[...] = gmid_o[...].astype(BF)
+    gmt[...] = gmid_o[...].T.astype(BF)
+    acc[...] = mid + line_of(pm)
+    gn2[...] = jnp.zeros_like(gn2)
+
+    def to_sibling(i):
+        return push(stage.at[i % 2, :, :, 1 - me.core], rc.at[i], cs.at[i], cr.at[i], me.at(me.pc))
+
+    def save(i):
+        return pltpu.make_async_copy(accb.at[i % 2], dw_o.at[:, quarter_at(j, i)], hs.at[i % 2])
+
+    def chip(i):
+        to_sibling(i).wait_recv()
+        for u in range(2):
+            for m in range(4):
+                accb[i % 2, u, m] = stage[i % 2, u, m, me.core] + rc[i, u, m]
+        save(i).start()
+
+    def pump1():
+        w.last(2, 1)
+        w.rest(1)
+
+    def pump2():
+        w.rest(2)
+
+    def pump3():
+        w.rest(3)
+
+    w.last(2, 0)
+    w.turn(2, 1)
+
+    @pl.loop(0, 4)
+    def _(i):
+        q = quarter_at(j, i)
+        pl.when(i == 1)(pump1)
+        pl.when(i == 2)(pump2)
+        pl.when(i == 3)(pump3)
+        pre = dot(n2[...], W2[q, 0])
+        c = 0.7978845608028654
+        t = jnp.tanh(c * (pre + 0.044715 * pre * pre * pre))
+        act = (0.5 * pre * (1.0 + t)).astype(BF)
+        slope = 0.5 * (1.0 + t) + 0.5 * pre * (1.0 - t * t) * (c * (1.0 + 3 * 0.044715 * pre * pre))
+        acc[...] += dot(act, W2[q, 1])
+        grad_pre = (contract_cols(gm[...], W2[q, 1]) * slope).astype(BF)
+        gn2[...] += contract_cols(grad_pre, W2[q, 0])
+
+        @pl.when(i >= 2)
+        def _():
+            to_sibling(i - 2).wait_send()
+            save(i - 2).wait()
+
+        for u, full in ((0, dot(n2t[...], grad_pre)), (1, dot(gmt[...], act))):
+            for n in range(8):
+                stage[i % 2, u, n // 2, n % 2] = full[96 * n : 96 * n + 96, :].astype(BF)
+        to_sibling(i).start()
+
+        @pl.when(i >= 1)
+        def _():
+            chip(i - 1)
+
+    out_o[...] = acc[...].astype(BF)
+    homes[12].start()
+    grad = gmid_o[...]
+    gn, h0 = gn2[...], hat[...]
+    vec_o[...] = jnp.zeros_like(vec_o)
+    vec_o[3:4, :] = rows_sum(gn * h0)
+    vec_o[4:5, :] = rows_sum(gn)
+    vec_o[5:6, :] = rows_sum(grad)
+    gmid = grad + norm_back(gn, line_of(pg), h0, scale)
+    gmid_o[...] = gmid
+    vec_o[2:3, :] = rows_sum(gmid)
+    gatt_o[...] = contract_cols(gmid.astype(BF), WO[...]).astype(BF)
+    for c in homes[9:12]:
+        c.start()
+    full = dot(gmid.T.astype(BF), att[...]).astype(BF)
+    for q in range(4):
+        for n in range(8):
+            wst[q, n // 2, n % 2, :, 0:192] = full[96 * n : 96 * n + 96, 192 * q : 192 * q + 192]
+            wst[q, n // 2, n % 2, :, 192:256] = jnp.zeros((96, 64), BF)
+    wo_copy = push(wst.at[:, :, 1 - me.core], wrc, ws, wr, me.at(me.pc))
+    wo_copy.start()
+    save(2).wait()
+    chip(3)
+    wo_copy.wait_recv()
+    for q in range(4):
+        for m in range(4):
+            wacc[q, m] = wst[q, m, me.core] + wrc[q, m]
+    wsave = pltpu.make_async_copy(wacc, dwo_o, hs.at[0])
+    to_sibling(2).wait_send()
+    to_sibling(3).wait_send()
+    wo_copy.wait_send()
+    wsave.start()
     for b in range(4):
 
         @pl.when(j != b)
@@ -485,31 +660,49 @@
                     ecopy(d, k, c).wait_send()
 
     w.finish()
-    for c in small_ids + here + keep:
+    for c in small_ids + here:
         c.wait()
-
-
-def front(ids, seg, step, ids8, tabt, timet, g1, b1, wq, w_up, w_down, w_out):
+    save(3).wait()
+    wsave.wait()
+    for c in homes:
+        c.wait()
+
+
+FRONT_KEPT = (
+    ((3, L, 192), BF),
+    ((L, 192), BF),
+    ((L, 192), BF),
+    ((192, L), BF),
+    ((L, D), BF),
+    ((256, D), F32),
+    ((12, 1, 256), F32),
+    ((1, L), F32),
+    ((L, 1), F32),
+    ((256, D), F32),
+    ((256, D), BF),
+    ((8, D), F32),
+    ((256, D), BF),
+)
+
+
+def front(*args):
     return pl.pallas_call(
         front_kernel,
-        out_shape=(
-            shape((3, L, 192), BF),
-            shape((L, 192), BF),
-            shape((L, 192), BF),
-            shape((192, L), BF),
-            shape((L, D), BF),
-            shape((256, D), F32),
-            shape((12, 1, 256), F32),
-            shape((256, D), BF),
-            shape((1, L), F32),
-            shape((L, 1), F32),
+        out_shape=tuple(shape(*a) for a in FRONT_KEPT)
+        + (
             shape((8, 8, 128), jnp.int32),
-            shape((4, 2, D, D), BF),
-            shape((D, D), BF),
+            shape((2, 4, 4, 96, D), BF),
+            shape((4, 4, 96, 256), BF),
         ),
-        in_specs=[VM] * 2 + [pl.BlockSpec(memory_space=pltpu.SMEM)] + [ANY] * 2 + [VM] * 4 + [ANY] * 3,
-        out_specs=(VM,) * 10 + (ANY,) * 3,
-        scratch_shapes=[
+        in_specs=[VM] * 2 + [pl.BlockSpec(memory_space=pltpu.SMEM)] + [ANY] * 3 + [VM] * 2 + [ANY] * 5 + [VM] * 4,
+        out_specs=(ANY,) * 16,
+        scratch_shapes=[pltpu.VMEM(*a) for a in FRONT_KEPT]
+        + [
+            pltpu.VMEM((576, D), BF),
+            pltpu.VMEM((256, D), BF),
+            pltpu.VMEM((192, 1000), BF),
+            pltpu.VMEM((4, 2, D, D), BF),
+            pltpu.VMEM((D, D), BF),
             pltpu.VMEM((192, 8192), BF),
             pltpu.VMEM((256, 2048), BF),
             pltpu.VMEM((4, 128, 384), BF),
@@ -522,8 +715,20 @@
             pltpu.VMEM((192, 256), F32),
             pltpu.VMEM((4, 128, 384), BF),
             pltpu.VMEM((4, 128, 384), BF),
-            pltpu.VMEM((2, D, D), BF),
-            pltpu.VMEM((192, D), BF),
+            pltpu.VMEM((256, D), BF),
+            pltpu.VMEM((256, D), F32),
+            pltpu.VMEM((256, D), BF),
+            pltpu.VMEM((D, 256), BF),
+            pltpu.VMEM((D, 256), BF),
+            pltpu.VMEM((256, D), BF),
+            pltpu.VMEM((256, D), F32),
+            pltpu.VMEM((256, D), F32),
+            pltpu.VMEM((2, 2, 4, 2, 96, D), BF),
+            pltpu.VMEM((4, 2, 4, 96, D), BF),
+            pltpu.VMEM((2, 2, 4, 96, D), BF),
+            pltpu.VMEM((4, 4, 2, 96, 256), BF),
+            pltpu.VMEM((4, 4, 96, 256), BF),
+            pltpu.VMEM((4, 4, 96, 256), BF),
             DMA((2, 3, 4)),
             DMA((2, 3, 4)),
             DMA((3,)),
@@ -532,16 +737,21 @@
             DMA((7,)),
             DMA((2, 3, 3)),
             DMA((2, 3, 3)),
-            DMA((2, 3, 2, 8)),
-            DMA((2, 3, 2, 8)),
+            DMA((2, 3, 3, 8)),
+            DMA((2, 3, 3, 8)),
             DMA((4,)),
             DMA((4,)),
-            DMA((6,)),
+            DMA((8,)),
+            DMA((4,)),
+            DMA((4,)),
+            DMA,
+            DMA,
+            DMA((2,)),
+            DMA((13,)),
         ],
         compiler_params=params(0),
         name="front",
-    )(ids, seg, step, ids8, tabt, timet, g1, b1, wq, w_up, w_down, w_out)
-
+    )(*args)
 
 def norm_stats(x):
     centered = x - jnp.mean(x, axis=1, keepdims=True)
@@ -556,118 +766,6 @@
 
 def rows_sum(x):
     return jnp.sum(x, axis=0, keepdims=True)
-
-
-def mid_kernel(
-    att, x, wo, w2, cot, segr, pa, pg, pb, pm,
-    out_o, gmid_o, gatt_o, dw_o, dwo_o, vec_o,
-    sm, hat, sc, n2, n2t, gmt, gm, acc, gn2,
-):
-    q = pl.program_id(0)
-    own = pl.ds(pl.multiple_of(256 * lax.axis_index("mp"), 256), 256)
-
-    def masked():
-        valid = across((segr[:, own] != 0.0).astype(F32))[:, 0:1]
-        return cot[...].astype(F32) * valid
-
-
-    @pl.when(q == 0)
-    def _():
-        mid = x[...] + dot(att[...], wo[...]) + line_of(pa)
-        sm[...] = mid
-        h, scale = norm_stats(mid)
-        hat[...] = h
-        sc[...] = scale
-        normed = (h * line_of(pg) + line_of(pb)).astype(BF)
-        n2[...] = normed
-        n2t[...] = normed.astype(F32).T.astype(BF)
-        grad = masked()
-        gm[...] = grad.astype(BF)
-        gmt[...] = grad.T.astype(BF)
-        acc[...] = mid + line_of(pm)
-        gn2[...] = jnp.zeros_like(gn2)
-
-    up, down = w2[0, 0], w2[0, 1]
-    pre = dot(n2[...], up)
-    c = 0.7978845608028654
-    cubic = c * (pre + 0.044715 * pre * pre * pre)
-    t = jnp.tanh(cubic)
-    act = (0.5 * pre * (1.0 + t)).astype(BF)
-    slope = 0.5 * (1.0 + t) + 0.5 * pre * (1.0 - t * t) * (c * (1.0 + 3 * 0.044715 * pre * pre))
-    acc[...] += dot(act, down)
-    grad_pre = (contract_cols(gm[...], down) * slope).astype(BF)
-    gn2[...] += contract_cols(grad_pre, up)
-    dw_o[0, 0] = dot(n2t[...], grad_pre).astype(BF)
-    dw_o[1, 0] = dot(gmt[...], act).astype(BF)
-
-    @pl.when(q == 3)
-    def _():
-        out_o[...] = acc[...].astype(BF)
-        grad = masked()
-        gn, h = gn2[...], hat[...]
-        gmid = grad + norm_back(gn, line_of(pg), h, sc[...])
-        gmid_o[...] = gmid
-        vec_o[...] = jnp.zeros_like(vec_o)
-        vec_o[2:3, :] = rows_sum(gmid)
-        vec_o[3:4, :] = rows_sum(gn * h)
-        vec_o[4:5, :] = rows_sum(gn)
-        vec_o[5:6, :] = rows_sum(grad)
-        ga = gmid.astype(BF)
-        gatt_o[...] = contract_cols(ga, wo[...]).astype(BF)
-        full = dot(gmid.T.astype(BF), att[...]).astype(BF)
-        for i in range(4):
-            dwo_o[i, :, 0:192] = full[:, 192 * i : 192 * i + 192]
-            dwo_o[i, :, 192:256] = jnp.zeros((D, 64), BF)
-
-
-def mid(att, x, wo, w2, cot, segr, pa, pg, pb, pm):
-    whole = lambda a: pl.BlockSpec(a.shape, lambda q: (0,) * a.ndim)
-    keep = lambda *dims: pl.BlockSpec(dims, lambda q: (0,) * len(dims))
-    return pl.pallas_call(
-        mid_kernel,
-        grid=(4,),
-        out_shape=(
-            shape((256, D), BF),
-            shape((256, D), F32),
-            shape((256, D), BF),
-            shape((2, 4, D, D), BF),
-            shape((4, D, 256), BF),
-            shape((8, D), F32),
-        ),
-        in_specs=[
-            whole(att),
-            whole(x),
-            whole(wo),
-            pl.BlockSpec((1, 2, D, D), lambda q: (q, 0, 0, 0)),
-            whole(cot),
-            whole(segr),
-            whole(pa),
-            whole(pg),
-            whole(pb),
-            whole(pm),
-        ],
-        out_specs=(
-            keep(256, D),
-            keep(256, D),
-            keep(256, D),
-            pl.BlockSpec((2, 1, D, D), lambda q: (0, q, 0, 0)),
-            keep(4, D, 256),
-            keep(8, D),
-        ),
-        scratch_shapes=[
-            pltpu.VMEM((256, D), F32),
-            pltpu.VMEM((256, D), F32),
-            pltpu.VMEM((256, 1), F32),
-            pltpu.VMEM((256, D), BF),
-            pltpu.VMEM((D, 256), BF),
-            pltpu.VMEM((D, 256), BF),
-            pltpu.VMEM((256, D), BF),
-            pltpu.VMEM((256, D), F32),
-            pltpu.VMEM((256, D), F32),
-        ],
-        compiler_params=pltpu.CompilerParams(vmem_limit_bytes=60 << 20, dimension_semantics=("arbitrary",)),
-        name="mid",
-    )(att, x, wo, w2, cot, segr, pa, pg, pb, pm)
 
 
 class Line:
@@ -759,14 +857,18 @@
         ]
 
     def load(self):
-        return pltpu.make_async_copy(self.src.at[:, :, self.me.core], self.acc, self.lsem)
+        src = self.src if self.rc is None else self.src.at[:, :, self.me.core]
+        return pltpu.make_async_copy(src, self.acc, self.lsem)
 
     def begin(self):
-        self.copies(0)[0].start()
         self.load().start()
+        if self.rc is not None:
+            self.copies(0)[0].start()
 
     def chip(self):
         self.load().wait()
+        if self.rc is None:
+            return
         self.copies(0)[0].wait_recv()
 
         @pl.loop(0, self.nq)
@@ -810,7 +912,8 @@
             self.acc[q, me.m, 0:48] = self.acc[q, me.m, 0:48] + self.ry2[q]
             self.acc[q, me.m, 48:96] = self.acc[q, me.m, 48:96] + self.rx2[q]
 
-        self.copies(0)[0].wait_send()
+        if self.rc is not None:
+            self.copies(0)[0].wait_send()
 
     def own(self, q):
         return self.acc.at[q, self.me.m]
@@ -820,12 +923,19 @@
 
 
 def back_kernel(
-    gatt, qm, k, v, kt, lse, n1, wq, x, gmid, segc, segr, g1, vec, IDS, step, dw, dwo,
+    h_gatt, h_qm, h_k, h_v, h_kt, h_lse, h_n1, h_wq, h_x, h_gmid, h_segc, h_segr, h_vec, h_ids, dw, dwo, g1, step,
     h_in, h_tok, h_up, h_down, h_out, h_qkv, h_sp,
-    *scratch,
+    gatt, qm, k, v, kt, lse, n1, wq, x, gmid, segc, segr, vec, IDS, gs, *scratch,
 ):
     me = Place()
     p, j = me.p, me.j
+    pairs = (
+        (h_gatt, gatt), (h_k, k), (h_qm, qm), (h_v, v), (h_segc, segc), (h_segr, segr), (h_lse, lse), (h_kt, kt),
+        (h_n1, n1), (h_wq, wq), (h_x, x), (h_gmid, gmid), (h_vec, vec), (h_ids, IDS),
+    )
+    loads = [pltpu.make_async_copy(src, dst, gs.at[i]) for i, (src, dst) in enumerate(pairs)]
+    for c in loads[:8]:
+        c.start()
     meet([me.z(1), me.z(2), me.z(3)] + [me.at((p + i) % 8) for i in range(1, 8)])
     it = iter(scratch)
     take = lambda n: [next(it) for _ in range(n)]
@@ -838,7 +948,8 @@
     sources = (dw.at[1], dw.at[0], dwo, qk)
     units, lines = [], []
     for i, src in enumerate(sources):
-        acc, rc, rx, ry, rx2, ry2, sems, lsem = take(8)
+        acc, rx, ry, rx2, ry2, sems, lsem = take(7)
+        rc = take(1)[0] if i == 3 else None
         unit = Unit(me, src, acc, rc, rx, ry, rx2, ry2, sems, lsem)
         units.append(unit)
         if i < 3:
@@ -856,6 +967,7 @@
     def to_heads(d):
         return push(sendb.at[d], gbuf.at[j], as_.at[d], ar.at[j], (p, d))
 
+    loads[0].wait()
     for d in range(4):
         sendb[d] = fold(gatt[:, 192 * d : 192 * d + 192])
 
@@ -864,27 +976,26 @@
             to_heads(d).start()
 
     gbuf[j] = sendb[j]
-    for u in units[:3]:
-        u.begin()
+    for i in (0, 2, 1):
+        units[i].begin()
+    for c in loads[8:]:
+        c.start()
     dk[...] = jnp.zeros_like(dk)
     dv[...] = jnp.zeros_like(dv)
 
-    def step0():
-        units[0].chip()
-        units[0].cross()
-
-    def step1():
-        units[2].chip()
-        units[2].cross()
-
-    def step2():
-        units[1].chip()
-
-    steps = {0: step0, 2: step1, 4: step2}
+    units[0].chip()
+    units[0].cross()
+    units[2].chip()
+    units[2].cross()
+    units[1].chip()
+    steps = {}
 
     def slot(i, n):
         for c, fn in {c: fn for c, fn in steps.items() if c % 3 == n}.items():
             pl.when(i == c // 3)(fn)
+
+    for c in loads[1:8]:
+        c.wait()
 
     @pl.loop(0, 4)
     def _(i):
@@ -925,6 +1036,8 @@
             dqt[part, lanes(b)] = dot(kt[part, :], dsb[:, 256 * h : 256 * h + 256]) * 0.125
         slot(i, 2)
 
+    for c in loads[8:]:
+        c.wait()
     for q, starts in ((3, ((3, 0),)), (0, ((0, 1),)), (2, ((2, 0),)), (1, ((1, 1), (1, 0), (2, 1)))):
         rows = slice(256 * q, 256 * q + 256)
         dq = dqt[:, rows].T.astype(BF)
@@ -1104,8 +1217,27 @@
         line.close()
 
 
-def back(gatt, qm, k, v, kt, lse, n1, wq, x, gmid, segc, segr, g1, vec, ids, step, dw, dwo):
-    scratch = [
+BACK_KEPT = (
+    ((256, D), BF),
+    ((3, L, 192), BF),
+    ((L, 192), BF),
+    ((L, 192), BF),
+    ((192, L), BF),
+    ((12, 1, 256), F32),
+    ((L, D), BF),
+    ((576, D), BF),
+    ((256, D), F32),
+    ((256, D), F32),
+    ((L, 1), F32),
+    ((1, L), F32),
+    ((8, D), F32),
+    ((8, 8, 128), jnp.int32),
+)
+
+
+def back(*args):
+    scratch = [pltpu.VMEM(*a) for a in BACK_KEPT] + [
+        DMA((14,)),
         pltpu.VMEM((4, 128, 384), BF),
         pltpu.VMEM((4, 128, 384), BF),
         pltpu.VMEM((3, 256, 192), BF),
@@ -1152,7 +1284,6 @@
     for i, (nq, w) in enumerate(SHAPES):
         scratch += [
             pltpu.VMEM((nq, 4, 96, w), BF),
-            pltpu.VMEM((nq, 4, 96, w), BF),
             pltpu.VMEM((nq, 2, 48, w), BF),
             pltpu.VMEM((nq, 2, 48, w), BF),
             pltpu.VMEM((nq, 48, w), BF),
@@ -1160,7 +1291,9 @@
             DMA((2, 7)),
             DMA,
         ]
-        if i < 3:
+        if i == 3:
+            scratch += [pltpu.VMEM((nq, 4, 96, w), BF)]
+        else:
             scratch += [pltpu.VMEM((4, 96, w), BF), pltpu.VMEM((4, 96, w), BF), DMA((4, 4))]
     return pl.pallas_call(
         back_kernel,
@@ -1173,12 +1306,12 @@
             shape((3, 96, 256), F32),
             shape((8, 8, D), F32),
         ),
-        in_specs=[VM] * 15 + [pl.BlockSpec(memory_space=pltpu.SMEM)] + [ANY] * 2,
+        in_specs=[ANY] * 16 + [VM, pl.BlockSpec(memory_space=pltpu.SMEM)],
         out_specs=(ANY,) * 7,
         scratch_shapes=scratch,
         compiler_params=params(1),
         name="back",
-    )(gatt, qm, k, v, kt, lse, n1, wq, x, gmid, segc, segr, g1, vec, ids, step, dw, dwo)
+    )(*args)
 
 
 def tail_kernel(sp, din, tok, up, down, wout, qkv, *outs):
@@ -1469,19 +1602,16 @@
     token_ids, segment_ids, timesteps, token_table, time_table, ln1_gain, ln1_bias, w_qkv, w_out, attn_bias,
     ln2_gain, ln2_bias, w_up, w_down, mlp_bias, cotangent,
 ):
-    ndp, width = 8, 192
+    width = 192
     ids8 = token_ids.reshape(8, 128)
     wq = w_qkv.transpose(1, 2, 0).reshape(3 * width, D)
-    qm, k, v, kt, normed_one, stream_in, lse, att_own, segr, segc, IDS, W2, WO = front(
-        token_ids, segment_ids, timesteps, ids8, token_table.T, time_table.T, ln1_gain, ln1_bias, wq, w_up, w_down, w_out
+    qm, k, v, kt, normed_one, stream_in, lse, segr, segc, grad_mid, grad_attended, vec, out, IDS, dw, dwo = front(
+        token_ids, segment_ids, timesteps, ids8, token_table.T, time_table.T, ln1_gain, ln1_bias, wq, w_up, w_down, w_out,
+        cotangent, attn_bias, ln2_gain, ln2_bias, mlp_bias,
     )
-    out, grad_mid, grad_attended, dw, dwo, vec = mid(
-        att_own, stream_in, WO, W2, cotangent, segr, attn_bias, ln2_gain, ln2_bias, mlp_bias
-    )
-    pieces = lambda a: a.reshape(a.shape[:-2] + (ndp // 2, 2, D // ndp, a.shape[-1]))
     input_grad, grad_token_table, g_up, g_down, g_out, g_qkv, SP = back(
-        grad_attended, qm, k, v, kt, lse, normed_one, wq, stream_in, grad_mid, segc, segr, ln1_gain, vec, IDS, timesteps,
-        pieces(dw), pieces(dwo),
+        grad_attended, qm, k, v, kt, lse, normed_one, wq, stream_in, grad_mid, segc, segr, vec, IDS, dw, dwo, ln1_gain,
+        timesteps,
     )
     o_time, o_in, o_tok, o_up, o_down, o_out, o_qkv, *sums = tail(
         SP, input_grad, grad_token_table, g_up, g_down, g_out, g_qkv

time: 202 us -> 187 us (0.926)
  Pallas kernels: 199 us -> 183 us
    pallas_call x2 -> x1, Pallas kernels: 100 us -> 89.3 us  [front(): pl.pallas_call(front_kernel, out_shape=tuple((shape(*a) for a in FRONT_KE...]
    pallas_call x1, Pallas kernels: 92.4 us -> 86.6 us  [back(): pl.pallas_call(back_kernel, out_shape=(shape((256, D), F32), shape((1024,...]
where the time goes in v4:
time: 187 us; the launch traced here: 185 us
  Pallas kernels  183 us (98%)
    pallas_call x1, Pallas kernels, front(): pl.pallas_call(front_kernel, out_shape=tuple((shape(*a) for a in FRONT_KE...  89.3 us
    pallas_call x1, Pallas kernels, back(): pl.pallas_call(back_kernel, out_shape=(shape((256, D), F32), shape((1024,...  86.6 us
    pallas_call x1, Pallas kernels, tail(): pl.pallas_call(tail_kernel, grid=(5,), out_shape=(shape((1000, D), F32),)...  7.08 us

profile of v4, /device:TPU:0, one launch (start us, length us, event | category | flops | bytes accessed | tf_op | source)
XLA Modules:
  0.0 185.1 jit_solution(8749404619227049624)
XLA Ops:
  1.3 89.3 %front.1 = (bf16[3,1024,192]{2,1,0:T(8,128)(2,1)}, bf16[1024,192]{1,0:T(8,128)(2,1)}, bf16[1024,192]{1,0:T(8,128)(2,1)}, bf16[192,1024]{1,0:T(8,128)(2,1)}, bf16...) custom-call(s32[1024]{0:T(1024)} %ids.1, ...), custom_call_target="tpu_custom_call" | custom-call | tf_op jit(solution)/shard_map/front/pallas_call | solution.py:689
  90.6 86.6 %back.1 = (f32[256,768]{1,0:T(8,128)}, f32[1024,192]{1,0:T(8,128)}, f32[96,768]{1,0:T(8,128)}, f32[96,768]{1,0:T(8,128)}, f32[96,256]{1,0:T(8,128)}, /*index=5*/f32[3,96,256]{2,1,0:T(8,128)}, f32[8,8,768]{2,1,0:T(8,128)}) custom-call(bf16[256,768]{1,0:T(8,128)(2,1)} %get-tuple-element.51.h_gatt, bf16[3,1024,192]{2,1,0:T(8,128)(2,1)} %get-tuple-element.52.h_qm, ...), custom_call_target="tpu_custom_call" | custom-call | tf_op jit(solution)/shard_map/back/pallas_call | solution.py:1298
  177.3 0.0 copy-start
  177.3 7.1 %tail.1 = (f32[1000,768]{1,0:T(8,128)}, f32[256,768]{1,0:T(8,128)}, f32[192,1024]{1,0:T(8,128)}, f32[96,768]{1,0:T(8,128)}, f32[96,768]{1,0:T(8,128)}, /*index=5...) custom-call(f32[8,8,768]{2,1,0:T(8,128)} %get-tuple-element.66.sp, ...), custom_call_target="tpu_custom_call" | custom-call | tf_op jit(solution)/shard_map/tail/pallas_call | solution.py:1351
  184.4 0.0 copy-done
  184.4 0.7 copy.32
Async XLA Ops:
  177.3 7.1 %copy-start = (bf16[256,768]{1,0:T(8,128)(2,1)S(1)}, bf16[256,768]{1,0:T(8,128)(2,1)}, u32[]{:S(2)}) copy-start(bf16[256,768]{1,0:T(8,128)(2,1)} %get-tuple-element.100) | copy-start | bytes 1179652

commit v5 on v4

--- a/solution.py
+++ b/solution.py
@@ -364,7 +364,7 @@
 
     def embed(c):
         token = across(ids_row[:, 256 * c : 256 * c + 256])
-        s[0, 0:256, 0:192] = jnp.zeros((256, 192), F32)
+        s[0:256, 0:192] = jnp.zeros((256, 192), F32)
 
         @pl.loop(0, 4)
         def _(v):
@@ -372,9 +372,9 @@
             for i in range(16):
                 word = lax.broadcasted_iota(jnp.int32, (256, 128), 1).astype(F32) + (base + 128.0 * i)
                 hot[:, 128 * i : 128 * i + 128] = (token == word).astype(F32).astype(BF)
-            s[0, 0:256, 0:192] += contract_cols(hot[...], tab[:, pl.ds(pl.multiple_of(2048 * v, 2048), 2048)])
-
-        eb[c] = fold(s[0, 0:256, 0:192].astype(BF))
+            s[0:256, 0:192] += contract_cols(hot[...], tab[:, pl.ds(pl.multiple_of(2048 * v, 2048), 2048)])
+
+        eb[c] = fold(s[0:256, 0:192].astype(BF))
         estart(0, c)
 
     fetch.wait()
@@ -487,10 +487,7 @@
         w.turn(1, 1)
         w.last(1, 0)
 
-    def step6():
-        w.spread(2, 1)
-
-    steps = {1: step0, 3: step1, 4: step2, 6: step3, 8: step4, 10: step5, 11: step6}
+    steps = {1: step0, 3: step1, 4: step2, 6: step3, 9: step5, 11: step4}
 
     def slot(i, n):
         for k, step in {k: v for k, v in steps.items() if k % 3 == n}.items():
@@ -500,16 +497,16 @@
     def _(i):
         b = (j + 1 + i) % 4
         sq = segr[0:1, lanes(b)]
-        for h in range(3):
-            s[h] = contract_cols(k_o[...], qm_o[h, lanes(b), :])
+        s[...] = contract_cols(k_o[...], qm_o[:, lanes(b), :].reshape(768, 192))
         slot(i, 0)
         top = [jnp.full((8, 256), -jnp.inf, F32)] * 3
         for c in range(L // CH):
             rows = slice(CH * c, CH * c + CH)
             ok = allowed(segc, sq, b, c)
             for h in range(3):
-                x = jnp.where(ok, s[h, rows, :], -1e30)
-                s[h, rows, :] = x
+                part = slice(256 * h, 256 * h + 256)
+                x = jnp.where(ok, s[rows, part], -1e30)
+                s[rows, part] = x
                 top[h] = jnp.maximum(top[h], jnp.max(groups(x), axis=0))
         top = [jnp.max(m, axis=0, keepdims=True) for m in top]
         slot(i, 1)
@@ -517,14 +514,16 @@
         for c in range(L // CH):
             rows = slice(CH * c, CH * c + CH)
             for h in range(3):
-                e = jnp.exp(s[h, rows, :] - top[h])
-                pb[h, rows, :] = e.astype(BF)
+                part = slice(256 * h, 256 * h + 256)
+                e = jnp.exp(s[rows, part] - top[h])
+                pb[rows, part] = e.astype(BF)
                 total[h] = total[h] + jnp.sum(groups(e), axis=0)
+        summed = dot(vt[...], pb[...])
         for h in range(3):
             t = jnp.sum(total[h], axis=0, keepdims=True)
             lse_o[3 * b + h] = top[h] + jnp.log(t)
             part = slice(64 * h, 64 * h + 64)
-            ot[part, :] = dot(vt[part, :], pb[h]) * (1.0 / t)
+            ot[part, :] = summed[part, 256 * h : 256 * h + 256] * (1.0 / t)
         sendb[b] = fold(ot[...].T.astype(BF))
 
         @pl.when(b != j)
@@ -535,6 +534,13 @@
 
     homes[6].start()
     attg[j] = sendb[j]
+    valid = across((segr[:, lanes(j)] != 0.0).astype(F32))[:, 0:1]
+    gmid_o[...] = cot[...].astype(F32) * valid
+    gm[...] = gmid_o[...].astype(BF)
+    gmt[...] = gmid_o[...].T.astype(BF)
+    gn2[...] = jnp.zeros_like(gn2)
+    vec_o[...] = jnp.zeros_like(vec_o)
+    vec_o[5:6, :] = rows_sum(gmid_o[...])
     w.out_rest()
     for q in range(4):
 
@@ -543,7 +549,6 @@
             push(attg.at[q], attg.at[q], as_.at[q], ar.at[q], me.z(1)).wait_recv()
 
     w.last(1, 1)
-    w.turn(2, 0)
     att[...] = jnp.concatenate([unfold(attg[q]) for q in range(4)], axis=1)
     mid = x_o[...] + dot(att[...], WO[...]) + line_of(pa)
     h0, scale = norm_stats(mid)
@@ -551,12 +556,7 @@
     normed = h0 * line_of(pg) + line_of(pb2)
     n2[...] = normed.astype(BF)
     n2t[...] = normed.T.astype(BF)
-    valid = across((segr[:, lanes(j)] != 0.0).astype(F32))[:, 0:1]
-    gmid_o[...] = cot[...].astype(F32) * valid
-    gm[...] = gmid_o[...].astype(BF)
-    gmt[...] = gmid_o[...].T.astype(BF)
     acc[...] = mid + line_of(pm)
-    gn2[...] = jnp.zeros_like(gn2)
 
     def to_sibling(i):
         return push(stage.at[i % 2, :, :, 1 - me.core], rc.at[i], cs.at[i], cr.at[i], me.at(me.pc))
@@ -572,17 +572,17 @@
         save(i).start()
 
     def pump1():
-        w.last(2, 1)
         w.rest(1)
+        w.turn(2, 0)
+        w.spread(2, 1)
 
     def pump2():
         w.rest(2)
+        w.last(2, 0)
 
     def pump3():
+        w.last(2, 1)
         w.rest(3)
-
-    w.last(2, 0)
-    w.turn(2, 1)
 
     @pl.loop(0, 4)
     def _(i):
@@ -598,6 +598,7 @@
         acc[...] += dot(act, W2[q, 1])
         grad_pre = (contract_cols(gm[...], W2[q, 1]) * slope).astype(BF)
         gn2[...] += contract_cols(grad_pre, W2[q, 0])
+        pl.when(i == 2)(functools.partial(w.turn, 2, 1))
 
         @pl.when(i >= 2)
         def _():
@@ -613,33 +614,28 @@
         def _():
             chip(i - 1)
 
-    out_o[...] = acc[...].astype(BF)
-    homes[12].start()
     grad = gmid_o[...]
     gn, h0 = gn2[...], hat[...]
-    vec_o[...] = jnp.zeros_like(vec_o)
     vec_o[3:4, :] = rows_sum(gn * h0)
     vec_o[4:5, :] = rows_sum(gn)
-    vec_o[5:6, :] = rows_sum(grad)
     gmid = grad + norm_back(gn, line_of(pg), h0, scale)
     gmid_o[...] = gmid
     vec_o[2:3, :] = rows_sum(gmid)
     gatt_o[...] = contract_cols(gmid.astype(BF), WO[...]).astype(BF)
     for c in homes[9:12]:
         c.start()
+    out_o[...] = acc[...].astype(BF)
+    homes[12].start()
     full = dot(gmid.T.astype(BF), att[...]).astype(BF)
-    for q in range(4):
-        for n in range(8):
-            wst[q, n // 2, n % 2, :, 0:192] = full[96 * n : 96 * n + 96, 192 * q : 192 * q + 192]
-            wst[q, n // 2, n % 2, :, 192:256] = jnp.zeros((96, 64), BF)
+    for n in range(8):
+        wst[0, n // 2, n % 2] = full[96 * n : 96 * n + 96, :]
     wo_copy = push(wst.at[:, :, 1 - me.core], wrc, ws, wr, me.at(me.pc))
     wo_copy.start()
     save(2).wait()
     chip(3)
     wo_copy.wait_recv()
-    for q in range(4):
-        for m in range(4):
-            wacc[q, m] = wst[q, m, me.core] + wrc[q, m]
+    for m in range(4):
+        wacc[0, m] = wst[0, m, me.core] + wrc[0, m]
     wsave = pltpu.make_async_copy(wacc, dwo_o, hs.at[0])
     to_sibling(2).wait_send()
     to_sibling(3).wait_send()
@@ -692,7 +688,7 @@
         + (
             shape((8, 8, 128), jnp.int32),
             shape((2, 4, 4, 96, D), BF),
-            shape((4, 4, 96, 256), BF),
+            shape((1, 4, 96, D), BF),
         ),
         in_specs=[VM] * 2 + [pl.BlockSpec(memory_space=pltpu.SMEM)] + [ANY] * 3 + [VM] * 2 + [ANY] * 5 + [VM] * 4,
         out_specs=(ANY,) * 16,
@@ -710,8 +706,8 @@
             pltpu.VMEM((16, 256), BF),
             pltpu.VMEM((4, 16, 256), BF),
             pltpu.VMEM((192, L), BF),
-            pltpu.VMEM((3, L, 256), F32),
-            pltpu.VMEM((3, L, 256), BF),
+            pltpu.VMEM((L, 768), F32),
+            pltpu.VMEM((L, 768), BF),
             pltpu.VMEM((192, 256), F32),
             pltpu.VMEM((4, 128, 384), BF),
             pltpu.VMEM((4, 128, 384), BF),
@@ -726,9 +722,9 @@
             pltpu.VMEM((2, 2, 4, 2, 96, D), BF),
             pltpu.VMEM((4, 2, 4, 96, D), BF),
             pltpu.VMEM((2, 2, 4, 96, D), BF),
-            pltpu.VMEM((4, 4, 2, 96, 256), BF),
-            pltpu.VMEM((4, 4, 96, 256), BF),
-            pltpu.VMEM((4, 4, 96, 256), BF),
+            pltpu.VMEM((1, 4, 2, 96, D), BF),
+            pltpu.VMEM((1, 4, 96, D), BF),
+            pltpu.VMEM((1, 4, 96, D), BF),
             DMA((2, 3, 4)),
             DMA((2, 3, 4)),
             DMA((3,)),
@@ -783,12 +779,6 @@
         def _():
             self.send(q, d).start()
 
-    def first(self):
-        for q in (3, 2, 1):
-            self.end(q, 0)
-        for q in (0, 1, 2):
-            self.end(q, 1)
-
     def inner(self, steps):
         for q, d, j in steps:
 
@@ -826,6 +816,34 @@
             @pl.when(j > q)
             def _():
                 self.send(q, 1).wait_send()
+
+
+class Halved:
+    def __init__(self, me, acc, up, down, sems, parts):
+        self.parts = parts
+        self.lines = [
+            Line(me, lambda q, r=r: acc(q).at[r], up.at[:, r], down.at[:, r], sems.at[i]) for i, r in enumerate(parts)
+        ]
+
+    def end(self, q, d):
+        for line in self.lines:
+            line.end(q, d)
+
+    def first(self):
+        for q, d in ((3, 0), (0, 1), (2, 0), (1, 1), (1, 0), (2, 1)):
+            self.end(q, d)
+
+    def inner(self, steps):
+        for line in self.lines:
+            line.inner(steps)
+
+    def finish(self, out):
+        for line, r in zip(self.lines, self.parts):
+            line.finish(out.at[r])
+
+    def close(self):
+        for line in self.lines:
+            line.close()
 
 
 NEAR = ((3, 0, 1), (0, 1, 2))
@@ -919,7 +937,7 @@
         return self.acc.at[q, self.me.m]
 
 
-SHAPES = ((4, 768), (4, 768), (4, 256), (3, 256))
+SHAPES = ((4, 768), (4, 768), (1, 768), (1, 640))
 
 
 def back_kernel(
@@ -943,7 +961,7 @@
     o_in, o_tok, o_up, o_down, o_out, o_qkv, o_sp, hs = take(8)
     as_, ar = take(2)
     gacc, gup, gdown, gsem = take(4)
-    qk, tb, X, hot, vbuf, SZ, vs = take(7)
+    qk, tb, X, hot, vbuf, SZ, vs, wz = take(8)
     vzs, vzr, ts, tr, ps, pr, vps, vpr, ls = take(9)
     sources = (dw.at[1], dw.at[0], dwo, qk)
     units, lines = [], []
@@ -954,9 +972,9 @@
         units.append(unit)
         if i < 3:
             up, down, sem = take(3)
-            lines.append(Line(me, unit.own, up, down, sem))
-    own = Line(me, lambda q: gacc.at[q], gup, gdown, gsem)
-
+            block = unit.own if i < 2 else lambda q: wz.at[q]
+            lines.append(Halved(me, block, up, down, sem, [pl.ds(0, 48), pl.ds(48, 48)]))
+    own = Halved(me, lambda q: gacc.at[q], gup, gdown, gsem, [pl.ds(0, 128), pl.ds(128, 128)])
     homes = [
         pltpu.make_async_copy(src, dst, hs.at[i])
         for i, (src, dst) in enumerate(
@@ -971,10 +989,8 @@
     for d in range(4):
         sendb[d] = fold(gatt[:, 192 * d : 192 * d + 192])
 
-        @pl.when(j != d)
-        def _():
-            to_heads(d).start()
-
+    for i in (3, 2, 1):
+        to_heads((j + i) % 4).start()
     gbuf[j] = sendb[j]
     for i in (0, 2, 1):
         units[i].begin()
@@ -988,7 +1004,10 @@
     units[2].chip()
     units[2].cross()
     units[1].chip()
-    steps = {}
+    def step3():
+        units[0].turn()
+
+    steps = {11: step3}
 
     def slot(i, n):
         for c, fn in {c: fn for c, fn in steps.items() if c % 3 == n}.items():
@@ -1009,8 +1028,8 @@
         do = unfold(gbuf[b]).astype(F32)
         for h in range(3):
             dom[h] = (do * head_mask(192, h)).astype(BF)
-            s[h] = contract_cols(k[...], qm[h, lanes(b), :])
-            dp[h] = contract_cols(v[...], dom[h])
+        s[...] = contract_cols(k[...], qm[:, lanes(b), :].reshape(768, 192))
+        dp[...] = contract_cols(v[...], dom[...].reshape(768, 192))
         slot(i, 0)
         ls_ = [lse[3 * b + h] for h in range(3)]
         inner = [jnp.zeros((8, 256), F32)] * 3
@@ -1018,22 +1037,24 @@
             rows = slice(CH * c, CH * c + CH)
             ok = allowed(segc, sq, b, c)
             for h in range(3):
-                e = jnp.exp(jnp.where(ok, s[h, rows, :], -1e30) - ls_[h])
-                s[h, rows, :] = e
-                pb[rows, 256 * h : 256 * h + 256] = e.astype(BF)
-                inner[h] = inner[h] + jnp.sum(groups(e * dp[h, rows, :]), axis=0)
+                part = slice(256 * h, 256 * h + 256)
+                e = jnp.exp(jnp.where(ok, s[rows, part], -1e30) - ls_[h])
+                s[rows, part] = e
+                pb[rows, part] = e.astype(BF)
+                inner[h] = inner[h] + jnp.sum(groups(e * dp[rows, part]), axis=0)
         inner = [jnp.sum(a, axis=0, keepdims=True) for a in inner]
         slot(i, 1)
         for c in range(L // CH):
             rows = slice(CH * c, CH * c + CH)
             for h in range(3):
-                grad = s[h, rows, :] * (dp[h, rows, :] - inner[h])
-                dsb[rows, 256 * h : 256 * h + 256] = grad.astype(BF)
+                part = slice(256 * h, 256 * h + 256)
+                dsb[rows, part] = (s[rows, part] * (dp[rows, part] - inner[h])).astype(BF)
         dv[...] += dot(pb[...], dom[...].reshape(768, 192))
         dk[...] += dot(dsb[...], qm[:, lanes(b), :].reshape(768, 192))
+        summed = dot(kt[...], dsb[...])
         for h in range(3):
             part = slice(64 * h, 64 * h + 64)
-            dqt[part, lanes(b)] = dot(kt[part, :], dsb[:, 256 * h : 256 * h + 256]) * 0.125
+            dqt[part, lanes(b)] = summed[part, 256 * h : 256 * h + 256] * 0.125
         slot(i, 2)
 
     for c in loads[8:]:
@@ -1046,14 +1067,14 @@
         gacc[q] = (total + dot(dv[rows, :].astype(BF), wq[384:576, :])).astype(BF)
         for block, d in starts:
             own.end(block, d)
-    units[0].turn()
     units[2].turn()
     units[1].cross()
     for i, grad in enumerate((dqn[...], dk[...].astype(BF), dv[...].astype(BF))):
         full = contract_rows(n1[...], grad).astype(BF)
         for piece in range(8):
-            qk[i, piece // 2, piece % 2, :, 0:192] = full[96 * piece : 96 * piece + 96, :]
-            qk[i, piece // 2, piece % 2, :, 192:256] = jnp.zeros((96, 64), BF)
+            qk[0, piece // 2, piece % 2, :, 192 * i : 192 * i + 192] = full[96 * piece : 96 * piece + 96, :]
+    for piece in range(8):
+        qk[0, piece // 2, piece % 2, :, 576:640] = jnp.zeros((96, 64), BF)
     units[3].begin()
     own.inner(NEAR)
     units[3].chip()
@@ -1062,96 +1083,107 @@
     lines[0].first()
     own.inner(FAR)
     units[2].settle()
+    for q in range(4):
+        wz[q, :, 0:192] = units[2].acc[0, me.m, :, 192 * q : 192 * q + 192]
+        wz[q, :, 192:256] = jnp.zeros((96, 64), BF)
     units[1].turn()
     units[3].turn()
-    own.finish(gn)
-
-    hat, scale = norm_stats(x[...])
-    grad = gn[...]
-    dx = gmid[...] + norm_back(grad, line_of(g1), hat, scale)
-    o_in[...] = dx
+    def to_columns(d, half):
+        return push(tb.at[d, half], X.at[p, j, half], ts.at[d, half], tr.at[j, half], (p, d))
+
+    sums = [jnp.zeros((1, D), F32)] * 3
+
+    def norm_half(half):
+        rows = slice(128 * half, 128 * half + 128)
+        own.lines[half].finish(gn.at[own.parts[half]])
+        hat, scale = norm_stats(x[rows, :])
+        grad = gn[rows, :]
+        dx = gmid[rows, :] + norm_back(grad, line_of(g1), hat, scale)
+        o_in[rows, :] = dx
+        dxb = dx.astype(BF)
+        for d in range(4):
+            tb[d, half] = fold(dxb[:, 192 * d : 192 * d + 192])
+        for i in (2, 1, 3):
+            to_columns((j + i) % 4, half).start()
+        X[p, j, half] = tb[j, half]
+        for n, v in enumerate((grad * hat, grad, dx)):
+            sums[n] = sums[n] + rows_sum(v)
+
+    def hop(ref, i, dev):
+        return push(ref, ref, ps.at[i], pr.at[i], me.at(dev))
+
+    def table(d, start=False):
+        vocab = 1024 * p + lax.broadcasted_iota(jnp.int32, (1024, 128), 0)
+        for g in range(8):
+            hot[:, 128 * g : 128 * g + 128] = (vocab == IDS[d, g : g + 1, :]).astype(F32).astype(BF)
+        rows = jnp.concatenate([unfold(X[d, q, i]) for q in range(4) for i in range(2)], axis=0)
+        part = dot(hot[...], rows)
+        if start:
+            o_tok[...] = part
+        else:
+            o_tok[...] += part
+
+    sent = []
+    here = me.pc - p
+
+    def spread(i, half):
+        q = quarter_at(j, i)
+        ref = X.at[p, q, half]
+        if i > 0:
+            push(ref, ref, ts.at[q, half], tr.at[q, half], me.z(1)).wait_recv()
+        for c in (hop(ref, 4 * q + 2 * half, me.px), hop(ref, 4 * q + 2 * half + 1, me.py)):
+            c.start()
+            sent.append(c)
+
+    def on_x(q, half):
+        return hop(X.at[me.py, q, half], 16 + 2 * q + half, me.px)
+
+    def on_y(q, half):
+        return hop(X.at[me.px, q, half], 16 + 2 * q + half, me.py)
+
+    def corner(i, half):
+        q = quarter_at(j, i)
+        hop(X.at[me.px, q, half], 4 * q + 2 * half, me.px).wait_recv()
+        hop(X.at[me.py, q, half], 4 * q + 2 * half + 1, me.py).wait_recv()
+
+        @pl.when(q < 2)
+        def _():
+            on_x(q, half).start()
+
+        @pl.when(q >= 2)
+        def _():
+            on_y(q, half).start()
+
+    def to_core(d, i):
+        c = hop(X.at[d], i, me.pc)
+        c.start()
+        sent.append(c)
+
+    norm_half(0)
+    spread(0, 0)
+    norm_half(1)
     homes[0].start()
-    dxb = dx.astype(BF)
-
-    def to_columns(d):
-        return push(tb.at[d], X.at[p, j], ts.at[d], tr.at[j], (p, d))
-
-    for d in range(4):
-        tb[d] = fold(dxb[:, 192 * d : 192 * d + 192])
-
-        @pl.when(j != d)
-        def _():
-            to_columns(d).start()
-
-    X[p, j] = tb[j]
     vbuf[...] = vec[...]
-    vbuf[0:1, :] = rows_sum(grad * hat)
-    vbuf[1:2, :] = rows_sum(grad)
-    vbuf[6:7, :] = rows_sum(dx)
+    vbuf[0:1, :] = sums[0]
+    vbuf[1:2, :] = sums[1]
+    vbuf[6:7, :] = sums[2]
     first = jnp.where(j == 0, step[0], 0).astype(F32)
     vbuf[7:8, :] = jnp.full((1, D), 1.0, F32) * first
     small = [push(vbuf, SZ.at[j], vzs.at[i - 1], vzr.at[i - 1], me.z(i)) for i in (1, 2, 3)]
     for c in small:
         c.start()
     SZ[j] = vbuf[...]
-
-    def hop(ref, i, dev):
-        return push(ref, ref, ps.at[i], pr.at[i], me.at(dev))
-
-    def table(d, start=False):
-        vocab = 1024 * p + lax.broadcasted_iota(jnp.int32, (1024, 128), 0)
-        for g in range(8):
-            hot[:, 128 * g : 128 * g + 128] = (vocab == IDS[d, g : g + 1, :]).astype(F32).astype(BF)
-        rows = jnp.concatenate([unfold(X[d, q]) for q in range(4)], axis=0)
-        part = dot(hot[...], rows)
-        if start:
-            o_tok[...] = part
-        else:
-            o_tok[...] += part
-
-    sent = []
-    here = me.pc - p
-
-    def spread(i):
-        q = (j + i) % 4
-        if i > 0:
-            push(X.at[p, q], X.at[p, q], ts.at[q], tr.at[q], me.z(1)).wait_recv()
-        for c in (hop(X.at[p, q], 2 * q, me.px), hop(X.at[p, q], 2 * q + 1, me.py)):
-            c.start()
-            sent.append(c)
-
-    def on_x(q):
-        return hop(X.at[me.py, q], 8 + q, me.px)
-
-    def on_y(q):
-        return hop(X.at[me.px, q], 8 + q, me.py)
-
-    def corner(i):
-        q = (j + i) % 4
-        hop(X.at[me.px, q], 2 * q, me.px).wait_recv()
-        hop(X.at[me.py, q], 2 * q + 1, me.py).wait_recv()
-
-        @pl.when(q < 2)
-        def _():
-            on_x(q).start()
-
-        @pl.when(q >= 2)
-        def _():
-            on_y(q).start()
-
-    def to_core(d, i):
-        c = hop(X.at[d], i, me.pc)
-        c.start()
-        sent.append(c)
-
-    spread(0)
+    spread(0, 1)
     lines[0].inner(NEAR)
     units[1].settle()
     lines[1].first()
-    spread(1)
-    spread(3)
+    spread(1, 0)
+    spread(2, 0)
+    spread(1, 1)
+    spread(2, 1)
     lines[2].first()
-    corner(0)
+    corner(0, 0)
+    corner(0, 1)
     for c in small:
         c.wait()
     vs[...] = SZ[0] + SZ[1] + SZ[2] + SZ[3]
@@ -1160,32 +1192,37 @@
         c.start()
     o_sp[p] = vs[...]
     lines[0].inner(FAR)
-    spread(2)
-    to_core(p, 12)
-    corner(1)
-    corner(3)
+    spread(3, 0)
+    spread(3, 1)
+    to_core(p, 24)
+    corner(1, 0)
+    corner(2, 0)
+    corner(1, 1)
+    corner(2, 1)
     table(p, start=True)
     lines[1].inner(NEAR)
-    corner(2)
-    to_core(me.px, 13)
-    to_core(me.py, 14)
+    corner(3, 0)
+    corner(3, 1)
+    to_core(me.px, 25)
+    to_core(me.py, 26)
     units[3].settle()
     lines[2].inner(NEAR)
-    hop(X.at[me.pc], 12, me.pc).wait_recv()
+    hop(X.at[me.pc], 24, me.pc).wait_recv()
     table(me.pc)
     lines[1].inner(FAR)
     table(me.px)
     for q in range(4):
-        hop(X.at[me.pd, q], 8 + q, me.px).wait_recv()
-    to_core(me.pd, 15)
+        for half in range(2):
+            hop(X.at[me.pd, q, half], 16 + 2 * q + half, me.px).wait_recv()
+    to_core(me.pd, 27)
     lines[2].inner(FAR)
     table(me.py)
     table(me.pd)
-    hop(X.at[me.px + here], 13, me.pc).wait_recv()
+    hop(X.at[me.px + here], 25, me.pc).wait_recv()
     table(me.px + here)
-    hop(X.at[me.py + here], 14, me.pc).wait_recv()
+    hop(X.at[me.py + here], 26, me.pc).wait_recv()
     table(me.py + here)
-    hop(X.at[me.pd + here], 15, me.pc).wait_recv()
+    hop(X.at[me.pd + here], 27, me.pc).wait_recv()
     table(me.pd + here)
     homes[1].start()
     lines[0].finish(o_down)
@@ -1194,8 +1231,7 @@
     homes[4].start()
     lines[1].finish(o_up)
     homes[2].start()
-    for i in range(3):
-        o_qkv[i] = units[3].acc[i, me.m].astype(F32)
+    o_qkv[...] = units[3].acc[0, me.m].astype(F32)
     homes[5].start()
     for c in out_v:
         c.wait()
@@ -1205,13 +1241,15 @@
     for c in sent:
         c.wait_send()
     for q in range(4):
-        on_x(q).wait_send() if q < 2 else on_y(q).wait_send()
+        for half in range(2):
+            on_x(q, half).wait_send() if q < 2 else on_y(q, half).wait_send()
     for d in range(4):
 
         @pl.when(j != d)
         def _():
             to_heads(d).wait_send()
-            to_columns(d).wait_send()
+            to_columns(d, 0).wait_send()
+            to_columns(d, 1).wait_send()
 
     for line in lines + [own]:
         line.close()
@@ -1241,8 +1279,8 @@
         pltpu.VMEM((4, 128, 384), BF),
         pltpu.VMEM((4, 128, 384), BF),
         pltpu.VMEM((3, 256, 192), BF),
-        pltpu.VMEM((3, L, 256), F32),
-        pltpu.VMEM((3, L, 256), F32),
+        pltpu.VMEM((L, 768), F32),
+        pltpu.VMEM((L, 768), F32),
         pltpu.VMEM((L, 768), BF),
         pltpu.VMEM((L, 768), BF),
         pltpu.VMEM((192, L), F32),
@@ -1255,7 +1293,7 @@
         pltpu.VMEM((96, D), F32),
         pltpu.VMEM((96, D), F32),
         pltpu.VMEM((96, 256), F32),
-        pltpu.VMEM((3, 96, 256), F32),
+        pltpu.VMEM((96, 640), F32),
         pltpu.VMEM((8, 8, D), F32),
         DMA((7,)),
         DMA((4,)),
@@ -1263,20 +1301,21 @@
         pltpu.VMEM((4, 256, D), BF),
         pltpu.VMEM((4, 256, D), BF),
         pltpu.VMEM((4, 256, D), BF),
-        DMA((4, 4)),
-        pltpu.VMEM((3, 4, 2, 96, 256), BF),
-        pltpu.VMEM((4, 128, 384), BF),
-        pltpu.VMEM((8, 4, 128, 384), BF),
+        DMA((2, 4, 4)),
+        pltpu.VMEM((1, 4, 2, 96, 640), BF),
+        pltpu.VMEM((4, 2, 64, 384), BF),
+        pltpu.VMEM((8, 4, 2, 64, 384), BF),
         pltpu.VMEM((1024, 1024), BF),
         pltpu.VMEM((8, D), F32),
         pltpu.VMEM((4, 8, D), F32),
         pltpu.VMEM((8, D), F32),
+        pltpu.VMEM((4, 96, 256), BF),
         DMA((3,)),
         DMA((3,)),
-        DMA((4,)),
-        DMA((4,)),
-        DMA((16,)),
-        DMA((16,)),
+        DMA((4, 2)),
+        DMA((4, 2)),
+        DMA((28,)),
+        DMA((28,)),
         DMA((7,)),
         DMA((7,)),
         DMA((2,)),
@@ -1294,7 +1333,8 @@
         if i == 3:
             scratch += [pltpu.VMEM((nq, 4, 96, w), BF)]
         else:
-            scratch += [pltpu.VMEM((4, 96, w), BF), pltpu.VMEM((4, 96, w), BF), DMA((4, 4))]
+            wide = w if i < 2 else 256
+            scratch += [pltpu.VMEM((4, 96, wide), BF), pltpu.VMEM((4, 96, wide), BF), DMA((2, 4, 4))]
     return pl.pallas_call(
         back_kernel,
         out_shape=(
@@ -1303,7 +1343,7 @@
             shape((96, D), F32),
             shape((96, D), F32),
             shape((96, 256), F32),
-            shape((3, 96, 256), F32),
+            shape((96, 640), F32),
             shape((8, 8, D), F32),
         ),
         in_specs=[ANY] * 16 + [VM, pl.BlockSpec(memory_space=pltpu.SMEM)],
@@ -1335,7 +1375,8 @@
         o_up[...] = up[...]
         o_down[...] = down[...]
         o_out[...] = wout[...].T[0:192, :]
-        o_qkv[...] = qkv[:, :, 0:192]
+        for n in range(3):
+            o_qkv[n] = qkv[:, 192 * n : 192 * n + 192]
 
 
 def tail(*args):

time: 187 us -> 184 us (0.984)
  Pallas kernels: 183 us -> 180 us
    pallas_call x1, Pallas kernels: 89.3 us -> 87 us  [front(): pl.pallas_call(front_kernel, out_shape=tuple((shape(*a) for a in FRONT_KE...]
where the time goes in v5:
time: 184 us; the launch traced here: 182 us
  Pallas kernels  180 us (98%)
    pallas_call x1, Pallas kernels, front(): pl.pallas_call(front_kernel, out_shape=tuple((shape(*a) for a in FRONT_KE...  87 us
    pallas_call x1, Pallas kernels, back(): pl.pallas_call(back_kernel, out_shape=(shape((256, D), F32), shape((1024,...  85.7 us
    pallas_call x1, Pallas kernels, tail(): pl.pallas_call(tail_kernel, grid=(5,), out_shape=(shape((1000, D), F32),)...  7.09 us

profile of v5, /device:TPU:0, one launch (start us, length us, event | category | flops | bytes accessed | tf_op | source)
XLA Modules:
  0.0 181.9 jit_solution(12818550047445974609)
XLA Ops:
  1.3 87.0 %front.1 = (bf16[3,1024,192]{2,1,0:T(8,128)(2,1)}, bf16[1024,192]{1,0:T(8,128)(2,1)}, bf16[1024,192]{1,0:T(8,128)(2,1)}, bf16[192,1024]{1,0:T(8,128)(2,1)}, bf16...) custom-call(s32[1024]{0:T(1024)} %ids.1, ...), custom_call_target="tpu_custom_call" | custom-call | tf_op jit(solution)/shard_map/front/pallas_call | solution.py:685
  88.3 85.7 %back.1 = (f32[256,768]{1,0:T(8,128)}, f32[1024,192]{1,0:T(8,128)}, f32[96,768]{1,0:T(8,128)}, f32[96,768]{1,0:T(8,128)}, f32[96,256]{1,0:T(8,128)}, /*index=5*/f32[96,640]{1,0:T(8,128)}, f32[8,8,768]{2,1,0:T(8,128)}) custom-call(bf16[256,768]{1,0:T(8,128)(2,1)} %get-tuple-element.51.h_gatt, bf16[3,1024,192]{2,1,0:T(8,128)(2,1)} %get-tuple-element.52.h_qm, ...), custom_call_target="tpu_custom_call" | custom-call | tf_op jit(solution)/shard_map/back/pallas_call | solution.py:1338
  174.1 0.0 copy-start
  174.1 7.1 %tail.1 = (f32[1000,768]{1,0:T(8,128)}, f32[256,768]{1,0:T(8,128)}, f32[192,1024]{1,0:T(8,128)}, f32[96,768]{1,0:T(8,128)}, f32[96,768]{1,0:T(8,128)}, /*index=5...) custom-call(f32[8,8,768]{2,1,0:T(8,128)} %get-tuple-element.66.sp, ...), custom_call_target="tpu_custom_call" | custom-call | tf_op jit(solution)/shard_map/tail/pallas_call | solution.py:1392
  181.2 0.0 copy-done
  181.2 0.7 copy.32
Async XLA Ops:
  174.1 7.1 %copy-start = (bf16[256,768]{1,0:T(8,128)(2,1)S(1)}, bf16[256,768]{1,0:T(8,128)(2,1)}, u32[]{:S(2)}) copy-start(bf16[256,768]{1,0:T(8,128)(2,1)} %get-tuple-element.100) | copy-start | bytes 1179652

commit v6 on v5

--- a/solution.py
+++ b/solution.py
@@ -1354,7 +1354,7 @@
     )(*args)
 
 
-def tail_kernel(sp, din, tok, up, down, wout, qkv, *outs):
+def tail_kernel(sp, din, tok, up, down, wout, qkv, res, *outs):
     o_time, o_din, o_tok, o_up, o_down, o_out, o_qkv = outs[:7]
     i = pl.program_id(0)
     row = (200 * i + lax.broadcasted_iota(jnp.int32, (200, D), 0)).astype(F32)
@@ -1368,8 +1368,9 @@
         sums = sp[0]
         for d in range(1, 8):
             sums = sums + sp[d]
-        for n, ref in enumerate(outs[7:]):
+        for n, ref in enumerate(outs[7:13]):
             ref[...] = sums[n : n + 1, :].reshape(D)
+        outs[13][...] = res[...]
         o_din[...] = din[...]
         o_tok[...] = tok[...].T
         o_up[...] = up[...]
@@ -1388,7 +1389,7 @@
         shape((96, D), F32),
         shape((192, 96), F32),
         shape((3, 96, 192), F32),
-    ) + (shape((D,), F32),) * 6
+    ) + (shape((D,), F32),) * 6 + (shape((256, D), BF),)
     return pl.pallas_call(
         tail_kernel,
         grid=(5,),
@@ -1655,10 +1656,10 @@
         timesteps,
     )
     o_time, o_in, o_tok, o_up, o_down, o_out, o_qkv, *sums = tail(
-        SP, input_grad, grad_token_table, g_up, g_down, g_out, g_qkv
+        SP, input_grad, grad_token_table, g_up, g_down, g_out, g_qkv, out
     )
     return (
-        out, o_in, o_tok.T, o_time, sums[0], sums[1], o_qkv.transpose(1, 0, 2), o_out, sums[2], sums[3], sums[4],
+        sums[6], o_in, o_tok.T, o_time, sums[0], sums[1], o_qkv.transpose(1, 0, 2), o_out, sums[2], sums[3], sums[4],
         o_up, o_down.T, sums[5],
     )
 

time: 184 us -> 183 us (level)
  no operation moved by 1% of the time
where the time goes in v6:
time: 183 us; the launch traced here: 182 us
  Pallas kernels  180 us (98%)
    pallas_call x1, Pallas kernels, front(): pl.pallas_call(front_kernel, out_shape=tuple((shape(*a) for a in FRONT_KE...  87 us
    pallas_call x1, Pallas kernels, back(): pl.pallas_call(back_kernel, out_shape=(shape((256, D), F32), shape((1024,...  85.7 us
    pallas_call x1, Pallas kernels, tail(): pl.pallas_call(tail_kernel, grid=(5,), out_shape=(shape((1000, D), F32),)...  7.33 us

profile of v6, /device:TPU:0, one launch (start us, length us, event | category | flops | bytes accessed | tf_op | source)
XLA Modules:
  0.0 181.6 jit_solution(6764952744863519957)
XLA Ops:
  1.3 87.0 %front.1 = (bf16[3,1024,192]{2,1,0:T(8,128)(2,1)}, bf16[1024,192]{1,0:T(8,128)(2,1)}, bf16[1024,192]{1,0:T(8,128)(2,1)}, bf16[192,1024]{1,0:T(8,128)(2,1)}, bf16...) custom-call(s32[1024]{0:T(1024)} %ids.1, ...), custom_call_target="tpu_custom_call" | custom-call | tf_op jit(solution)/shard_map/front/pallas_call | solution.py:685
  88.3 85.7 %back.1 = (f32[256,768]{1,0:T(8,128)}, f32[1024,192]{1,0:T(8,128)}, f32[96,768]{1,0:T(8,128)}, f32[96,768]{1,0:T(8,128)}, f32[96,256]{1,0:T(8,128)}, /*index=5*/f32[96,640]{1,0:T(8,128)}, f32[8,8,768]{2,1,0:T(8,128)}) custom-call(bf16[256,768]{1,0:T(8,128)(2,1)} %get-tuple-element.51.h_gatt, bf16[3,1024,192]{2,1,0:T(8,128)(2,1)} %get-tuple-element.52.h_qm, ...), custom_call_target="tpu_custom_call" | custom-call | tf_op jit(solution)/shard_map/back/pallas_call | solution.py:1338
  174.1 7.3 %tail.1 = (f32[1000,768]{1,0:T(8,128)}, f32[256,768]{1,0:T(8,128)}, f32[192,1024]{1,0:T(8,128)}, f32[96,768]{1,0:T(8,128)}, f32[96,768]{1,0:T(8,128)}, /*index=5...) custom-call(f32[8,8,768]{2,1,0:T(8,128)} %get-tuple-element.66.sp, ...), custom_call_target="tpu_custom_call" | custom-call | tf_op jit(solution)/shard_map/tail/pallas_call | solution.py:1393
